TPU v7x, 32 devices: a whole 2x2x4 slice. The times are simulated.
32 devices in a mesh: dp: 4 (over z), context: 8 (over y, x, core).
Axes of the slice: x: 2, y: 2, z: 4, core: 2. Of those that a mesh axis runs over, the one named last changes fastest.
Arguments:
- inputs: bfloat16 [4, 1024, 4096], P('dp', 'context'), may hold values from -6 to 6
- cotangent: bfloat16 [4, 1024, 4096], P('dp', 'context'), may hold values from -6 to 6
- rate: float32 [16, 4096], replicated, may hold values from 0 to 1, as said below
- residues: float32 [16, 4096], replicated, may hold values from -3 to 3
Outputs:
- grad_inputs: bfloat16 [4, 1024, 4096], P('dp', 'context')
- grad_residues: float32 [16, 4096], P(None, 'dp')
- grad_rate: float32 [16, 4096], P(None, 'dp')
Inputs may be any that keep to these rules, and one draw needn't show every extreme that they name: Every rate is positive.
All inputs are finite; a program needn't handle non-finite values.
Results may differ from a plain program's by a relative error of at most 0.001.
Values sent between devices are 32-bit elements; how exact they have to be, the bound alone decides.
No kernel may reach another device: no remote copies, remote signals or barrier semaphores. Data moves between devices by JAX's collectives and lax.ppermute only.
A program may use at most 192 MiB of HBM per device.

v0:
```python
import math

import jax
import jax.numpy as jnp
from jax import lax
from jax.sharding import PartitionSpec as P

block_span = 16
exact = lax.Precision.HIGHEST


def carried_in(value, axis, join, neutral, backward):
    count, mine = (lax.axis_size(axis), lax.axis_index(axis))
    pieces = jax.tree.map(lambda part: lax.all_gather(part, axis), value)
    if backward:
        pieces = jax.tree.map(lambda part: part[::-1], pieces)
        mine = count - 1 - mine
    subtotal = jax.tree.map(
        lambda part, zero: jnp.full_like(part, 0) + jnp.asarray(zero, part.dtype), value, neutral
    )

    def lap(position, subtotal):
        longer = join(subtotal, jax.tree.map(lambda part: part[position], pieces))
        return jax.tree.map(lambda new, old: jnp.where(position < mine, new, old), longer, subtotal)

    return lax.fori_loop(0, count - 1, lap, subtotal)


def combine_maps(earlier, later):
    return (earlier[0] * later[0], later[0] * earlier[1] + later[1])


def table_sum(table, values):
    return jnp.einsum("nkd,skd->snd", table, values, precision=exact)


def mode_sum(toward, adjoints_all):
    return jnp.einsum("nkd,snd->skd", toward, adjoints_all, precision=exact)


def to_blocks(array, block_width):
    lead = array.shape[:-1]
    block_count = array.shape[-1] // block_width
    moved = array.reshape(lead + (block_count, block_width))
    return jnp.moveaxis(moved, -2, 0)


def from_blocks(array):
    moved = jnp.moveaxis(array, 0, -2)
    lead = moved.shape[:-2]
    return moved.reshape(lead + (moved.shape[-2] * moved.shape[-1],))


def tables(rate_blk):
    positions = jnp.arange(block_span, dtype=jnp.float32)
    powers = jnp.exp(-rate_blk[:, None, :] * positions[None, :, None])
    flipped = powers[:, ::-1, :]
    return (positions, powers, flipped)


def per_device(inputs, cotangent, rate, residues):
    seq_rows = inputs.shape[1]
    channels = inputs.shape[2]
    sub_count = seq_rows // block_span
    block_width = 512
    input_blocks = to_blocks(inputs[0], block_width)
    cotan_blocks = to_blocks(cotangent[0], block_width)
    rate_blocks = to_blocks(rate, block_width)
    res_blocks = to_blocks(residues, block_width)

    def first_phase(packed):
        input_blk, cotan_blk, rate_blk, residues_blk = packed
        input_vals = input_blk.astype(jnp.float32).reshape(sub_count, block_span, block_width)
        cotan_vals = cotan_blk.astype(jnp.float32).reshape(sub_count, block_span, block_width)
        positions, powers, flipped = tables(rate_blk)
        span_decay = jnp.exp(-rate_blk * block_span)
        into_state = table_sum(flipped, input_vals)
        from_end = table_sum(powers, cotan_vals)

        def chain_step(carry, piece):
            return (span_decay * carry + piece, carry)

        zero_state = jnp.zeros_like(rate_blk)
        local_end, state_zero = lax.scan(chain_step, zero_state, into_state)
        local_start, adjoint_zero = lax.scan(chain_step, zero_state, from_end, reverse=True)
        return (local_end, local_start, state_zero, adjoint_zero, from_end)

    local_end, local_start, state_zero, adjoint_zero, from_end = lax.map(
        first_phase, (input_blocks, cotan_blocks, rate_blocks, res_blocks)
    )
    device_decay = jnp.exp(-rate_blocks * seq_rows)
    identity = (jnp.ones_like(device_decay), jnp.zeros_like(device_decay))
    state_in = carried_in((device_decay, local_end), "context", combine_maps, identity, False)[1]
    adjoint_in = carried_in((device_decay, local_start), "context", combine_maps, identity, True)[1]

    def second_phase(packed):
        (
            input_blk,
            cotan_blk,
            rate_blk,
            residues_blk,
            zero_states,
            zero_adjoints,
            state_start,
            adjoint_start,
            end_sums,
        ) = packed
        input_vals = input_blk.astype(jnp.float32).reshape(sub_count, block_span, block_width)
        cotan_vals = cotan_blk.astype(jnp.float32).reshape(sub_count, block_span, block_width)
        positions, powers, flipped = tables(rate_blk)
        decay_step = jnp.exp(-rate_blk)
        span_decay = jnp.exp(-rate_blk * block_span)
        impulse = jnp.sum(powers * residues_blk[:, None, :], axis=0)
        offsets = jnp.arange(sub_count, dtype=jnp.float32) * block_span
        states_all = (
            zero_states + jnp.exp(-rate_blk[None] * offsets[:, None, None]) * state_start[None]
        )
        adjoints_all = (
            zero_adjoints
            + jnp.exp(-rate_blk[None] * offsets[::-1, None, None]) * adjoint_start[None]
        )
        index_row = jnp.arange(block_span, dtype=jnp.int32)
        shifts = (
            index_row[None, :, None] - index_row[:, None, None] == index_row[None, None, :]
        ).astype(jnp.float32)
        toeplitz = jnp.einsum("jkl,ld->jkd", shifts, impulse, precision=exact)
        conv_local = jnp.einsum("jkd,skd->sjd", toeplitz, cotan_vals, precision=exact)
        cross_rows = jnp.einsum("skd,sjd->kjd", cotan_vals, input_vals, precision=exact)
        lag_sums = jnp.einsum("jkl,kjd->ld", shifts, cross_rows, precision=exact)
        toward = residues_blk[:, None, :] * flipped * decay_step[:, None, :]
        conv_cross = mode_sum(toward, adjoints_all)
        grad_block = (conv_local + conv_cross).astype(jnp.bfloat16).reshape(seq_rows, block_width)
        up_weight = (positions + 1.0)[None, :, None] * powers
        back_weight = (block_span - 1.0 - positions)[None, :, None] * flipped
        lag_weight = positions[None, :, None] * powers / decay_step[:, None, :]
        cotan_up = table_sum(up_weight, cotan_vals)
        input_back = table_sum(back_weight, input_vals)
        res_part = jnp.sum(states_all * decay_step[None] * end_sums, axis=0) + jnp.sum(
            powers * lag_sums[None], axis=1
        )
        cross_part = jnp.sum(
            states_all * adjoints_all * (block_span * span_decay)[None]
            + states_all * cotan_up
            + adjoints_all * input_back,
            axis=0,
        )
        pole_part = residues_blk * (cross_part + jnp.sum(lag_weight * lag_sums[None], axis=1))
        return (grad_block, res_part, -decay_step * pole_part)

    grad_blocks, res_parts, pole_parts = lax.map(
        second_phase,
        (
            input_blocks,
            cotan_blocks,
            rate_blocks,
            res_blocks,
            state_zero,
            adjoint_zero,
            state_in,
            adjoint_in,
            from_end,
        ),
    )
    grad_inputs = from_blocks(grad_blocks).reshape(1, seq_rows, channels)
    grad_scale = 1.0 / math.sqrt(lax.axis_size("dp") * seq_rows * lax.axis_size("context"))
    grad_terms = jnp.stack([from_blocks(res_parts), from_blocks(pole_parts)]) * grad_scale
    summed = lax.psum(grad_terms, "context")
    owned = lax.psum_scatter(summed, "dp", scatter_dimension=2, tiled=True)
    return (grad_inputs, owned[0], owned[1])


def solution(mesh):
    in_specs = (P("dp", "context", None), P("dp", "context", None), P(), P())
    out_specs = (P("dp", "context", None), P(None, "dp"), P(None, "dp"))
    return jax.shard_map(
        per_device, mesh=mesh, in_specs=in_specs, out_specs=out_specs, check_vma=False
    )
```

profile of v0, /device:TPU:0, one launch (start us, length us, event | category | flops | bytes accessed | tf_op | source)
XLA Modules:
  0.0 1044.1 jit_solution(9637138375832188954)
XLA Ops:
  14.1 235.2 %while.138 = (s32[]{:T(128)}, f32[8,16,512]{2,1,0:T(8,128)}, f32[8,16,512]{2,1,0:T(8,128)}, f32[8,8,16,512]{3,2,1,0:T(8,128)}, f32[8,8,16,512]{3,2,1,0:T(8,128)}...) while((s32[]{:T(128)}, f32[8,16,512]{2,1,0:T(8,128)}, ...), condition=%wide.region_5.6_spmd, body=%wide.region_0.5_spmd.sunk | while | flops 25518088 | bytes 11601989 | solution.py:88
  255.0 25.0 %all-gather.9.cloned.1.call-done = f32[64,16,512]{2,1,0:T(8,128)} async-done(((f32[8,16,512]{2,1,0:T(8,128)}), f32[64,16,512]{2,1,0:T(8,128)}) %all-gather.9.cloned.1.call-update) | async-done | bytes 2097168 | tf_op jit(solution)/shard_map/all_gather | solution.py:14
  281.8 28.0 %all-gather.7.cloned.1.call-done = f32[64,16,512]{2,1,0:T(8,128)} async-done(((f32[8,16,512]{2,1,0:T(8,128)}), f32[64,16,512]{2,1,0:T(8,128)}) %all-gather.7.cloned.1.call-update) | async-done | bytes 2097168 | tf_op jit(solution)/shard_map/all_gather | solution.py:14
  313.1 12.5 %while.140 = (s32[]{:T(128)}, f32[8,16,512]{2,1,0:T(8,128)}, s32[]{:T(128)}, f32[8,8,16,512]{3,2,1,0:T(8,128)}, f32[8,8,16,512]{3,2,1,0:T(8,128)S(1)}, /*index=5*/s32[]{:T(128)}, s32[]{:T(128)}) while((s32[]{:T(128)}, f32[8,16,512]{2,1,0:T(8,128)}, s32[]{:T(128)}, f32[8,8,16,512]{3,2,1,0:T(8,128)}, ...), condition=%wide.region_9.10_spmd.clone, body=%wide.region_8.9_spmd.clone.sunk | while | flops 262148 | bytes 1048677 | solution.py:26
  325.7 14.0 %all-gather.11.cloned.1.call-done = f32[64,16,512]{2,1,0:T(8,128)} async-done(((f32[8,16,512]{2,1,0:T(8,128)}), f32[64,16,512]{2,1,0:T(8,128)}) %all-gather.11.cloned.1.call-update) | async-done | bytes 2097168 | tf_op jit(solution)/shard_map/all_gather | solution.py:14
  339.7 13.0 %while.141 = (s32[]{:T(128)}, f32[8,16,512]{2,1,0:T(8,128)}, s32[]{:T(128)}, f32[8,8,16,512]{3,2,1,0:T(8,128)}, f32[8,8,16,512]{3,2,1,0:T(8,128)}, /*index=5*/s32[]{:T(128)}, s32[]{:T(128)}) while((s32[]{:T(128)}, f32[8,16,512]{2,1,0:T(8,128)}, s32[]{:T(128)}, f32[8,8,16,512]{3,2,1,0:T(8,128)}, f32[8,8,16,512]{3,2,1,0:T(8,128)}, ...), condition=%wide.region_7.8_spmd.clone, body=%wide.region_6.7_spmd.clone.sunk | while | flops 262148 | bytes 1048677 | solution.py:26
  352.7 602.0 %while.139 = (s32[]{:T(128)}, bf16[8,128,512]{2,1,0:T(8,128)(2,1)}, f32[8,16,512]{1,2,0:T(8,128)}, f32[8,16,512]{1,2,0:T(8,128)}, bf16[8,128,512]{2,1,0:T(8,128)...) while((s32[]{:T(128)}, bf16[8,128,512]{2,1,0:T(8,128)(2,1)}, ...), condition=%wide.region_16.17_spmd, body=%wide.region_10.16_spmd.sunk | while | flops 106221872 | bytes 21108352 | solution.py:150
  362.5 8.3 multiply_reduce_fusion.4
  392.4 8.3 fusion.98
  437.8 8.3 multiply_reduce_fusion.4
  467.7 8.3 fusion.98
  513.1 8.3 multiply_reduce_fusion.4
  543.0 8.3 fusion.98
  588.3 8.3 multiply_reduce_fusion.4
  618.2 8.3 fusion.98
  663.5 8.3 multiply_reduce_fusion.4
  693.4 8.3 fusion.98
  738.8 8.3 multiply_reduce_fusion.4
  768.7 8.3 fusion.98
  814.0 8.3 multiply_reduce_fusion.4
  843.9 8.3 fusion.98
  919.2 8.3 fusion.98
  960.2 21.8 %reduce-scatter.2.cloned.1.call-done = f32[2,16,1024]{2,1,0:T(8,128)} async-done(((f32[2,16,4096]{2,1,0:T(8,128)}), f32[2,16,1024]{2,1,0:T(8,128)}) %reduce-scatter.2.cloned.1.call-update) | async-done | bytes 131088 | tf_op jit(solution)/shard_map/reduce_scatter | solution.py:168
  983.9 52.2 %all-reduce.2.cloned.1.call-done = f32[2,16,1024]{2,1,0:T(8,128)} async-done(((f32[2,16,1024]{2,1,0:T(8,128)}), f32[2,16,1024]{2,1,0:T(8,128)}) %all-reduce.2.cloned.1.call-update) | async-done | bytes 131088 | tf_op jit(solution)/shard_map/psum | solution.py:167
  (1017 shorter events, 764.5 us)
Async XLA Ops:
  7.2 272.9 %all-gather.9.cloned.1.call-start = ((), (), s32[]{:S(2)}) async-start(), calls=%async_computation.2 | async-start | bytes 2359296 | tf_op jit(solution)/shard_map/all_gather | solution.py:14
  249.3 60.6 %all-gather.7.cloned.1.call-start = ((), (), s32[]{:S(2)}) async-start(), calls=%async_computation.1 | async-start | bytes 2359296 | tf_op jit(solution)/shard_map/all_gather | solution.py:14
  251.3 88.4 %all-gather.11.cloned.1.call-start = ((), (), s32[]{:S(2)}) async-start(), calls=%async_computation.3 | async-start | bytes 2359296 | tf_op jit(solution)/shard_map/all_gather | solution.py:14
  252.0 730.0 %reduce-scatter.2.cloned.1.call-start = ((), (), s32[]{:S(2)}) async-start(), calls=%async_computation.4 | async-start | bytes 655360 | tf_op jit(solution)/shard_map/reduce_scatter | solution.py:168
  392.4 10.1 copy-start.1
  392.4 10.1 copy-start.11
  429.1 8.6 copy-start.4
  467.7 10.1 copy-start.1
  467.7 10.1 copy-start.11
  542.9 10.1 copy-start.1
  542.9 10.1 copy-start.11
  618.2 10.1 copy-start.1
  618.2 10.1 copy-start.11
  654.8 8.6 copy-start.4
  693.4 10.1 copy-start.1
  693.4 10.1 copy-start.11
  768.6 10.1 copy-start.1
  768.6 10.1 copy-start.11
  843.9 10.1 copy-start.1
  843.9 10.1 copy-start.11
  919.2 10.1 copy-start.1
  919.2 10.1 copy-start.11
  957.0 25.0 %copy-start.19 = (bf16[8,128,512]{2,1,0:T(8,128)(2,1)S(1)}, bf16[8,128,512]{2,1,0:T(8,128)(2,1)}, u32[]{:S(2)}) copy-start(bf16[8,128,512]{2,1,0:T(8,128)(2,1)} %get-tuple-element.596) | copy-start | bytes 3145732
  960.2 75.9 %all-reduce.2.cloned.1.call-start = ((), (), s32[]{:S(2)}) async-start(), calls=%async_computation.5 | async-start | bytes 262144 | tf_op jit(solution)/shard_map/psum | solution.py:167
  (120 other events, 593.6 us)
Sparse Core Ops, SparseCore 0:
  249.4 30.5 all-gather.8
  281.9 27.8 all-gather.6
  311.8 27.8 all-gather.10
  960.3 21.6 reduce-scatter.1
  984.9 51.1 all-reduce.1
where the time goes:
time: 1050 us; the launch traced here: 1040 us
  local copies, waits for them, and re-layouts  359 us (34%)
  matrix products  338 us (32%)
  other arithmetic  185 us (18%)
  waiting for transfers between devices  142 us (14%)
  between operations  13.9 us (1%)
    dot_general x32, matrix products, table_sum(): return jnp.einsum('nkd,skd->snd', table, values, precision=exact)  191 us
    rev x16, local copies, waits for them, and re-layouts, tables(): flipped = powers[:, ::-1, :]  116 us
    all_gather x3, waiting for transfers between devices, carried_in(): pieces = jax.tree.map(lambda part: lax.all_gather(part, axis), value)  67.1 us
    reduce_sum x8, other arithmetic, second_phase(): jnp.sum(lag_weight * lag_sums[None], axis=1)  66.3 us
    dynamic_slice x72, local copies, waits for them, and re-layouts, per_device(): lax.map(first_phase, (input_blocks, cotan_blocks, rate_blocks, res_blocks))  59.3 us
    dot_general x8, matrix products, mode_sum(): return jnp.einsum('nkd,snd->skd', toward, adjoints_all, precision=exact)  52.9 us
    dot_general x8, matrix products, second_phase(): jnp.einsum('jkd,skd->sjd', toeplitz, cotan_vals, precision=exact)  52.6 us
    dynamic_slice x24, local copies, waits for them, and re-layouts, per_device(): lax.map(second_phase, (input_blocks, cotan_blocks, rate_blocks, res_block...  52.3 us
  transfers between devices with their start and end apart: 5, of which 5 were waited for; matrix products, arithmetic and copies ran while one was open for 2% of the time, Pallas kernels for 0%

commit v1 on v0

v1 whole, which is shorter than its diff:
```python
import functools
import math

import jax
import jax.numpy as jnp
from jax import lax
from jax.experimental import pallas as pl
from jax.experimental.pallas import tpu as pltpu
from jax.sharding import PartitionSpec as P

LANES = 128
SUBS = 8
SPAN = 8
PARTS = 6
END, START, DEND, DSTART, RES, POLE = range(PARTS)
f32 = jnp.float32


def horner(values, point):
    value, slope, scaled = values[0], None, None
    for item in values[1:]:
        if slope is None:
            slope = value
        elif scaled is not None and slope is values[0]:
            slope = scaled + value
        else:
            slope = slope * point + value
        scaled = value * point
        value = scaled + item
    return value, slope


def spread(tiles, scratch, rows, stride):
    for place, tile in enumerate(tiles):
        scratch[pl.ds(place, rows, stride=stride), :] = tile


def summary_kernel(where, *refs, rows, modes, together):
    x_tiles, c_tiles, r_tiles = refs[:SUBS], refs[SUBS : 2 * SUBS], refs[2 * SUBS : 3 * SUBS]
    out, rate_out, xs, cs, kept = refs[3 * SUBS :]
    blocks = rows // SPAN
    for place in range(SUBS):
        xs[pl.ds(place, rows, stride=SUBS), :] = x_tiles[place][...].astype(f32)
        cs[pl.ds(place, rows, stride=SUBS), :] = c_tiles[place][...].astype(f32)
        rate_out[pl.ds(place, modes, stride=SUBS), :] = r_tiles[place][...]

    def row(ref, index):
        return ref[pl.ds(pl.multiple_of(index * SUBS, SUBS), SUBS), :]

    zero = jnp.zeros((SUBS, LANES), f32)

    def lag_step(block, sums):
        xv = [row(xs, block * SPAN + k) for k in range(SPAN)]
        cv = [row(cs, block * SPAN + k) for k in range(SPAN)]
        return tuple(
            sums[lag] + sum(cv[k] * xv[k - lag] for k in range(lag, SPAN)) for lag in range(SPAN)
        )

    lags = lax.fori_loop(0, blocks, lag_step, (zero,) * SPAN)
    for lag in range(SPAN):
        kept[pl.ds(2 * together * blocks * SUBS + lag * SUBS, SUBS), :] = lags[lag]

    def slot(mode, block, which):
        return pl.ds(pl.multiple_of(((mode * blocks + block) * 2 + which) * SUBS, SUBS), SUBS)

    def some_modes(group, carry):
        ids = [group * together + m for m in range(together)]
        rates = [row(rate_out, n) for n in ids]
        poles = [jnp.exp(-r) for r in rates]
        spans = [jnp.exp(-r * SPAN) for r in rates]
        slopes = [jnp.exp(-r * (SPAN - 1)) * SPAN for r in rates]

        def forward(block, state):
            xv = [row(xs, block * SPAN + k) for k in range(SPAN)]
            new = []
            for m in range(together):
                now, dnow = state[m]
                value, slope = horner(xv, poles[m])
                push = slope + slopes[m] * now
                kept[slot(m, block, 0), :] = now
                kept[slot(m, block, 1), :] = push
                new.append((now * spans[m] + value, dnow * spans[m] + push))
            return tuple(new)

        ends = lax.fori_loop(0, blocks, forward, ((zero, zero),) * together, unroll=2)

        def backward(index, state):
            block = blocks - 1 - index
            cv = [row(cs, block * SPAN + k) for k in reversed(range(SPAN))]
            new = []
            for m in range(together):
                now, dnow, first, second = state[m]
                value, slope = horner(cv, poles[m])
                entry = kept[slot(m, block, 0), :]
                push = kept[slot(m, block, 1), :]
                first = first + entry * value
                second = second + (entry * slope + now * push)
                new.append(
                    (
                        now * spans[m] + value,
                        dnow * spans[m] + (slope + slopes[m] * now),
                        first,
                        second,
                    )
                )
            return tuple(new)

        starts = lax.fori_loop(0, blocks, backward, ((zero,) * 4,) * together, unroll=2)
        lagged = [
            kept[pl.ds(2 * together * blocks * SUBS + lag * SUBS, SUBS), :]
            for lag in reversed(range(SPAN))
        ]
        for m in range(together):
            value, slope = horner(lagged, poles[m])
            first, second = starts[m][2:]
            results = (
                ends[m][0],
                starts[m][0],
                ends[m][1],
                starts[m][1],
                poles[m] * first + value,
                first + poles[m] * second + slope,
            )
            for part in range(PARTS):
                base = pl.multiple_of((part * modes + ids[m]) * SUBS, SUBS)
                out[pl.ds(base, SUBS), :] = results[part]
        return carry

    lax.fori_loop(0, modes // together, some_modes, 0)


def pair_tiles(chips, core):
    def tile_map(place):
        q, chip = place % 4, chips[place // 4]
        return lambda i, w: (0, 8 * q + 2 * (w[0] ^ chip) + (w[1] ^ core))

    return tile_map


def next_tiles(first):
    return lambda place: lambda i, w: (0, first + place)


def summaries(where, inputs, cotangent, rate, tile_map):
    rows, modes = inputs.shape[0], rate.shape[0]
    together = 4

    tiles = lambda height: [pl.BlockSpec((height, LANES), tile_map(s)) for s in range(SUBS)]
    return pl.pallas_call(
        functools.partial(summary_kernel, rows=rows, modes=modes, together=together),
        grid_spec=pltpu.PrefetchScalarGridSpec(
            num_scalar_prefetch=1,
            grid=(1,),
            in_specs=tiles(rows) + tiles(rows) + tiles(modes),
            out_specs=[
                pl.BlockSpec((PARTS * modes * SUBS, LANES), lambda i, w: (0, 0)),
                pl.BlockSpec((modes * SUBS, LANES), lambda i, w: (0, 0)),
            ],
            scratch_shapes=[
                pltpu.VMEM((rows * SUBS, LANES), f32),
                pltpu.VMEM((rows * SUBS, LANES), f32),
                pltpu.VMEM(((2 * together * rows // SPAN + SPAN) * SUBS, LANES), f32),
            ],
        ),
        out_shape=[
            jax.ShapeDtypeStruct((PARTS * modes * SUBS, LANES), f32),
            jax.ShapeDtypeStruct((modes * SUBS, LANES), f32),
        ],
        name="summaries",
    )(where, *([inputs] * SUBS), *([cotangent] * SUBS), *([rate] * SUBS))


def joined(one, two, pole, power, slope):
    cross = one[END] * two[START]
    return (
        power * one[END] + two[END],
        one[START] + power * two[START],
        slope * one[END] + power * one[DEND] + two[DEND],
        one[DSTART] + slope * two[START] + power * two[DSTART],
        one[RES] + two[RES] + pole * cross,
        one[POLE] + two[POLE] + cross + pole * (one[DEND] * two[START] + one[END] * two[DSTART]),
    )


def pair_kernel(where, own, other, rates, send0, send1, hold0, hold1, *, rows, modes):
    def body(one, two):
        for n in range(modes):
            r = rates[pl.ds(n * SUBS, SUBS), :]
            power = jnp.exp(-r * rows)
            read = lambda ref: [ref[pl.ds((a * modes + n) * SUBS, SUBS), :] for a in range(PARTS)]
            first, second = read(one), read(two)
            result = joined(
                first, second, jnp.exp(-r), power, jnp.exp(-r * (rows - 1)) * float(rows)
            )
            for a in range(PARTS):
                send0[pl.ds((a * modes + n) * 4, 4), :] = result[a][:4]
                send1[pl.ds((a * modes + n) * 4, 4), :] = result[a][4:]
            for a, item in enumerate((second[START], power)):
                hold0[pl.ds((a * modes + n) * 4, 4), :] = item[:4]
                hold1[pl.ds((a * modes + n) * 4, 4), :] = item[4:]

    @pl.when(where[1] == 0)
    def _():
        body(own, other)

    @pl.when(where[1] != 0)
    def _():
        body(other, own)


def paired(where, own, other, rates, rows, modes):
    whole = lambda: pl.BlockSpec(memory_space=pltpu.VMEM)
    shape = lambda count: jax.ShapeDtypeStruct((count * modes * 4, LANES), f32)
    return pl.pallas_call(
        functools.partial(pair_kernel, rows=rows, modes=modes),
        in_specs=[pl.BlockSpec(memory_space=pltpu.SMEM), whole(), whole(), whole()],
        out_specs=[whole() for _ in range(4)],
        out_shape=[shape(PARTS), shape(PARTS), shape(2), shape(2)],
        name="paired",
    )(where, own, other, rates)


def chain_kernel(where, *refs, rows, modes, scale):
    pieces, r_tiles, res_tiles = refs[:4], refs[4:8], refs[8:12]
    backs, terms = refs[12:16], refs[16:20]
    ordered, adjoints, small, owned = refs[20:]
    size = modes * 4
    for j in range(4):
        ordered[where[0] ^ j] = pieces[j][...]
    for q in range(4):
        small[0, pl.ds(q, modes, stride=4), :] = r_tiles[q][...]
        small[1, pl.ds(q, modes, stride=4), :] = res_tiles[q][...]
    r = small[0]
    pole = jnp.exp(-r)
    power = jnp.exp(-r * rows)
    slope = jnp.exp(-r * (rows - 1)) * float(rows)
    read = lambda c, a: ordered[c, pl.ds(a * size, size), :]
    now, dnow = read(0, END), read(0, DEND)
    sum_res, sum_pole = read(0, RES), read(0, POLE)
    for c in range(1, 4):
        start, dstart = read(c, START), read(c, DSTART)
        cross = now * start
        sum_res = sum_res + read(c, RES) + pole * cross
        sum_pole = sum_pole + read(c, POLE) + cross + pole * (dnow * start + now * dstart)
        if c < 3:
            now, dnow = (
                power * now + read(c, END),
                slope * now + power * dnow + read(c, DEND),
            )
    back = jnp.zeros((size, LANES), f32)
    adjoints[3] = back
    for c in range(2, -1, -1):
        back = read(c + 1, START) + power * back
        adjoints[c] = back
    for j in range(4):
        backs[j][...] = adjoints[where[0] ^ j]
    owned[pl.ds(0, size), :] = sum_res * scale
    owned[pl.ds(size, size), :] = sum_pole * (-pole * small[1]) * scale
    for j in range(4):
        q = (where[2] + j) % 4
        for a in range(2):
            terms[j][pl.ds(a * modes, modes), :] = owned[pl.ds(a * size + q, modes, stride=4), :]


def chained(where, pieces, rate, residues, rows, scale):
    modes = rate.shape[0]

    def tile_map(q):
        return lambda i, w: (0, 8 * q + 2 * w[0] + w[1])

    whole = lambda height: pl.BlockSpec((height, LANES), lambda i, w: (0, 0))
    tiles = lambda: [pl.BlockSpec((modes, LANES), tile_map(q)) for q in range(4)]
    outs = pl.pallas_call(
        functools.partial(chain_kernel, rows=rows, modes=modes, scale=scale),
        grid_spec=pltpu.PrefetchScalarGridSpec(
            num_scalar_prefetch=1,
            grid=(1,),
            in_specs=[whole(PARTS * modes * 4) for _ in range(4)] + tiles() + tiles(),
            out_specs=[whole(modes * 4) for _ in range(4)] + [whole(2 * modes) for _ in range(4)],
            scratch_shapes=[
                pltpu.VMEM((4, PARTS * modes * 4, LANES), f32),
                pltpu.VMEM((4, modes * 4, LANES), f32),
                pltpu.VMEM((2, modes * 4, LANES), f32),
                pltpu.VMEM((2 * modes * 4, LANES), f32),
            ],
        ),
        out_shape=[jax.ShapeDtypeStruct((modes * 4, LANES), f32) for _ in range(4)]
        + [jax.ShapeDtypeStruct((2 * modes, LANES), f32) for _ in range(4)],
        name="chained",
    )(where, *pieces, *([rate] * 4), *([residues] * 4))
    return outs[:4], outs[4:]


def entry_kernel(where, *refs, modes):
    backs, holds, mine, theirs = refs[:4], refs[4:8], refs[8], refs[9]
    size = modes * 4

    def body(late, early):
        for j in range(4):
            back = backs[j][...]
            late[pl.ds(j * size, size), :] = back
            early[pl.ds(j * size, size), :] = holds[j][:size, :] + holds[j][size:, :] * back

    @pl.when(where[1] == 0)
    def _():
        body(theirs, mine)

    @pl.when(where[1] != 0)
    def _():
        body(mine, theirs)


def entries(where, backs, holds, modes):
    whole = lambda: pl.BlockSpec(memory_space=pltpu.VMEM)
    shape = jax.ShapeDtypeStruct((4 * modes * 4, LANES), f32)
    return pl.pallas_call(
        functools.partial(entry_kernel, modes=modes),
        in_specs=[pl.BlockSpec(memory_space=pltpu.SMEM)] + [whole() for _ in range(8)],
        out_specs=[whole(), whole()],
        out_shape=[shape, shape],
        name="entries",
    )(where, *backs, *holds)


def input_kernel(where, cot, rate, res, *refs, rows, modes, together):
    q = pl.program_id(0)
    size = modes * 4
    given, (out, cs, ys, ps, rs, ads) = refs[:-6], refs[-6:]
    for i in range(SUBS):
        lanes = pl.ds(i * LANES, LANES)
        cs[pl.ds(i, rows, stride=SUBS), :] = cot[:, lanes].astype(f32)
        ps[pl.ds(i, modes, stride=SUBS), :] = jnp.exp(-rate[:, lanes])
        rs[pl.ds(i, modes, stride=SUBS), :] = res[:, lanes]
    if len(given) == 1:
        spread([given[0][:, pl.ds(i * LANES, LANES)] for i in range(SUBS)], ads, modes, SUBS)
    for j in range(4 if len(given) == 2 else 0):
        for core, source in enumerate(given):
            i = 2 * (where[0] ^ j) + (where[1] ^ core)
            ads[pl.ds(i, modes, stride=SUBS), :] = source[pl.ds(j * size + q, modes, stride=4), :]

    for group in range(modes // together):
        at = [pl.ds((group * together + m) * SUBS, SUBS) for m in range(together)]
        poles = [ps[a, :] for a in at]
        weights = [rs[a, :] for a in at]

        def step(index, adjoint):
            here = pl.ds(pl.multiple_of((rows - 1 - index) * SUBS, SUBS), SUBS)
            value = cs[here, :]
            adjoint = tuple(a * p + value for a, p in zip(adjoint, poles))
            terms = [a * w for a, w in zip(adjoint, weights)]
            while len(terms) > 1:
                terms = [a + b for a, b in zip(terms[::2], terms[1::2])]
            ys[here, :] = terms[0] if group == 0 else ys[here, :] + terms[0]
            return adjoint

        lax.fori_loop(0, rows, step, tuple(ads[a, :] for a in at), unroll=4)
    for i in range(SUBS):
        out[:, pl.ds(i * LANES, LANES)] = ys[pl.ds(i, rows, stride=SUBS), :].astype(out.dtype)


def input_gradients(where, cotangent, rate, residues, *given):
    rows, channels = cotangent.shape
    modes = rate.shape[0]
    width = SUBS * LANES
    block = lambda height: pl.BlockSpec((height, width), lambda i, w: (0, i))
    whole = lambda: pl.BlockSpec((16 * modes, LANES), lambda i, w: (0, 0))
    scratch = lambda height: pltpu.VMEM((height * SUBS, LANES), f32)
    return pl.pallas_call(
        functools.partial(input_kernel, rows=rows, modes=modes, together=8),
        grid_spec=pltpu.PrefetchScalarGridSpec(
            num_scalar_prefetch=1,
            grid=(channels // width,),
            in_specs=[block(rows), block(modes), block(modes)]
            + ([block(modes)] if len(given) == 1 else [whole(), whole()]),
            out_specs=block(rows),
            scratch_shapes=[scratch(rows), scratch(rows), scratch(modes), scratch(modes), scratch(modes)],
        ),
        out_shape=jax.ShapeDtypeStruct((rows, channels), cotangent.dtype),
        name="input_gradients",
    )(where, cotangent, rate, residues, *given)


def place_kernel(where, *refs, modes):
    pieces, out_res, out_rate = refs[:4], refs[4], refs[5]
    for j in range(4):
        for core in range(2):
            i = 2 * (where[0] ^ j) + (where[1] ^ core)
            lanes = pl.ds(pl.multiple_of(i * LANES, LANES), LANES)
            out_res[:, lanes] = pieces[j][pl.ds(core * 2 * modes, modes), :]
            out_rate[:, lanes] = pieces[j][pl.ds((core * 2 + 1) * modes, modes), :]


def placed(where, pieces, modes):
    whole = lambda: pl.BlockSpec(memory_space=pltpu.VMEM)
    shape = jax.ShapeDtypeStruct((modes, SUBS * LANES), f32)
    return pl.pallas_call(
        functools.partial(place_kernel, modes=modes),
        in_specs=[pl.BlockSpec(memory_space=pltpu.SMEM)] + [whole() for _ in range(4)],
        out_specs=[whole(), whole()],
        out_shape=[shape, shape],
        name="placed",
    )(where, *pieces)


def crossed(value, distance):
    return lax.ppermute(value, "context", [(i, i ^ distance) for i in range(8)])


def shifted(value, distance):
    return lax.ppermute(value, "dp", [(i, (i + distance) % 4) for i in range(4)])


def four_by_eight(inputs, cotangent, rate, residues):
    x, c = inputs[0], cotangent[0]
    rows, modes = x.shape[0], rate.shape[0]
    context = lax.axis_index("context")
    where = jnp.stack([context // 2, context % 2, lax.axis_index("dp")]).astype(jnp.int32)
    sends, holds = {}, {}
    for chips in ((3, 2), (1, 0)):
        away, _ = summaries(where, x, c, rate, pair_tiles(chips, 1))
        other = crossed(away, 1)
        own, rates = summaries(where, x, c, rate, pair_tiles(chips, 0))
        sends[chips[0]], sends[chips[1]], holds[chips[0]], holds[chips[1]] = paired(
            where, own, other, rates, rows, modes
        )
    pieces = [sends[0]] + [crossed(sends[j], 2 * j) for j in (1, 2, 3)]
    scale = 1.0 / math.sqrt(4 * rows * 8)
    backs, terms = chained(where, pieces, rate, residues, 2 * rows, scale)
    shares = [terms[0]] + [shifted(terms[j], j) for j in (1, 2, 3)]
    backs = [backs[0]] + [crossed(backs[j], 2 * j) for j in (1, 2, 3)]
    mine, theirs = entries(where, backs, [holds[j] for j in range(4)], modes)
    theirs = crossed(theirs, 1)
    grad_inputs = input_gradients(where, c, rate, residues, mine, theirs)
    total = shares[0] + shares[1] + shares[2] + shares[3]
    both = jnp.concatenate([total, crossed(total, 1)])
    grad_residues, grad_rate = placed(
        where, [both] + [crossed(both, 2 * j) for j in (1, 2, 3)], modes
    )
    return (grad_inputs[None], grad_residues, grad_rate)


def any_mesh(inputs, cotangent, rate, residues):
    x, c = inputs[0], cotangent[0]
    rows, channels, modes = x.shape[0], x.shape[1], rate.shape[0]
    count, mine = lax.axis_size("context"), lax.axis_index("context")
    where = jnp.zeros((3,), jnp.int32)
    blocks = [
        summaries(where, x, c, rate, next_tiles(first))[0]
        for first in range(0, channels // LANES, SUBS)
    ]
    local = jnp.stack(blocks).reshape(-1, PARTS, modes, SUBS * LANES)
    local = jnp.moveaxis(local, 0, 2).reshape(PARTS, modes, channels)
    slabs = lax.all_gather(local, "context")
    pole, power = jnp.exp(-rate), jnp.exp(-rate * rows)
    slope = jnp.exp(-rate * (rows - 1)) * rows
    total = tuple(slabs[0])
    for place in range(1, count):
        total = joined(total, slabs[place], pole, power, slope)
    zero = jnp.zeros_like(pole)

    def behind(index, entry):
        place = count - 1 - index
        return jnp.where(place > mine, slabs[place, START] + power * entry, entry)

    entry = lax.fori_loop(0, count, behind, zero)
    grad_inputs = input_gradients(where, c, rate, residues, entry)
    scale = 1.0 / math.sqrt(lax.axis_size("dp") * rows * count)
    terms = jnp.stack([total[RES], total[POLE] * (-pole * residues)]) * scale
    owned = lax.psum_scatter(terms, "dp", scatter_dimension=2, tiled=True)
    return (grad_inputs[None], owned[0], owned[1])


def solution(mesh):
    tuned = mesh.shape["dp"] == 4 and mesh.shape["context"] == 8
    in_specs = (P("dp", "context", None), P("dp", "context", None), P(), P())
    out_specs = (P("dp", "context", None), P(None, "dp"), P(None, "dp"))
    return jax.shard_map(
        four_by_eight if tuned else any_mesh, mesh=mesh, in_specs=in_specs, out_specs=out_specs, check_vma=False
    )
```

time: 1050 us -> 80.7 us (0.08)
  local copies, waits for them, and re-layouts: 359 us -> 4.03 us
  matrix products: 338 us -> 0 us
  other arithmetic: 185 us -> 1.34 us
  waiting for transfers between devices: 142 us -> 12.8 us
  Pallas kernels: 0 us -> 43.1 us
  starting transfers between devices: 0.2 us -> 17.9 us
  between operations: 13.9 us -> 0.76 us
    dot_general x72 -> x0, matrix products: 338 us -> none  [the longest x32 191 us: table_sum(): return jnp.einsum('nkd,skd->snd', table, values, precision=exact)]
    rev x18 -> x0, local copies, waits for them, and re-layouts: 121 us -> none  [the longest x16 116 us: tables(): flipped = powers[:, ::-1, :]]
    dynamic_slice x96 -> x0, local copies, waits for them, and re-layouts: 112 us -> none  [the longest x72 59.3 us: per_device(): lax.map(first_phase, (input_blocks, cotan_blocks, rate_blocks, res_blocks))]
    reduce_sum x16 -> x0, other arithmetic: 90.2 us -> none  [the longest x8 66.3 us: second_phase(): jnp.sum(lag_weight * lag_sums[None], axis=1)]
    all_gather x3 -> x0, waiting for transfers between devices: 67.1 us -> none  [carried_in(): pieces = jax.tree.map(lambda part: lax.all_gather(part, axis), value)]
    psum x1 -> x0, waiting for transfers between devices: 52.2 us -> none  [per_device(): summed = lax.psum(grad_terms, 'context')]
    pallas_call x0 -> x10, Pallas kernels: none -> 43.1 us  [the longest x4 23.5 us: summaries(): pl.pallas_call(functools.partial(summary_kernel, rows=rows, modes=modes,...]
    dot_general x8 -> x0, local copies, waits for them, and re-layouts: 37.3 us -> none  [second_phase(): toeplitz = jnp.einsum('jkl,ld->jkd', shifts, impulse, precision=exact)]
  transfers between devices with their start and end apart: 5 -> 16, of which waited for: 5 -> 6; matrix products, arithmetic and copies ran while one was open for 2% -> 1% of each run, Pallas kernels for 0% -> 31%
where the time goes in v1:
time: 80.7 us; the launch traced here: 79.9 us
  Pallas kernels  43.1 us (53%)
  starting transfers between devices  17.9 us (22%)
  waiting for transfers between devices  12.8 us (16%)
  local copies, waits for them, and re-layouts  4.03 us (5%)
  other arithmetic  1.34 us (2%)
    pallas_call x4, Pallas kernels, summaries(): pl.pallas_call(functools.partial(summary_kernel, rows=rows, modes=modes,...  23.5 us
    ppermute x13, waiting for transfers between devices, crossed(): return lax.ppermute(value, 'context', [(i, i ^ distance) for i in range(8)])  12.8 us
    ppermute x13, starting transfers between devices, crossed(): return lax.ppermute(value, 'context', [(i, i ^ distance) for i in range(8)])  12.1 us
    pallas_call x1, Pallas kernels, input_gradients(): pl.pallas_call(functools.partial(input_kernel, rows=rows, modes=modes, to...  9.64 us
    ppermute x3, starting transfers between devices, shifted(): lax.ppermute(value, 'dp', [(i, (i + distance) % 4) for i in range(4)])  5.75 us
    unnamed x26, local copies, waits for them, and re-layouts  4.03 us
    pallas_call x2, Pallas kernels, paired(): pl.pallas_call(functools.partial(pair_kernel, rows=rows, modes=modes), in...  4.02 us
    pallas_call x1, Pallas kernels, chained(): pl.pallas_call(functools.partial(chain_kernel, rows=rows, modes=modes, sc...  2.74 us
  transfers between devices with their start and end apart: 16, of which 6 were waited for; matrix products, arithmetic and copies ran while one was open for 1% of the time, Pallas kernels for 31%

profile of v1, /device:TPU:0, one launch (start us, length us, event | category | flops | bytes accessed | tf_op | source)
XLA Modules:
  0.0 79.9 jit_solution(10225635793262800098)
XLA Ops:
  1.3 5.9 %summaries.7 = (f32[768,128]{1,0:T(8,128)}, f32[128,128]{1,0:T(8,128)}) custom-call(s32[3]{0:T(128)} %pad_add_fusion.where, bf16[128,4096]{1,0:T(8,128)(2,1)} %bitcast.39, bf16[128,4096]{1,0:T(8,128)(2,1)} %bitcast.40, bf16[128,4096]{1,0:T(8,128)(2,1)} %bitcast.41, bf16[128,4096]{1,0:T(8,128)(2,1)} %bitcast.42, bf16[128,4096]{1,0:T(8,128)(2,1)} %bitcast.43, ...), custom_call_target="tpu_custom_call" | custom-call | tf_op jit(solution)/shard_map/summaries/pallas_call | solution.py:149
  7.7 5.9 %summaries.5 = (f32[768,128]{1,0:T(8,128)}, f32[128,128]{1,0:T(8,128)}) custom-call(s32[3]{0:T(128)} %pad_add_fusion.where, bf16[128,4096]{1,0:T(8,128)(2,1)} %bitcast.54, bf16[128,4096]{1,0:T(8,128)(2,1)} %bitcast.48, bf16[128,4096]{1,0:T(8,128)(2,1)} %bitcast.49, bf16[128,4096]{1,0:T(8,128)(2,1)} %bitcast.50, bf16[128,4096]{1,0:T(8,128)(2,1)} %bitcast.51, ...), custom_call_target="tpu_custom_call" | custom-call | tf_op jit(solution)/shard_map/summaries/pallas_call | solution.py:149
  13.6 5.9 %summaries.6 = (f32[768,128]{1,0:T(8,128)}, f32[128,128]{1,0:T(8,128)}) custom-call(s32[3]{0:T(128)} %pad_add_fusion.where, bf16[128,4096]{1,0:T(8,128)(2,1)} %bitcast.55, bf16[128,4096]{1,0:T(8,128)(2,1)} %bitcast.56, bf16[128,4096]{1,0:T(8,128)(2,1)} %bitcast.57, bf16[128,4096]{1,0:T(8,128)(2,1)} %bitcast.58, bf16[128,4096]{1,0:T(8,128)(2,1)} %bitcast.59, ...), custom_call_target="tpu_custom_call" | custom-call | tf_op jit(solution)/shard_map/summaries/pallas_call | solution.py:149
  19.5 5.9 %summaries.4 = (f32[768,128]{1,0:T(8,128)}, f32[128,128]{1,0:T(8,128)}) custom-call(s32[3]{0:T(128)} %pad_add_fusion.where, bf16[128,4096]{1,0:T(8,128)(2,1)} %bitcast.63, bf16[128,4096]{1,0:T(8,128)(2,1)} %bitcast.64, bf16[128,4096]{1,0:T(8,128)(2,1)} %bitcast.65, bf16[128,4096]{1,0:T(8,128)(2,1)} %bitcast.66, bf16[128,4096]{1,0:T(8,128)(2,1)} %bitcast.67, ...), custom_call_target="tpu_custom_call" | custom-call | tf_op jit(solution)/shard_map/summaries/pallas_call | solution.py:149
  26.2 2.0 %paired.3 = (f32[384,128]{1,0:T(8,128)}, f32[384,128]{1,0:T(8,128)}, f32[128,128]{1,0:T(8,128)}, f32[128,128]{1,0:T(8,128)}) custom-call(s32[3]{0:T(128)} %pad_add_fusion.where, f32[768,128]{1,0:T(8,128)} %get-tuple-element.34.own, f32[768,128]{1,0:T(8,128)} %copy-done.1, f32[128,128]{1,0:T(8,128)} %get-tuple-element.36.rates), custom_call_target="tpu_custom_call" | custom-call | tf_op jit(solution)/shard_map/paired/pallas_call | solution.py:214
  28.2 3.0 %collective-permute-start.3 = (f32[384,128]{1,0:T(8,128)}, f32[384,128]{1,0:T(8,128)S(1)}, u32[]{:S(2)}, u32[]{:S(2)}) collective-permute-start(f32[384,128]{1,0:T(8,128)} %get-tuple-element.37), channel_id=1, source_target_pairs={{0,4},{1,5},{2,6},{3,7},{4,0},{5,1},{6,2},{7,3},{8,12},{9,13},{10,... | collective-permute-start | bytes 589832 | tf_op jit(solution)/shard_map/ppermute | solution.py:406
  31.1 1.4 %collective-permute-start.4 = (f32[384,128]{1,0:T(8,128)}, f32[384,128]{1,0:T(8,128)S(1)}, u32[]{:S(2)}, u32[]{:S(2)}) collective-permute-start(f32[384,128]{1,0:T(8,128)} %get-tuple-element.38), channel_id=1, source_target_pairs={{0,6},{1,7},{2,4},{3,5},{4,2},{5,3},{6,0},{7,1},{8,14},{9,15},{10,... | collective-permute-start | bytes 589832 | tf_op jit(solution)/shard_map/ppermute | solution.py:406
  33.3 2.0 %paired.2 = (f32[384,128]{1,0:T(8,128)}, f32[384,128]{1,0:T(8,128)}, f32[128,128]{1,0:T(8,128)}, f32[128,128]{1,0:T(8,128)}) custom-call(s32[3]{0:T(128)} %pad_add_fusion.where, f32[768,128]{1,0:T(8,128)} %get-tuple-element.29.own, f32[768,128]{1,0:T(8,128)} %copy-done, f32[128,128]{1,0:T(8,128)} %get-tuple-element.31.rates), custom_call_target="tpu_custom_call" | custom-call | tf_op jit(solution)/shard_map/paired/pallas_call | solution.py:214
  35.4 5.3 %collective-permute-done.3.refs_2_ = f32[384,128]{1,0:T(8,128)S(1)} collective-permute-done((f32[384,128]{1,0:T(8,128)}, f32[384,128]{1,0:T(8,128)S(1)}, u32[]{:S(2)}, u32[]{:S(2)}) %collective-permute-start.3) | collective-permute-done | bytes 196640 | tf_op jit(solution)/shard_map/ppermute | solution.py:406
  40.7 1.2 %collective-permute-done.1.refs_1_ = f32[384,128]{1,0:T(8,128)S(1)} collective-permute-done((f32[384,128]{1,0:T(8,128)}, f32[384,128]{1,0:T(8,128)S(1)}, u32[]{:S(2)}, u32[]{:S(2)}) %collective-permute-start.1) | collective-permute-done | bytes 196640 | tf_op jit(solution)/shard_map/ppermute | solution.py:406
  42.6 2.7 %chained.1 = (f32[64,128]{1,0:T(8,128)}, f32[64,128]{1,0:T(8,128)}, f32[64,128]{1,0:T(8,128)}, f32[64,128]{1,0:T(8,128)}, f32[32,128]{1,0:T(8,128)}, /*index=5*/...) custom-call(s32[3]{0:T(128)} %pad_add_fusion.where, f32[384,128]{1,0:T(8,128)} %get-tuple-element.32.refs_0_, ...), custom_call_target="tpu_custom_call" | custom-call | tf_op jit(solution)/shard_map/chained/pallas_call | solution.py:273
  45.3 1.8 %collective-permute-start.9 = (f32[32,128]{1,0:T(8,128)}, f32[32,128]{1,0:T(8,128)S(1)}, u32[]{:S(2)}, u32[]{:S(2)}) collective-permute-start(f32[32,128]{1,0:T(8,128)} %get-tuple-element.50), channel_id=1, source_target_pairs={{0,8},{8,16},{16,24},{24,0},{1,9},{9,17},{17,25},{25,1},{2,10},{10... | collective-permute-start | bytes 49160 | tf_op jit(solution)/shard_map/ppermute | solution.py:410
  47.2 2.6 %collective-permute-start.10 = (f32[32,128]{1,0:T(8,128)}, f32[32,128]{1,0:T(8,128)S(1)}, u32[]{:S(2)}, u32[]{:S(2)}) collective-permute-start(f32[32,128]{1,0:T(8,128)} %get-tuple-element.51), channel_id=1, source_target_pairs={{0,16},{8,24},{16,0},{24,8},{1,17},{9,25},{17,1},{25,9},{2,18},{10... | collective-permute-start | bytes 49160 | tf_op jit(solution)/shard_map/ppermute | solution.py:410
  49.7 1.3 %collective-permute-start.11 = (f32[32,128]{1,0:T(8,128)}, f32[32,128]{1,0:T(8,128)S(1)}, u32[]{:S(2)}, u32[]{:S(2)}) collective-permute-start(f32[32,128]{1,0:T(8,128)} %get-tuple-element.52), channel_id=1, source_target_pairs={{0,24},{8,0},{16,8},{24,16},{1,25},{9,1},{17,9},{25,17},{2,26},{10... | collective-permute-start | bytes 49160 | tf_op jit(solution)/shard_map/ppermute | solution.py:410
  51.1 1.5 %collective-permute-start.5 = (f32[64,128]{1,0:T(8,128)}, f32[64,128]{1,0:T(8,128)S(1)}, u32[]{:S(2)}, u32[]{:S(2)}) collective-permute-start(f32[64,128]{1,0:T(8,128)} %get-tuple-element.40), channel_id=1, source_target_pairs={{0,2},{1,3},{2,0},{3,1},{4,6},{5,7},{6,4},{7,5},{8,10},{9,11},{10,... | collective-permute-start | bytes 98312 | tf_op jit(solution)/shard_map/ppermute | solution.py:406
  52.6 1.5 %collective-permute-start.6 = (f32[64,128]{1,0:T(8,128)}, f32[64,128]{1,0:T(8,128)S(1)}, u32[]{:S(2)}, u32[]{:S(2)}) collective-permute-start(f32[64,128]{1,0:T(8,128)} %get-tuple-element.41), channel_id=1, source_target_pairs={{0,4},{1,5},{2,6},{3,7},{4,0},{5,1},{6,2},{7,3},{8,12},{9,13},{10,... | collective-permute-start | bytes 98312 | tf_op jit(solution)/shard_map/ppermute | solution.py:406
  55.4 1.4 %collective-permute-done.6.refs_2_ = f32[64,128]{1,0:T(8,128)S(1)} collective-permute-done((f32[64,128]{1,0:T(8,128)}, f32[64,128]{1,0:T(8,128)S(1)}, u32[]{:S(2)}, u32[]{:S(2)}) %collective-permute-start.6) | collective-permute-done | bytes 32800 | tf_op jit(solution)/shard_map/ppermute | solution.py:406
  56.7 2.4 %collective-permute-done.7.refs_3_ = f32[64,128]{1,0:T(8,128)S(1)} collective-permute-done((f32[64,128]{1,0:T(8,128)}, f32[64,128]{1,0:T(8,128)S(1)}, u32[]{:S(2)}, u32[]{:S(2)}) %collective-permute-start.7) | collective-permute-done | bytes 32800 | tf_op jit(solution)/shard_map/ppermute | solution.py:406
  59.7 1.8 %entries.1 = (f32[256,128]{1,0:T(8,128)}, f32[256,128]{1,0:T(8,128)}) custom-call(s32[3]{0:T(128)} %pad_add_fusion.where, f32[64,128]{1,0:T(8,128)} %get-tuple-element.39.refs_0_, f32[64,128]{1,0:T(8,128)} %copy-done.7, f32[64,128]{1,0:T(8,128)} %copy-done.8, f32[64,128]{1,0:T(8,128)} %copy-done.9, f32[128,128]{1,0:T(8,128)} %get-tuple-element.43.refs_4_, ...), custom_call_target="tpu_custom_call" | custom-call | tf_op jit(solution)/shard_map/entries/pallas_call | solution.py:316
  62.1 1.5 %collective-permute-start.14 = (f32[64,128]{1,0:T(8,128)S(1)}, f32[64,128]{1,0:T(8,128)S(1)}, u32[]{:S(2)}, u32[]{:S(2)}) collective-permute-start(f32[64,128]{1,0:T(8,128)S(1)} %pad_maximum_fusion.refs_0_), channel_id=1, source_target_pairs={{0,4},{1,5},{2,6},{3,7},{4,0},{5,1},{6,2},{7,3},{8,12},{9,13},{10,... | collective-permute-start | bytes 98312 | tf_op jit(solution)/shard_map/ppermute | solution.py:406
  63.6 1.5 %collective-permute-start.13 = (f32[64,128]{1,0:T(8,128)S(1)}, f32[64,128]{1,0:T(8,128)S(1)}, u32[]{:S(2)}, u32[]{:S(2)}) collective-permute-start(f32[64,128]{1,0:T(8,128)S(1)} %pad_maximum_fusion.refs_0_), channel_id=1, source_target_pairs={{0,2},{1,3},{2,0},{3,1},{4,6},{5,7},{6,4},{7,5},{8,10},{9,11},{10,... | collective-permute-start | bytes 98312 | tf_op jit(solution)/shard_map/ppermute | solution.py:406
  65.1 1.7 %collective-permute-done.15.refs_3_ = f32[64,128]{1,0:T(8,128)S(1)} collective-permute-done((f32[64,128]{1,0:T(8,128)S(1)}, f32[64,128]{1,0:T(8,128)S(1)}, u32[]{:S(2)}, u32[]{:S(2)}) %collective-permute-start.15) | collective-permute-done | bytes 32800 | tf_op jit(solution)/shard_map/ppermute | solution.py:406
  68.1 1.5 %placed.1 = (f32[16,1024]{1,0:T(8,128)}, f32[16,1024]{1,0:T(8,128)}) custom-call(s32[3]{0:T(128)} %pad_add_fusion.where, f32[64,128]{1,0:T(8,128)} %copy-done.6, f32[64,128]{1,0:T(8,128)} %copy-done.12, f32[64,128]{1,0:T(8,128)} %copy-done.11, f32[64,128]{1,0:T(8,128)} %copy-done.10), custom_call_target="tpu_custom_call" | custom-call | tf_op jit(solution)/shard_map/placed/pallas_call | solution.py:396
  70.2 9.6 %input_gradients.1 = bf16[128,4096]{1,0:T(8,128)(2,1)} custom-call(s32[3]{0:T(128)} %pad_add_fusion.where, bf16[128,4096]{1,0:T(8,128)(2,1)} %bitcast.38, f32[16,4096]{1,0:T(8,128)} %rate.1, f32[16,4096]{1,0:T(8,128)} %res.1, f32[256,128]{1,0:T(8,128)} %get-tuple-element.47.refs_0_, f32[256,128]{1,0:T(8,128)} %copy-done.5), custom_call_target="tpu_custom_call" | custom-call | tf_op jit(solution)/shard_map/input_gradients/pallas_call | solution.py:368
  (47 shorter events, 7.9 us)
Async XLA Ops:
  7.1 18.2 %collective-permute-start.2 = (f32[768,128]{1,0:T(8,128)}, f32[768,128]{1,0:T(8,128)S(1)}, u32[]{:S(2)}, u32[]{:S(2)}) collective-permute-start(f32[768,128]{1,0:T(8,128)} %get-tuple-element.35), channel_id=1, source_target_pairs={{0,1},{1,0},{2,3},{3,2},{4,5},{5,4},{6,7},{7,6},{8,9},{9,8},{10,11... | collective-permute-start | bytes 1179656 | tf_op jit(solution)/shard_map/ppermute | solution.py:406
  13.5 19.1 %collective-permute-start = (f32[768,128]{1,0:T(8,128)}, f32[768,128]{1,0:T(8,128)S(1)}, u32[]{:S(2)}, u32[]{:S(2)}) collective-permute-start(f32[768,128]{1,0:T(8,128)} %get-tuple-element.30), channel_id=1, source_target_pairs={{0,1},{1,0},{2,3},{3,2},{4,5},{5,4},{6,7},{7,6},{8,9},{9,8},{10,11... | collective-permute-start | bytes 1179656 | tf_op jit(solution)/shard_map/ppermute | solution.py:406
  25.4 0.8 copy-start.1
  28.2 12.5 %collective-permute-start.3 = (f32[384,128]{1,0:T(8,128)}, f32[384,128]{1,0:T(8,128)S(1)}, u32[]{:S(2)}, u32[]{:S(2)}) collective-permute-start(f32[384,128]{1,0:T(8,128)} %get-tuple-element.37), channel_id=1, source_target_pairs={{0,4},{1,5},{2,6},{3,7},{4,0},{5,1},{6,2},{7,3},{8,12},{9,13},{10,... | collective-permute-start | bytes 589832 | tf_op jit(solution)/shard_map/ppermute | solution.py:406
  31.1 9.5 %collective-permute-start.4 = (f32[384,128]{1,0:T(8,128)}, f32[384,128]{1,0:T(8,128)S(1)}, u32[]{:S(2)}, u32[]{:S(2)}) collective-permute-start(f32[384,128]{1,0:T(8,128)} %get-tuple-element.38), channel_id=1, source_target_pairs={{0,6},{1,7},{2,4},{3,5},{4,2},{5,3},{6,0},{7,1},{8,14},{9,15},{10,... | collective-permute-start | bytes 589832 | tf_op jit(solution)/shard_map/ppermute | solution.py:406
  35.3 6.6 %collective-permute-start.1 = (f32[384,128]{1,0:T(8,128)}, f32[384,128]{1,0:T(8,128)S(1)}, u32[]{:S(2)}, u32[]{:S(2)}) collective-permute-start(f32[384,128]{1,0:T(8,128)} %get-tuple-element.33), channel_id=1, source_target_pairs={{0,2},{1,3},{2,0},{3,1},{4,6},{5,7},{6,4},{7,5},{8,10},{9,11},{10,... | collective-permute-start | bytes 589832 | tf_op jit(solution)/shard_map/ppermute | solution.py:406
  40.7 1.3 %copy-start.2 = (f32[384,128]{1,0:T(8,128)}, f32[384,128]{1,0:T(8,128)S(1)}, u32[]{:S(2)}) copy-start(f32[384,128]{1,0:T(8,128)S(1)} %collective-permute-done.3.refs_2_) | copy-start | bytes 589828
  40.7 1.3 %copy-start.3 = (f32[384,128]{1,0:T(8,128)}, f32[384,128]{1,0:T(8,128)S(1)}, u32[]{:S(2)}) copy-start(f32[384,128]{1,0:T(8,128)S(1)} %collective-permute-done.4.refs_3_) | copy-start | bytes 589828
  45.3 8.8 %collective-permute-start.9 = (f32[32,128]{1,0:T(8,128)}, f32[32,128]{1,0:T(8,128)S(1)}, u32[]{:S(2)}, u32[]{:S(2)}) collective-permute-start(f32[32,128]{1,0:T(8,128)} %get-tuple-element.50), channel_id=1, source_target_pairs={{0,8},{8,16},{16,24},{24,0},{1,9},{9,17},{17,25},{25,1},{2,10},{10... | collective-permute-start | bytes 49160 | tf_op jit(solution)/shard_map/ppermute | solution.py:410
  47.2 7.4 %collective-permute-start.10 = (f32[32,128]{1,0:T(8,128)}, f32[32,128]{1,0:T(8,128)S(1)}, u32[]{:S(2)}, u32[]{:S(2)}) collective-permute-start(f32[32,128]{1,0:T(8,128)} %get-tuple-element.51), channel_id=1, source_target_pairs={{0,16},{8,24},{16,0},{24,8},{1,17},{9,25},{17,1},{25,9},{2,18},{10... | collective-permute-start | bytes 49160 | tf_op jit(solution)/shard_map/ppermute | solution.py:410
  49.7 4.8 %collective-permute-start.11 = (f32[32,128]{1,0:T(8,128)}, f32[32,128]{1,0:T(8,128)S(1)}, u32[]{:S(2)}, u32[]{:S(2)}) collective-permute-start(f32[32,128]{1,0:T(8,128)} %get-tuple-element.52), channel_id=1, source_target_pairs={{0,24},{8,0},{16,8},{24,16},{1,25},{9,1},{17,9},{25,17},{2,26},{10... | collective-permute-start | bytes 49160 | tf_op jit(solution)/shard_map/ppermute | solution.py:410
  51.1 4.2 %collective-permute-start.5 = (f32[64,128]{1,0:T(8,128)}, f32[64,128]{1,0:T(8,128)S(1)}, u32[]{:S(2)}, u32[]{:S(2)}) collective-permute-start(f32[64,128]{1,0:T(8,128)} %get-tuple-element.40), channel_id=1, source_target_pairs={{0,2},{1,3},{2,0},{3,1},{4,6},{5,7},{6,4},{7,5},{8,10},{9,11},{10,... | collective-permute-start | bytes 98312 | tf_op jit(solution)/shard_map/ppermute | solution.py:406
  52.6 4.1 %collective-permute-start.6 = (f32[64,128]{1,0:T(8,128)}, f32[64,128]{1,0:T(8,128)S(1)}, u32[]{:S(2)}, u32[]{:S(2)}) collective-permute-start(f32[64,128]{1,0:T(8,128)} %get-tuple-element.41), channel_id=1, source_target_pairs={{0,4},{1,5},{2,6},{3,7},{4,0},{5,1},{6,2},{7,3},{8,12},{9,13},{10,... | collective-permute-start | bytes 98312 | tf_op jit(solution)/shard_map/ppermute | solution.py:406
  54.1 5.0 %collective-permute-start.7 = (f32[64,128]{1,0:T(8,128)}, f32[64,128]{1,0:T(8,128)S(1)}, u32[]{:S(2)}, u32[]{:S(2)}) collective-permute-start(f32[64,128]{1,0:T(8,128)} %get-tuple-element.42), channel_id=1, source_target_pairs={{0,6},{1,7},{2,4},{3,5},{4,2},{5,3},{6,0},{7,1},{8,14},{9,15},{10,... | collective-permute-start | bytes 98312 | tf_op jit(solution)/shard_map/ppermute | solution.py:406
  55.3 6.2 %collective-permute-start.12 = (f32[32,128]{1,0:T(8,128)S(1)}, f32[32,128]{1,0:T(8,128)S(1)}, u32[]{:S(2)}, u32[]{:S(2)}) collective-permute-start(f32[32,128]{1,0:T(8,128)S(1)} %add_add_fusion), channel_id=1, source_target_pairs={{0,1},{1,0},{2,3},{3,2},{4,5},{5,4},{6,7},{7,6},{8,9},{9,8},{10,11... | collective-permute-start | bytes 49160 | tf_op jit(solution)/shard_map/ppermute | solution.py:406
  55.3 3.8 %copy-start.7 = (f32[64,128]{1,0:T(8,128)}, f32[64,128]{1,0:T(8,128)S(1)}, u32[]{:S(2)}) copy-start(f32[64,128]{1,0:T(8,128)S(1)} %collective-permute-done.5.refs_1_) | copy-start | bytes 98308
  56.7 2.4 %copy-start.8 = (f32[64,128]{1,0:T(8,128)}, f32[64,128]{1,0:T(8,128)S(1)}, u32[]{:S(2)}) copy-start(f32[64,128]{1,0:T(8,128)S(1)} %collective-permute-done.6.refs_2_) | copy-start | bytes 98308
  61.5 8.1 %collective-permute-start.8 = (f32[256,128]{1,0:T(8,128)}, f32[256,128]{1,0:T(8,128)S(1)}, u32[]{:S(2)}, u32[]{:S(2)}) collective-permute-start(f32[256,128]{1,0:T(8,128)} %get-tuple-element.48), channel_id=1, source_target_pairs={{0,1},{1,0},{2,3},{3,2},{4,5},{5,4},{6,7},{7,6},{8,9},{9,8},{10,11... | collective-permute-start | bytes 393224 | tf_op jit(solution)/shard_map/ppermute | solution.py:406
  61.5 6.0 %copy-start.6 = (f32[64,128]{1,0:T(8,128)}, f32[64,128]{1,0:T(8,128)S(1)}, u32[]{:S(2)}) copy-start(f32[64,128]{1,0:T(8,128)S(1)} %pad_maximum_fusion.refs_0_) | copy-start | bytes 98308
  61.5 5.2 %collective-permute-start.15 = (f32[64,128]{1,0:T(8,128)S(1)}, f32[64,128]{1,0:T(8,128)S(1)}, u32[]{:S(2)}, u32[]{:S(2)}) collective-permute-start(f32[64,128]{1,0:T(8,128)S(1)} %pad_maximum_fusion.refs_0_), channel_id=1, source_target_pairs={{0,6},{1,7},{2,4},{3,5},{4,2},{5,3},{6,0},{7,1},{8,14},{9,15},{10,... | collective-permute-start | bytes 98312 | tf_op jit(solution)/shard_map/ppermute | solution.py:406
  62.1 4.7 %collective-permute-start.14 = (f32[64,128]{1,0:T(8,128)S(1)}, f32[64,128]{1,0:T(8,128)S(1)}, u32[]{:S(2)}, u32[]{:S(2)}) collective-permute-start(f32[64,128]{1,0:T(8,128)S(1)} %pad_maximum_fusion.refs_0_), channel_id=1, source_target_pairs={{0,4},{1,5},{2,6},{3,7},{4,0},{5,1},{6,2},{7,3},{8,12},{9,13},{10,... | collective-permute-start | bytes 98312 | tf_op jit(solution)/shard_map/ppermute | solution.py:406
  63.6 3.9 %collective-permute-start.13 = (f32[64,128]{1,0:T(8,128)S(1)}, f32[64,128]{1,0:T(8,128)S(1)}, u32[]{:S(2)}, u32[]{:S(2)}) collective-permute-start(f32[64,128]{1,0:T(8,128)S(1)} %pad_maximum_fusion.refs_0_), channel_id=1, source_target_pairs={{0,2},{1,3},{2,0},{3,1},{4,6},{5,7},{6,4},{7,5},{8,10},{9,11},{10,... | collective-permute-start | bytes 98312 | tf_op jit(solution)/shard_map/ppermute | solution.py:406
  66.7 0.8 copy-start.10
  66.8 0.8 copy-start.11
  (5 other events, 3.3 us)

commit v2 on v1

v2 whole, which is shorter than its diff:
```python
import functools
import math

import jax
import jax.numpy as jnp
from jax import lax
from jax.experimental import pallas as pl
from jax.experimental.pallas import tpu as pltpu
from jax.sharding import PartitionSpec as P

LANES = 128
SUBS = 8
SPAN = 8
PARTS = 6
END, START, DEND, DSTART, RES, POLE = range(PARTS)
f32 = jnp.float32


def here(value):
    return pltpu.with_memory_space_constraint(value, pltpu.VMEM)


def vmem():
    return pl.BlockSpec(memory_space=pltpu.VMEM)


def position():
    context = lax.axis_index("context")
    return context // 2, context % 2, lax.axis_index("dp")


def room(megabytes):
    return pltpu.CompilerParams(vmem_limit_bytes=megabytes << 20)


def work(operations, touched):
    return pl.CostEstimate(flops=operations, transcendentals=0, bytes_accessed=touched)


def local_call(kernel, name, shapes, operands, scratch=(), megabytes=2, cost=None):
    return pl.pallas_call(
        kernel,
        in_specs=[vmem() for _ in operands],
        out_specs=[vmem() for _ in shapes],
        out_shape=[pltpu.VMEM(shape, f32) for shape in shapes],
        scratch_shapes=[pltpu.VMEM(shape, f32) for shape in scratch],
        compiler_params=room(megabytes),
        cost_estimate=cost,
        name=name,
    )(*[here(item) for item in operands])


def horner(values, point):
    value, slope, scaled = values[0], None, None
    for item in values[1:]:
        if slope is None:
            slope = value
        elif scaled is not None and slope is values[0]:
            slope = scaled + value
        else:
            slope = slope * point + value
        scaled = value * point
        value = scaled + item
    return value, slope


def spread(tiles, scratch, rows, stride):
    for place, tile in enumerate(tiles):
        scratch[pl.ds(place, rows, stride=stride), :] = tile


def summary_kernel(x, c, rate, *refs, **static):
    summarize(x, c, rate, *refs[-5:], **static)


def first_kernel(x, c, rate, res, out, rate_out, x_in, c_in, rate_in, res_in, xs, cs, kept, done, **static):
    chip, _, _ = position()
    width = 4 * LANES
    copies = []
    for pair in range(2):
        for q in range(4):
            start = 8 * LANES * q + width * ((chip // 2) ^ (1 - pair))
            lanes = pl.ds(pl.multiple_of(start, width), width)
            copies += [(ref.at[:, lanes], into.at[:, lanes]) for ref, into in ((x, x_in), (c, c_in))]
        if pair == 0:
            copies.append((rate, rate_in))
    copies.append((res, res_in))
    copies = [
        pltpu.make_async_copy(source, into, done.at[place])
        for place, (source, into) in enumerate(copies)
    ]
    for copy in copies:
        copy.start()
    for copy in copies[:9]:
        copy.wait()
    summarize(x_in, c_in, rate_in, out, rate_out, xs, cs, kept, **static)
    for copy in copies[9:]:
        copy.wait()


def summarize(x, c, rate, out, rate_out, xs, cs, kept, *, tile_of, rows, modes, together):
    blocks = rows // SPAN
    for place in range(SUBS):
        lanes = pl.ds(pl.multiple_of(tile_of(place) * LANES, LANES), LANES)
        xs[pl.ds(place, rows, stride=SUBS), :] = x[:, lanes].astype(f32)
        cs[pl.ds(place, rows, stride=SUBS), :] = c[:, lanes].astype(f32)
        rate_out[pl.ds(place, modes, stride=SUBS), :] = rate[:, lanes]

    def row(ref, index):
        return ref[pl.ds(pl.multiple_of(index * SUBS, SUBS), SUBS), :]

    zero = jnp.zeros((SUBS, LANES), f32)

    def lag_step(block, sums):
        xv = [row(xs, block * SPAN + k) for k in range(SPAN)]
        cv = [row(cs, block * SPAN + k) for k in range(SPAN)]
        return tuple(
            sums[lag] + sum(cv[k] * xv[k - lag] for k in range(lag, SPAN)) for lag in range(SPAN)
        )

    lags = lax.fori_loop(0, blocks, lag_step, (zero,) * SPAN)
    for lag in range(SPAN):
        kept[pl.ds(2 * together * blocks * SUBS + lag * SUBS, SUBS), :] = lags[lag]

    def slot(mode, block, which):
        return pl.ds(pl.multiple_of(((mode * blocks + block) * 2 + which) * SUBS, SUBS), SUBS)

    def some_modes(group, carry):
        ids = [group * together + m for m in range(together)]
        rates = [row(rate_out, n) for n in ids]
        poles = [jnp.exp(-r) for r in rates]
        spans = [jnp.exp(-r * SPAN) for r in rates]
        slopes = [jnp.exp(-r * (SPAN - 1)) * SPAN for r in rates]

        def forward(block, state):
            xv = [row(xs, block * SPAN + k) for k in range(SPAN)]
            new = []
            for m in range(together):
                now, dnow = state[m]
                value, slope = horner(xv, poles[m])
                push = slope + slopes[m] * now
                kept[slot(m, block, 0), :] = now
                kept[slot(m, block, 1), :] = push
                new.append((now * spans[m] + value, dnow * spans[m] + push))
            return tuple(new)

        ends = lax.fori_loop(0, blocks, forward, ((zero, zero),) * together, unroll=True)

        def backward(index, state):
            block = blocks - 1 - index
            cv = [row(cs, block * SPAN + k) for k in reversed(range(SPAN))]
            new = []
            for m in range(together):
                now, dnow, first, second = state[m]
                value, slope = horner(cv, poles[m])
                entry = kept[slot(m, block, 0), :]
                push = kept[slot(m, block, 1), :]
                first = first + entry * value
                second = second + (entry * slope + now * push)
                new.append(
                    (
                        now * spans[m] + value,
                        dnow * spans[m] + (slope + slopes[m] * now),
                        first,
                        second,
                    )
                )
            return tuple(new)

        starts = lax.fori_loop(0, blocks, backward, ((zero,) * 4,) * together, unroll=True)
        lagged = [
            kept[pl.ds(2 * together * blocks * SUBS + lag * SUBS, SUBS), :]
            for lag in reversed(range(SPAN))
        ]
        for m in range(together):
            value, slope = horner(lagged, poles[m])
            first, second = starts[m][2:]
            results = (
                ends[m][0],
                starts[m][0],
                ends[m][1],
                starts[m][1],
                poles[m] * first + value,
                first + poles[m] * second + slope,
            )
            for part in range(PARTS):
                base = pl.multiple_of((part * modes + ids[m]) * SUBS, SUBS)
                out[pl.ds(base, SUBS), :] = results[part]
        return carry

    lax.fori_loop(0, modes // together, some_modes, 0)


def pair_tiles(chips, core):
    def tile_of(place):
        chip, half, _ = position()
        return 8 * (place % 4) + 2 * (chip ^ chips[place // 4]) + (half ^ core)

    return tile_of


def next_tiles(first):
    return lambda place: first + place


def summary_parts(rows, modes, tile_of):
    together = 2
    kept = (2 * together * rows // SPAN + SPAN) * SUBS
    static = dict(tile_of=tile_of, rows=rows, modes=modes, together=together)
    shapes = [(PARTS * modes * SUBS, LANES), (modes * SUBS, LANES)]
    cost = work(10 * rows * modes * SUBS * LANES, 4 << 20)
    return static, shapes, [(rows * SUBS, LANES), (rows * SUBS, LANES), (kept, LANES)], cost


def summaries(inputs, cotangent, rate, tile_of, after=()):
    static, shapes, scratch, cost = summary_parts(inputs.shape[0], rate.shape[0], tile_of)
    kernel = functools.partial(summary_kernel, **static)
    return local_call(
        kernel, "summaries", shapes, [inputs, cotangent, rate, *after], scratch, 4, cost
    )


def first_summaries(inputs, cotangent, rate, residues, tile_of):
    static, shapes, scratch, cost = summary_parts(inputs.shape[0], rate.shape[0], tile_of)
    operands = (inputs, cotangent, rate, residues)
    return pl.pallas_call(
        functools.partial(first_kernel, **static),
        in_specs=[pl.BlockSpec(memory_space=pltpu.HBM) for _ in operands],
        out_specs=[vmem() for _ in range(6)],
        out_shape=[pltpu.VMEM(shape, f32) for shape in shapes]
        + [pltpu.VMEM(item.shape, item.dtype) for item in operands],
        scratch_shapes=[pltpu.VMEM(shape, f32) for shape in scratch]
        + [pltpu.SemaphoreType.DMA((18,))],
        compiler_params=room(4),
        cost_estimate=cost,
        name="first_summaries",
    )(*[pltpu.with_memory_space_constraint(item, pltpu.HBM) for item in operands])


def joined(one, two, pole, power, slope):
    cross = one[END] * two[START]
    return (
        power * one[END] + two[END],
        one[START] + power * two[START],
        slope * one[END] + power * one[DEND] + two[DEND],
        one[DSTART] + slope * two[START] + power * two[DSTART],
        one[RES] + two[RES] + pole * cross,
        one[POLE] + two[POLE] + cross + pole * (one[DEND] * two[START] + one[END] * two[DSTART]),
    )


def pair_kernel(own, other, rates, send0, send1, hold0, hold1, *, rows, modes):
    def body(one, two):
        for n in range(modes):
            r = rates[pl.ds(n * SUBS, SUBS), :]
            power = jnp.exp(-r * rows)
            read = lambda ref: [ref[pl.ds((a * modes + n) * SUBS, SUBS), :] for a in range(PARTS)]
            first, second = read(one), read(two)
            result = joined(
                first, second, jnp.exp(-r), power, jnp.exp(-r * (rows - 1)) * float(rows)
            )
            for a in range(PARTS):
                send0[pl.ds((a * modes + n) * 4, 4), :] = result[a][:4]
                send1[pl.ds((a * modes + n) * 4, 4), :] = result[a][4:]
            for a, item in enumerate((second[START], power)):
                hold0[pl.ds((a * modes + n) * 4, 4), :] = item[:4]
                hold1[pl.ds((a * modes + n) * 4, 4), :] = item[4:]

    core = position()[1]

    @pl.when(core == 0)
    def _():
        body(own, other)

    @pl.when(core != 0)
    def _():
        body(other, own)


def paired(own, other, rates, rows, modes):
    return local_call(
        functools.partial(pair_kernel, rows=rows, modes=modes),
        "paired",
        [(count * modes * 4, LANES) for count in (PARTS, PARTS, 2, 2)],
        [own, other, rates],
    )


def chain_kernel(*refs, rows, modes, scale):
    pieces, (rate, residues) = refs[:4], refs[4:6]
    backs, terms = refs[6:10], refs[10:14]
    ordered, adjoints, small, owned = refs[14:]
    chip, core, depth = position()
    size = modes * 4
    for j in range(4):
        ordered[chip ^ j] = pieces[j][...]
    for q in range(4):
        lanes = pl.ds(pl.multiple_of((8 * q + 2 * chip + core) * LANES, LANES), LANES)
        small[0, pl.ds(q, modes, stride=4), :] = rate[:, lanes]
        small[1, pl.ds(q, modes, stride=4), :] = residues[:, lanes]
    r = small[0]
    pole = jnp.exp(-r)
    power = jnp.exp(-r * rows)
    slope = jnp.exp(-r * (rows - 1)) * float(rows)
    read = lambda c, a: ordered[c, pl.ds(a * size, size), :]
    now, dnow = read(0, END), read(0, DEND)
    sum_res, sum_pole = read(0, RES), read(0, POLE)
    for c in range(1, 4):
        start, dstart = read(c, START), read(c, DSTART)
        cross = now * start
        sum_res = sum_res + read(c, RES) + pole * cross
        sum_pole = sum_pole + read(c, POLE) + cross + pole * (dnow * start + now * dstart)
        if c < 3:
            now, dnow = (
                power * now + read(c, END),
                slope * now + power * dnow + read(c, DEND),
            )
    back = jnp.zeros((size, LANES), f32)
    adjoints[3] = back
    for c in range(2, -1, -1):
        back = read(c + 1, START) + power * back
        adjoints[c] = back
    for j in range(4):
        backs[j][...] = adjoints[chip ^ j]
    owned[pl.ds(0, size), :] = sum_res * scale
    owned[pl.ds(size, size), :] = sum_pole * (-pole * small[1]) * scale
    for j in range(4):
        q = (depth + j) % 4
        for a in range(2):
            terms[j][pl.ds(a * modes, modes), :] = owned[pl.ds(a * size + q, modes, stride=4), :]


def chained(pieces, rate, residues, rows, scale):
    modes = rate.shape[0]
    size = modes * 4
    outs = local_call(
        functools.partial(chain_kernel, rows=rows, modes=modes, scale=scale),
        "chained",
        [(size, LANES)] * 4 + [(2 * modes, LANES)] * 4,
        [*pieces, rate, residues],
        [(4, PARTS * size, LANES), (4, size, LANES), (2, size, LANES), (2 * size, LANES)],
    )
    return outs[:4], outs[4:]


def entry_kernel(*refs, modes):
    backs, holds, mine, theirs = refs[:4], refs[4:8], refs[8], refs[9]
    size = modes * 4

    def body(late, early):
        for j in range(4):
            back = backs[j][...]
            late[pl.ds(j * size, size), :] = back
            early[pl.ds(j * size, size), :] = holds[j][:size, :] + holds[j][size:, :] * back

    core = position()[1]

    @pl.when(core == 0)
    def _():
        body(theirs, mine)

    @pl.when(core != 0)
    def _():
        body(mine, theirs)


def entries(backs, holds, modes):
    return local_call(
        functools.partial(entry_kernel, modes=modes),
        "entries",
        [(4 * modes * 4, LANES)] * 2,
        [*backs, *holds],
    )


def input_kernel(cot, rate, res, *refs, rows, modes, together):
    given, (out, cs, ys, ps, rs, ads, sent, done) = refs[:-8], refs[-8:]
    chip, half, _ = position() if len(given) == 2 else (None,) * 3
    width = SUBS * LANES

    def copy(q):
        lanes = pl.ds(pl.multiple_of(q * width, width), width)
        return pltpu.make_async_copy(sent.at[q], out.at[:, lanes], done.at[q])

    def one_block(q, carry):
        block_of_inputs(q, cot, rate, res, given, (chip, half), sent, (cs, ys, ps, rs, ads), rows, modes, together)
        copy(q).start()
        return carry

    count = cot.shape[1] // width
    lax.fori_loop(0, count, one_block, 0)
    for q in range(count):
        copy(q).wait()


def block_of_inputs(q, cot, rate, res, given, place, sent, scratch, rows, modes, together):
    cs, ys, ps, rs, ads = scratch
    size = modes * 4

    def tile(i):
        return pl.ds(pl.multiple_of((q * SUBS + i) * LANES, LANES), LANES)

    for i in range(SUBS):
        lanes = tile(i)
        cs[pl.ds(i, rows, stride=SUBS), :] = cot[:, lanes].astype(f32)
        ps[pl.ds(i, modes, stride=SUBS), :] = jnp.exp(-rate[:, lanes])
        rs[pl.ds(i, modes, stride=SUBS), :] = res[:, lanes]
    if len(given) == 1:
        spread([given[0][:, tile(i)] for i in range(SUBS)], ads, modes, SUBS)
    for j in range(4 if len(given) == 2 else 0):
        for core, source in enumerate(given):
            i = 2 * (place[0] ^ j) + (place[1] ^ core)
            ads[pl.ds(i, modes, stride=SUBS), :] = source[pl.ds(j * size + q, modes, stride=4), :]

    for group in range(modes // together):
        at = [pl.ds((group * together + m) * SUBS, SUBS) for m in range(together)]
        poles = [ps[a, :] for a in at]
        weights = [rs[a, :] for a in at]

        def step(index, adjoint):
            now = pl.ds(pl.multiple_of((rows - 1 - index) * SUBS, SUBS), SUBS)
            value = cs[now, :]
            adjoint = tuple(a * p + value for a, p in zip(adjoint, poles))
            terms = [a * w for a, w in zip(adjoint, weights)]
            while len(terms) > 1:
                terms = [a + b for a, b in zip(terms[::2], terms[1::2])]
            ys[now, :] = terms[0] if group == 0 else ys[now, :] + terms[0]
            return adjoint

        lax.fori_loop(0, rows, step, tuple(ads[a, :] for a in at), unroll=4)
    for i in range(SUBS):
        sent[q, :, pl.ds(i * LANES, LANES)] = ys[pl.ds(i, rows, stride=SUBS), :].astype(sent.dtype)


def input_gradients(cotangent, rate, residues, *given):
    rows, channels = cotangent.shape
    modes = rate.shape[0]
    width = SUBS * LANES
    scratch = lambda height: pltpu.VMEM((height * SUBS, LANES), f32)
    operands = (cotangent, rate, residues, *given)
    return pl.pallas_call(
        functools.partial(input_kernel, rows=rows, modes=modes, together=8),
        in_specs=[vmem() for _ in operands],
        out_specs=pl.BlockSpec(memory_space=pl.ANY),
        out_shape=jax.ShapeDtypeStruct((rows, channels), cotangent.dtype),
        scratch_shapes=[
            scratch(rows),
            scratch(rows),
            scratch(modes),
            scratch(modes),
            scratch(modes),
            pltpu.VMEM((channels // width, rows, width), cotangent.dtype),
            pltpu.SemaphoreType.DMA((channels // width,)),
        ],
        compiler_params=room(5),
        cost_estimate=pl.CostEstimate(
            flops=4 * rows * channels * modes,
            transcendentals=modes * channels,
            bytes_accessed=2 * rows * channels,
        ),
        name="input_gradients",
    )(*[here(item) for item in operands])


def place_kernel(*refs, modes):
    pieces, (out_res, out_rate) = refs[:4], refs[-2:]
    chip, half, _ = position()
    for j in range(4):
        for core in range(2):
            i = 2 * (chip ^ j) + (half ^ core)
            lanes = pl.ds(pl.multiple_of(i * LANES, LANES), LANES)
            out_res[:, lanes] = pieces[j][pl.ds(core * 2 * modes, modes), :]
            out_rate[:, lanes] = pieces[j][pl.ds((core * 2 + 1) * modes, modes), :]


def placed(pieces, modes, after):
    shape = jax.ShapeDtypeStruct((modes, SUBS * LANES), f32)
    return pl.pallas_call(
        functools.partial(place_kernel, modes=modes),
        in_specs=[vmem() for _ in pieces] + [pl.BlockSpec(memory_space=pltpu.HBM)],
        out_specs=[vmem(), vmem()],
        out_shape=[shape, shape],
        compiler_params=room(2),
        name="placed",
    )(
        *[here(item) for item in pieces],
        pltpu.with_memory_space_constraint(after, pltpu.HBM),
    )


def crossed(value, distance):
    return lax.ppermute(value, "context", [(i, i ^ distance) for i in range(8)])


def shifted(value, distance):
    return lax.ppermute(value, "dp", [(i, (i + distance) % 4) for i in range(4)])


def four_by_eight(inputs, cotangent, rate, residues):
    x, c = inputs[0], cotangent[0]
    rows, modes = x.shape[0], rate.shape[0]
    sends, holds, after = {}, {}, ()
    for chips in ((3, 2), (1, 0)):
        if after:
            away, _ = summaries(x, c, rate, pair_tiles(chips, 1), after)
        else:
            away, _, x, c, rate, residues = first_summaries(
                x, c, rate, residues, pair_tiles(chips, 1)
            )
        other = crossed(away, 1)
        own, rates = summaries(x, c, rate, pair_tiles(chips, 0))
        sends[chips[0]], sends[chips[1]], holds[chips[0]], holds[chips[1]] = paired(
            own, other, rates, rows, modes
        )
        after = (holds[chips[0]],)
    pieces = [sends[0]] + [crossed(sends[j], 2 * j) for j in (1, 2, 3)]
    scale = 1.0 / math.sqrt(4 * rows * 8)
    backs, terms = chained(pieces, rate, residues, 2 * rows, scale)
    shares = [terms[0]] + [shifted(terms[j], j) for j in (1, 2, 3)]
    backs = [backs[0]] + [crossed(backs[j], 2 * j) for j in (1, 2, 3)]
    mine, theirs = entries(backs, [holds[j] for j in range(4)], modes)
    theirs = crossed(theirs, 1)
    grad_inputs = input_gradients(c, rate, residues, mine, theirs)
    total = shares[0] + shares[1] + shares[2] + shares[3]
    both = jnp.concatenate([total, crossed(total, 1)])
    gathered = [both] + [crossed(both, 2 * j) for j in (1, 2, 3)]
    grad_residues, grad_rate = placed(gathered, modes, grad_inputs)
    return (grad_inputs[None], grad_residues, grad_rate)


def any_mesh(inputs, cotangent, rate, residues):
    x, c = inputs[0], cotangent[0]
    rows, channels, modes = x.shape[0], x.shape[1], rate.shape[0]
    count, mine = lax.axis_size("context"), lax.axis_index("context")
    blocks = [
        summaries(x, c, rate, next_tiles(first))[0]
        for first in range(0, channels // LANES, SUBS)
    ]
    local = jnp.stack(blocks).reshape(-1, PARTS, modes, SUBS * LANES)
    local = jnp.moveaxis(local, 0, 2).reshape(PARTS, modes, channels)
    slabs = lax.all_gather(local, "context")
    pole, power = jnp.exp(-rate), jnp.exp(-rate * rows)
    slope = jnp.exp(-rate * (rows - 1)) * rows
    total = tuple(slabs[0])
    for place in range(1, count):
        total = joined(total, slabs[place], pole, power, slope)
    zero = jnp.zeros_like(pole)

    def behind(index, entry):
        place = count - 1 - index
        return jnp.where(place > mine, slabs[place, START] + power * entry, entry)

    entry = lax.fori_loop(0, count, behind, zero)
    grad_inputs = input_gradients(c, rate, residues, entry)
    scale = 1.0 / math.sqrt(lax.axis_size("dp") * rows * count)
    terms = jnp.stack([total[RES], total[POLE] * (-pole * residues)]) * scale
    owned = lax.psum_scatter(terms, "dp", scatter_dimension=2, tiled=True)
    return (grad_inputs[None], owned[0], owned[1])


def solution(mesh):
    tuned = mesh.shape["dp"] == 4 and mesh.shape["context"] == 8
    in_specs = (P("dp", "context", None), P("dp", "context", None), P(), P())
    out_specs = (P("dp", "context", None), P(None, "dp"), P(None, "dp"))
    return jax.shard_map(
        four_by_eight if tuned else any_mesh, mesh=mesh, in_specs=in_specs, out_specs=out_specs, check_vma=False
    )
```

time: 80.7 us -> 55 us (0.68)
  Pallas kernels: 43.1 us -> 23.7 us
  local copies, waits for them, and re-layouts: 4.03 us -> 0 us
  other arithmetic: 1.34 us -> 0.01 us
    pallas_call x9, Pallas kernels: 33.5 us -> 15.8 us  [the longest x7 9.88 us: local_call(): pl.pallas_call(kernel, in_specs=[vmem() for _ in operands], out_specs=[vm...]
    unnamed x26 -> x0, local copies, waits for them, and re-layouts: 4.03 us -> none
    pallas_call x1, Pallas kernels: 9.64 us -> 7.88 us  [input_gradients(): pl.pallas_call(functools.partial(input_kernel, rows=rows, modes=modes, to...]
    ppermute x3, waiting for transfers between devices: 0.01 us -> 1.37 us  [shifted(): lax.ppermute(value, 'dp', [(i, (i + distance) % 4) for i in range(4)])]
    ppermute x3, starting transfers between devices: 5.75 us -> 4.83 us  [shifted(): lax.ppermute(value, 'dp', [(i, (i + distance) % 4) for i in range(4)])]
    ppermute x13, waiting for transfers between devices: 12.8 us -> 11.9 us  [crossed(): return lax.ppermute(value, 'context', [(i, i ^ distance) for i in range(8)])]
  transfers between devices with their start and end apart: 16 -> 16, of which waited for: 6 -> 5; matrix products, arithmetic and copies ran while one was open for 1% -> 0% of each run, Pallas kernels for 31% -> 26%
where the time goes in v2:
time: 55 us; the launch traced here: 54.9 us
  Pallas kernels  23.7 us (43%)
  starting transfers between devices  17.2 us (31%)
  waiting for transfers between devices  13.2 us (24%)
  between operations  0.77 us (1%)
    ppermute x13, starting transfers between devices, crossed(): return lax.ppermute(value, 'context', [(i, i ^ distance) for i in range(8)])  12.3 us
    ppermute x13, waiting for transfers between devices, crossed(): return lax.ppermute(value, 'context', [(i, i ^ distance) for i in range(8)])  11.9 us
    pallas_call x7, Pallas kernels, local_call(): pl.pallas_call(kernel, in_specs=[vmem() for _ in operands], out_specs=[vm...  9.88 us
    pallas_call x1, Pallas kernels, input_gradients(): pl.pallas_call(functools.partial(input_kernel, rows=rows, modes=modes, to...  7.88 us
    pallas_call x1, Pallas kernels, first_summaries(): pl.pallas_call(functools.partial(first_kernel, **static), in_specs=[pl.Bl...  5.25 us
    ppermute x3, starting transfers between devices, shifted(): lax.ppermute(value, 'dp', [(i, (i + distance) % 4) for i in range(4)])  4.83 us
    ppermute x3, waiting for transfers between devices, shifted(): lax.ppermute(value, 'dp', [(i, (i + distance) % 4) for i in range(4)])  1.37 us
  transfers between devices with their start and end apart: 16, of which 5 were waited for; matrix products, arithmetic and copies ran while one was open for 0% of the time, Pallas kernels for 26%

profile of v2, /device:TPU:0, one launch (start us, length us, event | category | flops | bytes accessed | tf_op | source)
XLA Modules:
  0.0 54.9 jit_solution(14069687432334328540)
XLA Ops:
  0.6 5.2 %first_summaries.1 = (f32[768,128]{1,0:T(8,128)S(1)}, f32[128,128]{1,0:T(8,128)}, bf16[128,4096]{1,0:T(8,128)(2,1)S(1)}, bf16[128,4096]{1,0:T(8,128)(2,1)S(1)}, ...) custom-call(bf16[128,4096]{1,0:T(8,128)(2,1)} %bitcast.4, bf16[128,4096]{1,0:T(8,128)(2,1)} %bitcast.5, f32[16,4096]{1,0:T(8,128)} %rate.1, ...), custom_call_target="tpu_custom_call" | custom-call | flops 20971520 | bytes 4194304 | tf_op jit(solution)/shard_map/first_summaries/pallas_call | solution.py:226
  5.9 0.5 collective-permute-start
  6.4 3.0 %summaries.4 = (f32[768,128]{1,0:T(8,128)S(1)}, f32[128,128]{1,0:T(8,128)S(1)}) custom-call(bf16[128,4096]{1,0:T(8,128)(2,1)S(1)} %get-tuple-element.36.x, bf16[128,4096]{1,0:T(8,128)(2,1)S(1)} %get-tuple-element.33.c.cot, f32[16,4096]{1,0:T(8,128)S(1)} %get-tuple-element.34.rate.refs_4_), custom_call_target="tpu_custom_call" | custom-call | flops 20971520 | bytes 4194304 | tf_op jit(solution)/shard_map/summaries/pallas_call | solution.py:41
  9.6 3.4 %summaries.5 = (f32[768,128]{1,0:T(8,128)S(1)}, f32[128,128]{1,0:T(8,128)}) custom-call(bf16[128,4096]{1,0:T(8,128)(2,1)S(1)} %get-tuple-element.36.x, bf16[128,4096]{1,0:T(8,128)(2,1)S(1)} %get-tuple-element.33.c.cot, f32[16,4096]{1,0:T(8,128)S(1)} %get-tuple-element.34.rate.refs_4_, f32[128,128]{1,0:T(8,128)S(1)} %get-tuple-element.41.refs_0_.refs_7_), custom_call_target="tpu_custom_call" | custom-call | flops 20971520 | bytes 4194304 | tf_op jit(solution)/shard_map/summaries/pallas_call | solution.py:41
  13.0 3.0 %summaries.3 = (f32[768,128]{1,0:T(8,128)S(1)}, f32[128,128]{1,0:T(8,128)S(1)}) custom-call(bf16[128,4096]{1,0:T(8,128)(2,1)S(1)} %get-tuple-element.36.x, bf16[128,4096]{1,0:T(8,128)(2,1)S(1)} %get-tuple-element.33.c.cot, f32[16,4096]{1,0:T(8,128)S(1)} %get-tuple-element.34.rate.refs_4_), custom_call_target="tpu_custom_call" | custom-call | flops 20971520 | bytes 4194304 | tf_op jit(solution)/shard_map/summaries/pallas_call | solution.py:41
  16.1 3.0 %collective-permute-start.3 = (f32[384,128]{1,0:T(8,128)S(1)}, f32[384,128]{1,0:T(8,128)S(1)}, u32[]{:S(2)}, u32[]{:S(2)}) collective-permute-start(f32[384,128]{1,0:T(8,128)S(1)} %get-tuple-element.46), channel_id=1, source_target_pairs={{0,4},{1,5},{2,6},{3,7},{4,0},{5,1},{6,2},{7,3},{8,12},{9,13},{10,... | collective-permute-start | bytes 589832 | tf_op jit(solution)/shard_map/ppermute | solution.py:492
  19.1 1.4 %collective-permute-start.4 = (f32[384,128]{1,0:T(8,128)S(1)}, f32[384,128]{1,0:T(8,128)S(1)}, u32[]{:S(2)}, u32[]{:S(2)}) collective-permute-start(f32[384,128]{1,0:T(8,128)S(1)} %get-tuple-element.47), channel_id=1, source_target_pairs={{0,6},{1,7},{2,4},{3,5},{4,2},{5,3},{6,0},{7,1},{8,14},{9,15},{10,... | collective-permute-start | bytes 589832 | tf_op jit(solution)/shard_map/ppermute | solution.py:492
  20.8 7.6 %collective-permute-done.3.refs_2_ = f32[384,128]{1,0:T(8,128)S(1)} collective-permute-done((f32[384,128]{1,0:T(8,128)S(1)}, f32[384,128]{1,0:T(8,128)S(1)}, u32[]{:S(2)}, u32[]{:S(2)}) %collective-permute-start.3) | collective-permute-done | bytes 196640 | tf_op jit(solution)/shard_map/ppermute | solution.py:492
  28.4 1.3 %collective-permute-done.2.refs_1_ = f32[384,128]{1,0:T(8,128)S(1)} collective-permute-done((f32[384,128]{1,0:T(8,128)S(1)}, f32[384,128]{1,0:T(8,128)S(1)}, u32[]{:S(2)}, u32[]{:S(2)}) %collective-permute-start.2) | collective-permute-done | bytes 196640 | tf_op jit(solution)/shard_map/ppermute | solution.py:492
  29.7 0.2 chained.1
  29.9 2.8 %collective-permute-start.10 = (f32[32,128]{1,0:T(8,128)S(1)}, f32[32,128]{1,0:T(8,128)S(1)}, u32[]{:S(2)}, u32[]{:S(2)}) collective-permute-start(f32[32,128]{1,0:T(8,128)S(1)} %get-tuple-element.59), channel_id=1, source_target_pairs={{0,16},{8,24},{16,0},{24,8},{1,17},{9,25},{17,1},{25,9},{2,18},{10... | collective-permute-start | bytes 49160 | tf_op jit(solution)/shard_map/ppermute | solution.py:496
  32.7 1.3 %collective-permute-start.11 = (f32[32,128]{1,0:T(8,128)S(1)}, f32[32,128]{1,0:T(8,128)S(1)}, u32[]{:S(2)}, u32[]{:S(2)}) collective-permute-start(f32[32,128]{1,0:T(8,128)S(1)} %get-tuple-element.60), channel_id=1, source_target_pairs={{0,24},{8,0},{16,8},{24,16},{1,25},{9,1},{17,9},{25,17},{2,26},{10... | collective-permute-start | bytes 49160 | tf_op jit(solution)/shard_map/ppermute | solution.py:496
  34.1 0.7 %collective-permute-start.9 = (f32[32,128]{1,0:T(8,128)S(1)}, f32[32,128]{1,0:T(8,128)S(1)}, u32[]{:S(2)}, u32[]{:S(2)}) collective-permute-start(f32[32,128]{1,0:T(8,128)S(1)} %get-tuple-element.58), channel_id=1, source_target_pairs={{0,8},{8,16},{16,24},{24,0},{1,9},{9,17},{17,25},{25,1},{2,10},{10... | collective-permute-start | bytes 49160 | tf_op jit(solution)/shard_map/ppermute | solution.py:496
  34.7 1.5 %collective-permute-start.5 = (f32[64,128]{1,0:T(8,128)S(1)}, f32[64,128]{1,0:T(8,128)S(1)}, u32[]{:S(2)}, u32[]{:S(2)}) collective-permute-start(f32[64,128]{1,0:T(8,128)S(1)} %get-tuple-element.49), channel_id=1, source_target_pairs={{0,2},{1,3},{2,0},{3,1},{4,6},{5,7},{6,4},{7,5},{8,10},{9,11},{10,... | collective-permute-start | bytes 98312 | tf_op jit(solution)/shard_map/ppermute | solution.py:492
  36.2 1.5 %collective-permute-start.6 = (f32[64,128]{1,0:T(8,128)S(1)}, f32[64,128]{1,0:T(8,128)S(1)}, u32[]{:S(2)}, u32[]{:S(2)}) collective-permute-start(f32[64,128]{1,0:T(8,128)S(1)} %get-tuple-element.50), channel_id=1, source_target_pairs={{0,4},{1,5},{2,6},{3,7},{4,0},{5,1},{6,2},{7,3},{8,12},{9,13},{10,... | collective-permute-start | bytes 98312 | tf_op jit(solution)/shard_map/ppermute | solution.py:492
  37.7 0.5 collective-permute-start.7
  38.2 1.4 %collective-permute-done.9 = f32[32,128]{1,0:T(8,128)S(1)} collective-permute-done((f32[32,128]{1,0:T(8,128)S(1)}, f32[32,128]{1,0:T(8,128)S(1)}, u32[]{:S(2)}, u32[]{:S(2)}) %collective-permute-start.9) | collective-permute-done | bytes 16416 | tf_op jit(solution)/shard_map/ppermute | solution.py:496
  39.6 0.5 collective-permute-done.6.refs_2_
  40.1 2.4 %collective-permute-done.7.refs_3_ = f32[64,128]{1,0:T(8,128)S(1)} collective-permute-done((f32[64,128]{1,0:T(8,128)S(1)}, f32[64,128]{1,0:T(8,128)S(1)}, u32[]{:S(2)}, u32[]{:S(2)}) %collective-permute-start.7) | collective-permute-done | bytes 32800 | tf_op jit(solution)/shard_map/ppermute | solution.py:492
  42.7 0.6 %collective-permute-start.13 = (f32[64,128]{1,0:T(8,128)S(1)}, f32[64,128]{1,0:T(8,128)S(1)}, u32[]{:S(2)}, u32[]{:S(2)}) collective-permute-start(f32[64,128]{1,0:T(8,128)S(1)} %pad_maximum_fusion.refs_0_), channel_id=1, source_target_pairs={{0,2},{1,3},{2,0},{3,1},{4,6},{5,7},{6,4},{7,5},{8,10},{9,11},{10,... | collective-permute-start | bytes 98312 | tf_op jit(solution)/shard_map/ppermute | solution.py:492
  43.3 0.5 collective-permute-start.14
  43.8 2.4 %collective-permute-start.15 = (f32[64,128]{1,0:T(8,128)S(1)}, f32[64,128]{1,0:T(8,128)S(1)}, u32[]{:S(2)}, u32[]{:S(2)}) collective-permute-start(f32[64,128]{1,0:T(8,128)S(1)} %pad_maximum_fusion.refs_0_), channel_id=1, source_target_pairs={{0,6},{1,7},{2,4},{3,5},{4,2},{5,3},{6,0},{7,1},{8,14},{9,15},{10,... | collective-permute-start | bytes 98312 | tf_op jit(solution)/shard_map/ppermute | solution.py:492
  46.3 7.9 %input_gradients.1.refs_4_ = bf16[128,4096]{1,0:T(8,128)(2,1)} custom-call(bf16[128,4096]{1,0:T(8,128)(2,1)S(1)} %get-tuple-element.33.c.cot, f32[16,4096]{1,0:T(8,128)S(1)} %get-tuple-element.34.rate.refs_4_, f32[16,4096]{1,0:T(8,128)S(1)} %get-tuple-element.35.refs_5_.res, f32[256,128]{1,0:T(8,128)S(1)} %get-tuple-element.55.refs_0_, ...), custom_call_target="tpu_custom_call" | custom-call | flops 33554432 | bytes 1048576 | tf_op jit(solution)/shard_map/input_gradients/pallas_call | solution.py:441
  54.2 0.7 %placed.1 = (f32[16,1024]{1,0:T(8,128)}, f32[16,1024]{1,0:T(8,128)}) custom-call(f32[64,128]{1,0:T(8,128)S(1)} %pad_maximum_fusion.refs_0_, f32[64,128]{1,0:T(8,128)S(1)} %collective-permute-done.13.refs_1_, f32[64,128]{1,0:T(8,128)S(1)} %collective-permute-done.14.refs_2_, f32[64,128]{1,0:T(8,128)S(1)} %collective-permute-done.15.refs_3_, ...), custom_call_target="tpu_custom_call" | custom-call | tf_op jit(solution)/shard_map/placed/pallas_call | solution.py:478
  (20 shorter events, 0.6 us)
Async XLA Ops:
  5.9 3.6 %collective-permute-start = (f32[768,128]{1,0:T(8,128)S(1)}, f32[768,128]{1,0:T(8,128)S(1)}, u32[]{:S(2)}, u32[]{:S(2)}) collective-permute-start(f32[768,128]{1,0:T(8,128)S(1)} %get-tuple-element.39), channel_id=1, source_target_pairs={{0,1},{1,0},{2,3},{3,2},{4,5},{5,4},{6,7},{7,6},{8,9},{9,8},{10,11... | collective-permute-start | bytes 1179656 | tf_op jit(solution)/shard_map/ppermute | solution.py:492
  13.0 7.6 %collective-permute-start.1 = (f32[768,128]{1,0:T(8,128)S(1)}, f32[768,128]{1,0:T(8,128)S(1)}, u32[]{:S(2)}, u32[]{:S(2)}) collective-permute-start(f32[768,128]{1,0:T(8,128)S(1)} %get-tuple-element.42), channel_id=1, source_target_pairs={{0,1},{1,0},{2,3},{3,2},{4,5},{5,4},{6,7},{7,6},{8,9},{9,8},{10,11... | collective-permute-start | bytes 1179656 | tf_op jit(solution)/shard_map/ppermute | solution.py:492
  16.1 12.3 %collective-permute-start.3 = (f32[384,128]{1,0:T(8,128)S(1)}, f32[384,128]{1,0:T(8,128)S(1)}, u32[]{:S(2)}, u32[]{:S(2)}) collective-permute-start(f32[384,128]{1,0:T(8,128)S(1)} %get-tuple-element.46), channel_id=1, source_target_pairs={{0,4},{1,5},{2,6},{3,7},{4,0},{5,1},{6,2},{7,3},{8,12},{9,13},{10,... | collective-permute-start | bytes 589832 | tf_op jit(solution)/shard_map/ppermute | solution.py:492
  19.1 9.3 %collective-permute-start.4 = (f32[384,128]{1,0:T(8,128)S(1)}, f32[384,128]{1,0:T(8,128)S(1)}, u32[]{:S(2)}, u32[]{:S(2)}) collective-permute-start(f32[384,128]{1,0:T(8,128)S(1)} %get-tuple-element.47), channel_id=1, source_target_pairs={{0,6},{1,7},{2,4},{3,5},{4,2},{5,3},{6,0},{7,1},{8,14},{9,15},{10,... | collective-permute-start | bytes 589832 | tf_op jit(solution)/shard_map/ppermute | solution.py:492
  20.7 9.1 %collective-permute-start.2 = (f32[384,128]{1,0:T(8,128)S(1)}, f32[384,128]{1,0:T(8,128)S(1)}, u32[]{:S(2)}, u32[]{:S(2)}) collective-permute-start(f32[384,128]{1,0:T(8,128)S(1)} %get-tuple-element.45), channel_id=1, source_target_pairs={{0,2},{1,3},{2,0},{3,1},{4,6},{5,7},{6,4},{7,5},{8,10},{9,11},{10,... | collective-permute-start | bytes 589832 | tf_op jit(solution)/shard_map/ppermute | solution.py:492
  29.9 7.8 %collective-permute-start.10 = (f32[32,128]{1,0:T(8,128)S(1)}, f32[32,128]{1,0:T(8,128)S(1)}, u32[]{:S(2)}, u32[]{:S(2)}) collective-permute-start(f32[32,128]{1,0:T(8,128)S(1)} %get-tuple-element.59), channel_id=1, source_target_pairs={{0,16},{8,24},{16,0},{24,8},{1,17},{9,25},{17,1},{25,9},{2,18},{10... | collective-permute-start | bytes 49160 | tf_op jit(solution)/shard_map/ppermute | solution.py:496
  32.7 5.5 %collective-permute-start.11 = (f32[32,128]{1,0:T(8,128)S(1)}, f32[32,128]{1,0:T(8,128)S(1)}, u32[]{:S(2)}, u32[]{:S(2)}) collective-permute-start(f32[32,128]{1,0:T(8,128)S(1)} %get-tuple-element.60), channel_id=1, source_target_pairs={{0,24},{8,0},{16,8},{24,16},{1,25},{9,1},{17,9},{25,17},{2,26},{10... | collective-permute-start | bytes 49160 | tf_op jit(solution)/shard_map/ppermute | solution.py:496
  34.1 5.5 %collective-permute-start.9 = (f32[32,128]{1,0:T(8,128)S(1)}, f32[32,128]{1,0:T(8,128)S(1)}, u32[]{:S(2)}, u32[]{:S(2)}) collective-permute-start(f32[32,128]{1,0:T(8,128)S(1)} %get-tuple-element.58), channel_id=1, source_target_pairs={{0,8},{8,16},{16,24},{24,0},{1,9},{9,17},{17,25},{25,1},{2,10},{10... | collective-permute-start | bytes 49160 | tf_op jit(solution)/shard_map/ppermute | solution.py:496
  34.7 4.9 %collective-permute-start.5 = (f32[64,128]{1,0:T(8,128)S(1)}, f32[64,128]{1,0:T(8,128)S(1)}, u32[]{:S(2)}, u32[]{:S(2)}) collective-permute-start(f32[64,128]{1,0:T(8,128)S(1)} %get-tuple-element.49), channel_id=1, source_target_pairs={{0,2},{1,3},{2,0},{3,1},{4,6},{5,7},{6,4},{7,5},{8,10},{9,11},{10,... | collective-permute-start | bytes 98312 | tf_op jit(solution)/shard_map/ppermute | solution.py:492
  36.2 3.9 %collective-permute-start.6 = (f32[64,128]{1,0:T(8,128)S(1)}, f32[64,128]{1,0:T(8,128)S(1)}, u32[]{:S(2)}, u32[]{:S(2)}) collective-permute-start(f32[64,128]{1,0:T(8,128)S(1)} %get-tuple-element.50), channel_id=1, source_target_pairs={{0,4},{1,5},{2,6},{3,7},{4,0},{5,1},{6,2},{7,3},{8,12},{9,13},{10,... | collective-permute-start | bytes 98312 | tf_op jit(solution)/shard_map/ppermute | solution.py:492
  37.7 4.8 %collective-permute-start.7 = (f32[64,128]{1,0:T(8,128)S(1)}, f32[64,128]{1,0:T(8,128)S(1)}, u32[]{:S(2)}, u32[]{:S(2)}) collective-permute-start(f32[64,128]{1,0:T(8,128)S(1)} %get-tuple-element.51), channel_id=1, source_target_pairs={{0,6},{1,7},{2,4},{3,5},{4,2},{5,3},{6,0},{7,1},{8,14},{9,15},{10,... | collective-permute-start | bytes 98312 | tf_op jit(solution)/shard_map/ppermute | solution.py:492
  39.6 3.1 %collective-permute-start.12 = (f32[32,128]{1,0:T(8,128)S(1)}, f32[32,128]{1,0:T(8,128)S(1)}, u32[]{:S(2)}, u32[]{:S(2)}) collective-permute-start(f32[32,128]{1,0:T(8,128)S(1)} %add_add_fusion), channel_id=1, source_target_pairs={{0,1},{1,0},{2,3},{3,2},{4,5},{5,4},{6,7},{7,6},{8,9},{9,8},{10,11... | collective-permute-start | bytes 49160 | tf_op jit(solution)/shard_map/ppermute | solution.py:492
  42.6 3.7 %collective-permute-start.8 = (f32[256,128]{1,0:T(8,128)S(1)}, f32[256,128]{1,0:T(8,128)S(1)}, u32[]{:S(2)}, u32[]{:S(2)}) collective-permute-start(f32[256,128]{1,0:T(8,128)S(1)} %get-tuple-element.56), channel_id=1, source_target_pairs={{0,1},{1,0},{2,3},{3,2},{4,5},{5,4},{6,7},{7,6},{8,9},{9,8},{10,11... | collective-permute-start | bytes 393224 | tf_op jit(solution)/shard_map/ppermute | solution.py:492
  42.7 11.4 %collective-permute-start.13 = (f32[64,128]{1,0:T(8,128)S(1)}, f32[64,128]{1,0:T(8,128)S(1)}, u32[]{:S(2)}, u32[]{:S(2)}) collective-permute-start(f32[64,128]{1,0:T(8,128)S(1)} %pad_maximum_fusion.refs_0_), channel_id=1, source_target_pairs={{0,2},{1,3},{2,0},{3,1},{4,6},{5,7},{6,4},{7,5},{8,10},{9,11},{10,... | collective-permute-start | bytes 98312 | tf_op jit(solution)/shard_map/ppermute | solution.py:492
  43.3 10.9 %collective-permute-start.14 = (f32[64,128]{1,0:T(8,128)S(1)}, f32[64,128]{1,0:T(8,128)S(1)}, u32[]{:S(2)}, u32[]{:S(2)}) collective-permute-start(f32[64,128]{1,0:T(8,128)S(1)} %pad_maximum_fusion.refs_0_), channel_id=1, source_target_pairs={{0,4},{1,5},{2,6},{3,7},{4,0},{5,1},{6,2},{7,3},{8,12},{9,13},{10,... | collective-permute-start | bytes 98312 | tf_op jit(solution)/shard_map/ppermute | solution.py:492
  43.8 10.4 %collective-permute-start.15 = (f32[64,128]{1,0:T(8,128)S(1)}, f32[64,128]{1,0:T(8,128)S(1)}, u32[]{:S(2)}, u32[]{:S(2)}) collective-permute-start(f32[64,128]{1,0:T(8,128)S(1)} %pad_maximum_fusion.refs_0_), channel_id=1, source_target_pairs={{0,6},{1,7},{2,4},{3,5},{4,2},{5,3},{6,0},{7,1},{8,14},{9,15},{10,... | collective-permute-start | bytes 98312 | tf_op jit(solution)/shard_map/ppermute | solution.py:492

commit v3 on v2

--- a/solution.py
+++ b/solution.py
@@ -12,6 +12,7 @@
 SUBS = 8
 SPAN = 8
 PARTS = 6
+ORDER = (3, 2, 1, 0)
 END, START, DEND, DSTART, RES, POLE = range(PARTS)
 f32 = jnp.float32
 
@@ -33,21 +34,16 @@
     return pltpu.CompilerParams(vmem_limit_bytes=megabytes << 20)
 
 
-def work(operations, touched):
-    return pl.CostEstimate(flops=operations, transcendentals=0, bytes_accessed=touched)
-
-
-def local_call(kernel, name, shapes, operands, scratch=(), megabytes=2, cost=None):
+def local_call(kernel, name, shapes, operands, scratch=(), megabytes=2, after=()):
     return pl.pallas_call(
         kernel,
-        in_specs=[vmem() for _ in operands],
+        in_specs=[vmem() for _ in operands] + [far_away() for _ in after],
         out_specs=[vmem() for _ in shapes],
         out_shape=[pltpu.VMEM(shape, f32) for shape in shapes],
         scratch_shapes=[pltpu.VMEM(shape, f32) for shape in scratch],
         compiler_params=room(megabytes),
-        cost_estimate=cost,
         name=name,
-    )(*[here(item) for item in operands])
+    )(*[here(item) for item in operands], *[outside(item) for item in after])
 
 
 def horner(values, point):
@@ -70,19 +66,20 @@
 
 
 def summary_kernel(x, c, rate, *refs, **static):
-    summarize(x, c, rate, *refs[-5:], **static)
-
-
-def first_kernel(x, c, rate, res, out, rate_out, x_in, c_in, rate_in, res_in, xs, cs, kept, done, **static):
+    summarize(x, c, rate, *refs[-7:], **static)
+
+
+def first_kernel(*refs, **static):
+    x, c, rate, res, *outs, x_in, c_in, rate_in, res_in, xs, cs, held, kept, done = refs
     chip, _, _ = position()
-    width = 4 * LANES
+    width = 2 * LANES
     copies = []
-    for pair in range(2):
+    for away in ORDER:
         for q in range(4):
-            start = 8 * LANES * q + width * ((chip // 2) ^ (1 - pair))
+            start = 8 * LANES * q + width * (chip ^ away)
             lanes = pl.ds(pl.multiple_of(start, width), width)
             copies += [(ref.at[:, lanes], into.at[:, lanes]) for ref, into in ((x, x_in), (c, c_in))]
-        if pair == 0:
+        if away == ORDER[0]:
             copies.append((rate, rate_in))
     copies.append((res, res_in))
     copies = [
@@ -93,18 +90,18 @@
         copy.start()
     for copy in copies[:9]:
         copy.wait()
-    summarize(x_in, c_in, rate_in, out, rate_out, xs, cs, kept, **static)
+    summarize(x_in, c_in, rate_in, *outs, xs, cs, held, kept, **static)
     for copy in copies[9:]:
         copy.wait()
 
 
-def summarize(x, c, rate, out, rate_out, xs, cs, kept, *, tile_of, rows, modes, together):
+def summarize(x, c, rate, theirs, ours, our_rates, xs, cs, rates, kept, *, tile_of, rows, modes, together):
     blocks = rows // SPAN
     for place in range(SUBS):
         lanes = pl.ds(pl.multiple_of(tile_of(place) * LANES, LANES), LANES)
         xs[pl.ds(place, rows, stride=SUBS), :] = x[:, lanes].astype(f32)
         cs[pl.ds(place, rows, stride=SUBS), :] = c[:, lanes].astype(f32)
-        rate_out[pl.ds(place, modes, stride=SUBS), :] = rate[:, lanes]
+        rates[pl.ds(place, modes, stride=SUBS), :] = rate[:, lanes]
 
     def row(ref, index):
         return ref[pl.ds(pl.multiple_of(index * SUBS, SUBS), SUBS), :]
@@ -127,10 +124,10 @@
 
     def some_modes(group, carry):
         ids = [group * together + m for m in range(together)]
-        rates = [row(rate_out, n) for n in ids]
-        poles = [jnp.exp(-r) for r in rates]
-        spans = [jnp.exp(-r * SPAN) for r in rates]
-        slopes = [jnp.exp(-r * (SPAN - 1)) * SPAN for r in rates]
+        decays = [row(rates, n) for n in ids]
+        poles = [jnp.exp(-r) for r in decays]
+        spans = [jnp.exp(-r * SPAN) for r in decays]
+        slopes = [jnp.exp(-r * (SPAN - 1)) * SPAN for r in decays]
 
         def forward(block, state):
             xv = [row(xs, block * SPAN + k) for k in range(SPAN)]
@@ -184,17 +181,19 @@
                 first + poles[m] * second + slope,
             )
             for part in range(PARTS):
-                base = pl.multiple_of((part * modes + ids[m]) * SUBS, SUBS)
-                out[pl.ds(base, SUBS), :] = results[part]
+                half = pl.ds((part * modes + ids[m]) * 4, 4)
+                theirs[half, :] = results[part][:4]
+                ours[half, :] = results[part][4:]
+            our_rates[pl.ds(ids[m] * 4, 4), :] = decays[m][4:]
         return carry
 
     lax.fori_loop(0, modes // together, some_modes, 0)
 
 
-def pair_tiles(chips, core):
+def chip_tiles(away):
     def tile_of(place):
         chip, half, _ = position()
-        return 8 * (place % 4) + 2 * (chip ^ chips[place // 4]) + (half ^ core)
+        return 8 * (place % 4) + 2 * (chip ^ away) + (half ^ (1 - place // 4))
 
     return tile_of
 
@@ -207,34 +206,33 @@
     together = 2
     kept = (2 * together * rows // SPAN + SPAN) * SUBS
     static = dict(tile_of=tile_of, rows=rows, modes=modes, together=together)
-    shapes = [(PARTS * modes * SUBS, LANES), (modes * SUBS, LANES)]
-    cost = work(10 * rows * modes * SUBS * LANES, 4 << 20)
-    return static, shapes, [(rows * SUBS, LANES), (rows * SUBS, LANES), (kept, LANES)], cost
+    shapes = [(PARTS * modes * 4, LANES), (PARTS * modes * 4, LANES), (modes * 4, LANES)]
+    scratch = [(rows * SUBS, LANES), (rows * SUBS, LANES), (modes * SUBS, LANES), (kept, LANES)]
+    return static, shapes, scratch
 
 
 def summaries(inputs, cotangent, rate, tile_of, after=()):
-    static, shapes, scratch, cost = summary_parts(inputs.shape[0], rate.shape[0], tile_of)
+    static, shapes, scratch = summary_parts(inputs.shape[0], rate.shape[0], tile_of)
     kernel = functools.partial(summary_kernel, **static)
     return local_call(
-        kernel, "summaries", shapes, [inputs, cotangent, rate, *after], scratch, 4, cost
+        kernel, "summaries", shapes, [inputs, cotangent, rate, *after], scratch, megabytes=4
     )
 
 
 def first_summaries(inputs, cotangent, rate, residues, tile_of):
-    static, shapes, scratch, cost = summary_parts(inputs.shape[0], rate.shape[0], tile_of)
+    static, shapes, scratch = summary_parts(inputs.shape[0], rate.shape[0], tile_of)
     operands = (inputs, cotangent, rate, residues)
     return pl.pallas_call(
         functools.partial(first_kernel, **static),
-        in_specs=[pl.BlockSpec(memory_space=pltpu.HBM) for _ in operands],
-        out_specs=[vmem() for _ in range(6)],
+        in_specs=[far_away() for _ in operands],
+        out_specs=[vmem() for _ in range(len(shapes) + 4)],
         out_shape=[pltpu.VMEM(shape, f32) for shape in shapes]
         + [pltpu.VMEM(item.shape, item.dtype) for item in operands],
         scratch_shapes=[pltpu.VMEM(shape, f32) for shape in scratch]
-        + [pltpu.SemaphoreType.DMA((18,))],
+        + [pltpu.SemaphoreType.DMA((34,))],
         compiler_params=room(4),
-        cost_estimate=cost,
         name="first_summaries",
-    )(*[pltpu.with_memory_space_constraint(item, pltpu.HBM) for item in operands])
+    )(*[outside(item) for item in operands])
 
 
 def joined(one, two, pole, power, slope):
@@ -249,22 +247,21 @@
     )
 
 
-def pair_kernel(own, other, rates, send0, send1, hold0, hold1, *, rows, modes):
+def pair_kernel(own, other, rates, *refs, rows, modes):
+    send, hold = refs[-2:]
+    size = modes * 4
+
     def body(one, two):
-        for n in range(modes):
-            r = rates[pl.ds(n * SUBS, SUBS), :]
-            power = jnp.exp(-r * rows)
-            read = lambda ref: [ref[pl.ds((a * modes + n) * SUBS, SUBS), :] for a in range(PARTS)]
-            first, second = read(one), read(two)
-            result = joined(
-                first, second, jnp.exp(-r), power, jnp.exp(-r * (rows - 1)) * float(rows)
-            )
-            for a in range(PARTS):
-                send0[pl.ds((a * modes + n) * 4, 4), :] = result[a][:4]
-                send1[pl.ds((a * modes + n) * 4, 4), :] = result[a][4:]
-            for a, item in enumerate((second[START], power)):
-                hold0[pl.ds((a * modes + n) * 4, 4), :] = item[:4]
-                hold1[pl.ds((a * modes + n) * 4, 4), :] = item[4:]
+        r = rates[...]
+        power = jnp.exp(-r * rows)
+        slope = jnp.exp(-r * (rows - 1)) * float(rows)
+        read = lambda ref: [ref[pl.ds(a * size, size), :] for a in range(PARTS)]
+        second = read(two)
+        result = joined(read(one), second, jnp.exp(-r), power, slope)
+        for a in range(PARTS):
+            send[pl.ds(a * size, size), :] = result[a]
+        hold[pl.ds(0, size), :] = second[START]
+        hold[pl.ds(size, size), :] = power
 
     core = position()[1]
 
@@ -277,19 +274,19 @@
         body(other, own)
 
 
-def paired(own, other, rates, rows, modes):
+def paired(own, other, rates, rows, modes, after):
     return local_call(
         functools.partial(pair_kernel, rows=rows, modes=modes),
         "paired",
-        [(count * modes * 4, LANES) for count in (PARTS, PARTS, 2, 2)],
-        [own, other, rates],
+        [(PARTS * modes * 4, LANES), (2 * modes * 4, LANES)],
+        [own, other, rates, *after],
     )
 
 
 def chain_kernel(*refs, rows, modes, scale):
     pieces, (rate, residues) = refs[:4], refs[4:6]
-    backs, terms = refs[6:10], refs[10:14]
-    ordered, adjoints, small, owned = refs[14:]
+    back_keep, back_send, term_keep, term_send = refs[6:10]
+    ordered, adjoints, small, owned = refs[10:]
     chip, core, depth = position()
     size = modes * 4
     for j in range(4):
@@ -320,36 +317,61 @@
     for c in range(2, -1, -1):
         back = read(c + 1, START) + power * back
         adjoints[c] = back
-    for j in range(4):
-        backs[j][...] = adjoints[chip ^ j]
+    for place in range(2):
+        rows_of = pl.ds(place * size, size)
+        back_keep[rows_of, :] = adjoints[chip ^ (2 * place)]
+        back_send[rows_of, :] = adjoints[chip ^ (2 * place + 1)]
     owned[pl.ds(0, size), :] = sum_res * scale
     owned[pl.ds(size, size), :] = sum_pole * (-pole * small[1]) * scale
-    for j in range(4):
-        q = (depth + j) % 4
-        for a in range(2):
-            terms[j][pl.ds(a * modes, modes), :] = owned[pl.ds(a * size + q, modes, stride=4), :]
+    for place in range(2):
+        for ref, q in ((term_keep, 2 * place + depth % 2), (term_send, 2 * place + 1 - depth % 2)):
+            for a in range(2):
+                ref[pl.ds((place * 2 + a) * modes, modes), :] = owned[
+                    pl.ds(a * size + q, modes, stride=4), :
+                ]
 
 
 def chained(pieces, rate, residues, rows, scale):
     modes = rate.shape[0]
     size = modes * 4
-    outs = local_call(
+    return local_call(
         functools.partial(chain_kernel, rows=rows, modes=modes, scale=scale),
         "chained",
-        [(size, LANES)] * 4 + [(2 * modes, LANES)] * 4,
+        [(2 * size, LANES)] * 2 + [(4 * modes, LANES)] * 2,
         [*pieces, rate, residues],
         [(4, PARTS * size, LANES), (4, size, LANES), (2, size, LANES), (2 * size, LANES)],
     )
-    return outs[:4], outs[4:]
+
+
+def halve_kernel(kept, got, keep, send):
+    upper = position()[2] // 2
+    half = kept.shape[0] // 2
+    for ref, place in ((keep, upper), (send, 1 - upper)):
+        at = pl.ds(pl.multiple_of(place * half, half), half)
+        ref[...] = kept[at, :] + got[at, :]
+
+
+def stack_kernel(one, two, *refs):
+    out = refs[-1]
+    half = out.shape[0] // 2
+    out[:half, :] = one[-half:, :]
+    out[half:, :] = two[-half:, :]
+
+
+def stacked(one, two, rows, after=(), near=()):
+    operands = [one, two, *near]
+    return local_call(stack_kernel, "stacked", [(2 * rows, LANES)], operands, after=after)[0]
 
 
 def entry_kernel(*refs, modes):
-    backs, holds, mine, theirs = refs[:4], refs[4:8], refs[8], refs[9]
+    kept, near, far = refs[:3]
+    holds, (mine, theirs) = refs[3:7], refs[-2:]
     size = modes * 4
+    backs = [kept[:size, :], near[:size, :], far[:size, :], far[size:, :]]
 
     def body(late, early):
         for j in range(4):
-            back = backs[j][...]
+            back = backs[j]
             late[pl.ds(j * size, size), :] = back
             early[pl.ds(j * size, size), :] = holds[j][:size, :] + holds[j][size:, :] * back
 
@@ -364,30 +386,43 @@
         body(mine, theirs)
 
 
-def entries(backs, holds, modes):
+def entries(backs, holds, modes, after):
     return local_call(
         functools.partial(entry_kernel, modes=modes),
         "entries",
         [(4 * modes * 4, LANES)] * 2,
-        [*backs, *holds],
-    )
-
-
-def input_kernel(cot, rate, res, *refs, rows, modes, together):
+        [*backs, *holds, *after],
+    )
+
+
+def input_kernel(cot, rate, res, *refs, blocks, rows, modes, together):
     given, (out, cs, ys, ps, rs, ads, sent, done) = refs[:-8], refs[-8:]
+    given = [ref for ref in given if ref.dtype == f32]
     chip, half, _ = position() if len(given) == 2 else (None,) * 3
     width = SUBS * LANES
+    first, count = blocks
 
     def copy(q):
-        lanes = pl.ds(pl.multiple_of(q * width, width), width)
+        lanes = pl.ds(pl.multiple_of((first + q) * width, width), width)
         return pltpu.make_async_copy(sent.at[q], out.at[:, lanes], done.at[q])
 
     def one_block(q, carry):
-        block_of_inputs(q, cot, rate, res, given, (chip, half), sent, (cs, ys, ps, rs, ads), rows, modes, together)
+        block_of_inputs(
+            first + q,
+            cot,
+            rate,
+            res,
+            given,
+            (chip, half),
+            sent.at[q],
+            (cs, ys, ps, rs, ads),
+            rows,
+            modes,
+            together,
+        )
         copy(q).start()
         return carry
 
-    count = cot.shape[1] // width
     lax.fori_loop(0, count, one_block, 0)
     for q in range(count):
         copy(q).wait()
@@ -427,21 +462,35 @@
             ys[now, :] = terms[0] if group == 0 else ys[now, :] + terms[0]
             return adjoint
 
-        lax.fori_loop(0, rows, step, tuple(ads[a, :] for a in at), unroll=4)
+        lax.fori_loop(0, rows, step, tuple(ads[a, :] for a in at), unroll=8)
     for i in range(SUBS):
-        sent[q, :, pl.ds(i * LANES, LANES)] = ys[pl.ds(i, rows, stride=SUBS), :].astype(sent.dtype)
-
-
-def input_gradients(cotangent, rate, residues, *given):
+        sent[:, pl.ds(i * LANES, LANES)] = ys[pl.ds(i, rows, stride=SUBS), :].astype(sent.dtype)
+
+
+def far_away():
+    return pl.BlockSpec(memory_space=pltpu.HBM)
+
+
+def outside(value):
+    return pltpu.with_memory_space_constraint(value, pltpu.HBM)
+
+
+def input_gradients(cotangent, rate, residues, given, blocks, onto=None):
     rows, channels = cotangent.shape
     modes = rate.shape[0]
     width = SUBS * LANES
     scratch = lambda height: pltpu.VMEM((height * SUBS, LANES), f32)
-    operands = (cotangent, rate, residues, *given)
+    operands = [here(item) for item in (cotangent, rate, residues, *given)]
+    specs = [vmem() for _ in operands]
+    aliases = {}
+    if onto is not None:
+        aliases = {len(operands): 0}
+        operands.append(outside(onto))
+        specs.append(far_away())
     return pl.pallas_call(
-        functools.partial(input_kernel, rows=rows, modes=modes, together=8),
-        in_specs=[vmem() for _ in operands],
-        out_specs=pl.BlockSpec(memory_space=pl.ANY),
+        functools.partial(input_kernel, blocks=blocks, rows=rows, modes=modes, together=16),
+        in_specs=specs,
+        out_specs=far_away(),
         out_shape=jax.ShapeDtypeStruct((rows, channels), cotangent.dtype),
         scratch_shapes=[
             scratch(rows),
@@ -449,42 +498,39 @@
             scratch(modes),
             scratch(modes),
             scratch(modes),
-            pltpu.VMEM((channels // width, rows, width), cotangent.dtype),
-            pltpu.SemaphoreType.DMA((channels // width,)),
+            pltpu.VMEM((blocks[1], rows, width), cotangent.dtype),
+            pltpu.SemaphoreType.DMA((blocks[1],)),
         ],
+        input_output_aliases=aliases,
         compiler_params=room(5),
-        cost_estimate=pl.CostEstimate(
-            flops=4 * rows * channels * modes,
-            transcendentals=modes * channels,
-            bytes_accessed=2 * rows * channels,
-        ),
         name="input_gradients",
-    )(*[here(item) for item in operands])
+    )(*operands)
 
 
 def place_kernel(*refs, modes):
-    pieces, (out_res, out_rate) = refs[:4], refs[-2:]
+    pieces, (out_res, out_rate) = refs[:2], refs[-2:]
     chip, half, _ = position()
     for j in range(4):
         for core in range(2):
             i = 2 * (chip ^ j) + (half ^ core)
             lanes = pl.ds(pl.multiple_of(i * LANES, LANES), LANES)
-            out_res[:, lanes] = pieces[j][pl.ds(core * 2 * modes, modes), :]
-            out_rate[:, lanes] = pieces[j][pl.ds((core * 2 + 1) * modes, modes), :]
+            row = ((j % 2) * 2 + core) * 2 * modes
+            out_res[:, lanes] = pieces[j // 2][pl.ds(row, modes), :]
+            out_rate[:, lanes] = pieces[j // 2][pl.ds(row + modes, modes), :]
 
 
 def placed(pieces, modes, after):
     shape = jax.ShapeDtypeStruct((modes, SUBS * LANES), f32)
     return pl.pallas_call(
         functools.partial(place_kernel, modes=modes),
-        in_specs=[vmem() for _ in pieces] + [pl.BlockSpec(memory_space=pltpu.HBM)],
+        in_specs=[vmem() for _ in pieces] + [far_away()],
         out_specs=[vmem(), vmem()],
         out_shape=[shape, shape],
         compiler_params=room(2),
         name="placed",
     )(
         *[here(item) for item in pieces],
-        pltpu.with_memory_space_constraint(after, pltpu.HBM),
+        outside(after),
     )
 
 
@@ -493,38 +539,54 @@
 
 
 def shifted(value, distance):
-    return lax.ppermute(value, "dp", [(i, (i + distance) % 4) for i in range(4)])
+    return lax.ppermute(value, "dp", [(i, i ^ distance) for i in range(4)])
 
 
 def four_by_eight(inputs, cotangent, rate, residues):
     x, c = inputs[0], cotangent[0]
     rows, modes = x.shape[0], rate.shape[0]
-    sends, holds, after = {}, {}, ()
-    for chips in ((3, 2), (1, 0)):
-        if after:
-            away, _ = summaries(x, c, rate, pair_tiles(chips, 1), after)
-        else:
-            away, _, x, c, rate, residues = first_summaries(
-                x, c, rate, residues, pair_tiles(chips, 1)
-            )
-        other = crossed(away, 1)
-        own, rates = summaries(x, c, rate, pair_tiles(chips, 0))
-        sends[chips[0]], sends[chips[1]], holds[chips[0]], holds[chips[1]] = paired(
-            own, other, rates, rows, modes
-        )
-        after = (holds[chips[0]],)
-    pieces = [sends[0]] + [crossed(sends[j], 2 * j) for j in (1, 2, 3)]
+    theirs, ours, rates, x, c, rate, residues = first_summaries(
+        x, c, rate, residues, chip_tiles(ORDER[0])
+    )
+    sends, holds, got = {}, {}, {}
+    waiting = (ORDER[0], ours, crossed(theirs, 1), rates)
+
+    def pair(waiting, after=()):
+        away, ours, others, rates = waiting
+        sends[away], holds[away] = paired(ours, others, rates, rows, modes, after)
+        if away:
+            got[away] = crossed(sends[away], 2 * away)
+
+    for away in ORDER[1:]:
+        if away == 0:
+            pair(waiting, (landed,))
+        after = {2: (), 1: (holds.get(3),), 0: (holds.get(2), holds.get(1))}[away]
+        theirs, ours, next_rates = summaries(x, c, rate, chip_tiles(away), after)
+        if away == 1:
+            landed = stacked(got[3], next_rates, 8)
+            pair(waiting, (landed,))
+        elif away:
+            pair(waiting, (next_rates,))
+        waiting = (away, ours, crossed(theirs, 1), next_rates)
+    pair(waiting, (stacked(got[1], got[2], 8),))
     scale = 1.0 / math.sqrt(4 * rows * 8)
-    backs, terms = chained(pieces, rate, residues, 2 * rows, scale)
-    shares = [terms[0]] + [shifted(terms[j], j) for j in (1, 2, 3)]
-    backs = [backs[0]] + [crossed(backs[j], 2 * j) for j in (1, 2, 3)]
-    mine, theirs = entries(backs, [holds[j] for j in range(4)], modes)
-    theirs = crossed(theirs, 1)
-    grad_inputs = input_gradients(c, rate, residues, mine, theirs)
-    total = shares[0] + shares[1] + shares[2] + shares[3]
-    both = jnp.concatenate([total, crossed(total, 1)])
-    gathered = [both] + [crossed(both, 2 * j) for j in (1, 2, 3)]
-    grad_residues, grad_rate = placed(gathered, modes, grad_inputs)
+    back_keep, back_send, term_keep, term_send = chained(
+        [sends[0], got[1], got[2], got[3]], rate, residues, 2 * rows, scale
+    )
+    half = (2 * modes, LANES)
+    keep, send = local_call(
+        halve_kernel, "halved", [half, half], [term_keep, shifted(term_send, 1)]
+    )
+    near = crossed(back_send, 2)
+    total = keep + shifted(send, 2)
+    far = crossed(stacked(back_keep, near, 4 * modes, (), (send,)), 4)
+    mine, others = entries([back_keep, near, far], [holds[j] for j in range(4)], modes, (total,))
+    entry = (mine, crossed(others, 1))
+    both = stacked(total, crossed(total, 1), 2 * modes)
+    grad_inputs = input_gradients(c, rate, residues, entry, (0, 2))
+    four = stacked(both, crossed(both, 2), 4 * modes, (grad_inputs,))
+    grad_inputs = input_gradients(c, rate, residues, entry, (2, 2), grad_inputs)
+    grad_residues, grad_rate = placed([four, crossed(four, 4)], modes, grad_inputs)
     return (grad_inputs[None], grad_residues, grad_rate)
 
 
@@ -533,10 +595,10 @@
     rows, channels, modes = x.shape[0], x.shape[1], rate.shape[0]
     count, mine = lax.axis_size("context"), lax.axis_index("context")
     blocks = [
-        summaries(x, c, rate, next_tiles(first))[0]
-        for first in range(0, channels // LANES, SUBS)
+        summaries(x, c, rate, next_tiles(first))[:2] for first in range(0, channels // LANES, SUBS)
     ]
-    local = jnp.stack(blocks).reshape(-1, PARTS, modes, SUBS * LANES)
+    local = jnp.stack([half for pair in blocks for half in pair])
+    local = local.reshape(-1, PARTS, modes, 4 * LANES)
     local = jnp.moveaxis(local, 0, 2).reshape(PARTS, modes, channels)
     slabs = lax.all_gather(local, "context")
     pole, power = jnp.exp(-rate), jnp.exp(-rate * rows)
@@ -551,7 +613,8 @@
         return jnp.where(place > mine, slabs[place, START] + power * entry, entry)
 
     entry = lax.fori_loop(0, count, behind, zero)
-    grad_inputs = input_gradients(c, rate, residues, entry)
+    blocks = (0, channels // (SUBS * LANES))
+    grad_inputs = input_gradients(c, rate, residues, [entry], blocks)
     scale = 1.0 / math.sqrt(lax.axis_size("dp") * rows * count)
     terms = jnp.stack([total[RES], total[POLE] * (-pole * residues)]) * scale
     owned = lax.psum_scatter(terms, "dp", scatter_dimension=2, tiled=True)

time: 55 us -> 48.9 us (0.89)
  waiting for transfers between devices: 13.2 us -> 8.83 us
  Pallas kernels: 23.7 us -> 22.1 us
    ppermute x13, waiting for transfers between devices: 11.9 us -> 4.45 us  [crossed(): return lax.ppermute(value, 'context', [(i, i ^ distance) for i in range(8)])]
    ppermute x3 -> x2, waiting for transfers between devices: 1.37 us -> 4.39 us  [shifted(): return lax.ppermute(value, 'dp', [(i, i ^ distance) for i in range(4)])]
    pallas_call x9 -> x18, Pallas kernels: 23 us -> 21.4 us  [the longest x15 9.53 us: local_call(): pl.pallas_call(kernel, in_specs=[vmem() for _ in operands] + [far_away()...]
    ppermute x3 -> x2, starting transfers between devices: 4.83 us -> 4.17 us  [shifted(): return lax.ppermute(value, 'dp', [(i, i ^ distance) for i in range(4)])]
  transfers between devices with their start and end apart: 16 -> 15, of which waited for: 5 -> 6; matrix products, arithmetic and copies ran while one was open for 0% -> 0% of each run, Pallas kernels for 26% -> 34%
where the time goes in v3:
time: 48.9 us; the launch traced here: 48.7 us
  Pallas kernels  22.1 us (45%)
  starting transfers between devices  17 us (35%)
  waiting for transfers between devices  8.83 us (18%)
  between operations  0.8 us (2%)
    ppermute x13, starting transfers between devices, crossed(): return lax.ppermute(value, 'context', [(i, i ^ distance) for i in range(8)])  12.9 us
    pallas_call x15, Pallas kernels, local_call(): pl.pallas_call(kernel, in_specs=[vmem() for _ in operands] + [far_away()...  9.53 us
    pallas_call x2, Pallas kernels, input_gradients(): pl.pallas_call(functools.partial(input_kernel, blocks=blocks, rows=rows,...  7.23 us
    pallas_call x1, Pallas kernels, first_summaries(): pl.pallas_call(functools.partial(first_kernel, **static), in_specs=[far_a...  4.62 us
    ppermute x13, waiting for transfers between devices, crossed(): return lax.ppermute(value, 'context', [(i, i ^ distance) for i in range(8)])  4.45 us
    ppermute x2, waiting for transfers between devices, shifted(): return lax.ppermute(value, 'dp', [(i, i ^ distance) for i in range(4)])  4.39 us
    ppermute x2, starting transfers between devices, shifted(): return lax.ppermute(value, 'dp', [(i, i ^ distance) for i in range(4)])  4.17 us
  transfers between devices with their start and end apart: 15, of which 6 were waited for; matrix products, arithmetic and copies ran while one was open for 0% of the time, Pallas kernels for 34%

profile of v3, /device:TPU:0, one launch (start us, length us, event | category | flops | bytes accessed | tf_op | source)
XLA Modules:
  0.0 48.7 jit_solution(10273855843117212590)
XLA Ops:
  0.6 4.6 %first_summaries.1 = (f32[384,128]{1,0:T(8,128)S(1)}, f32[384,128]{1,0:T(8,128)S(1)}, f32[64,128]{1,0:T(8,128)S(1)}, bf16[128,4096]{1,0:T(8,128)(2,1)S(1)}, bf16...) custom-call(bf16[128,4096]{1,0:T(8,128)(2,1)} %bitcast.4, bf16[128,4096]{1,0:T(8,128)(2,1)} %bitcast.5, ...), custom_call_target="tpu_custom_call" | custom-call | tf_op jit(solution)/shard_map/first_summaries/pallas_call | solution.py:225
  5.3 0.5 %collective-permute-start.1 = (f32[384,128]{1,0:T(8,128)S(1)}, f32[384,128]{1,0:T(8,128)S(1)}, u32[]{:S(2)}, u32[]{:S(2)}) collective-permute-start(f32[384,128]{1,0:T(8,128)S(1)} %get-tuple-element.45), channel_id=1, source_target_pairs={{0,1},{1,0},{2,3},{3,2},{4,5},{5,4},{6,7},{7,6},{8,9},{9,8},{10,11... | collective-permute-start | bytes 589832 | tf_op jit(solution)/shard_map/ppermute | solution.py:538
  5.8 3.0 %summaries.3 = (f32[384,128]{1,0:T(8,128)S(1)}, f32[384,128]{1,0:T(8,128)S(1)}, f32[64,128]{1,0:T(8,128)S(1)}) custom-call(bf16[128,4096]{1,0:T(8,128)(2,1)S(1)} %get-tuple-element.40.x, bf16[128,4096]{1,0:T(8,128)(2,1)S(1)} %get-tuple-element.37.c.cot, f32[16,4096]{1,0:T(8,128)S(1)} %get-tuple-element.38.rate.refs_4_), custom_call_target="tpu_custom_call" | custom-call | tf_op jit(solution)/shard_map/summaries/pallas_call | solution.py:38
  8.9 3.5 %collective-permute-start.2 = (f32[384,128]{1,0:T(8,128)S(1)}, f32[384,128]{1,0:T(8,128)S(1)}, u32[]{:S(2)}, u32[]{:S(2)}) collective-permute-start(f32[384,128]{1,0:T(8,128)S(1)} %get-tuple-element.47), channel_id=1, source_target_pairs={{0,6},{1,7},{2,4},{3,5},{4,2},{5,3},{6,0},{7,1},{8,14},{9,15},{10,... | collective-permute-start | bytes 589832 | tf_op jit(solution)/shard_map/ppermute | solution.py:538
  12.7 3.0 %summaries.4 = (f32[384,128]{1,0:T(8,128)S(1)}, f32[384,128]{1,0:T(8,128)S(1)}, f32[64,128]{1,0:T(8,128)S(1)}) custom-call(bf16[128,4096]{1,0:T(8,128)(2,1)S(1)} %get-tuple-element.40.x, bf16[128,4096]{1,0:T(8,128)(2,1)S(1)} %get-tuple-element.37.c.cot, f32[16,4096]{1,0:T(8,128)S(1)} %get-tuple-element.38.rate.refs_4_, ...), custom_call_target="tpu_custom_call" | custom-call | tf_op jit(solution)/shard_map/summaries/pallas_call | solution.py:38
  15.7 0.4 collective-permute-start.3
  16.1 1.9 %collective-permute-done.2.one.refs_3_ = f32[384,128]{1,0:T(8,128)S(1)} collective-permute-done((f32[384,128]{1,0:T(8,128)S(1)}, f32[384,128]{1,0:T(8,128)S(1)}, u32[]{:S(2)}, u32[]{:S(2)}) %collective-permute-start.2) | collective-permute-done | bytes 196640 | tf_op jit(solution)/shard_map/ppermute | solution.py:538
  18.1 1.8 %collective-permute-start.6 = (f32[384,128]{1,0:T(8,128)S(1)}, f32[384,128]{1,0:T(8,128)S(1)}, u32[]{:S(2)}, u32[]{:S(2)}) collective-permute-start(f32[384,128]{1,0:T(8,128)S(1)} %get-tuple-element.58), channel_id=1, source_target_pairs={{0,4},{1,5},{2,6},{3,7},{4,0},{5,1},{6,2},{7,3},{8,12},{9,13},{10,... | collective-permute-start | bytes 589832 | tf_op jit(solution)/shard_map/ppermute | solution.py:538
  19.9 1.6 %collective-permute-start.5 = (f32[384,128]{1,0:T(8,128)S(1)}, f32[384,128]{1,0:T(8,128)S(1)}, u32[]{:S(2)}, u32[]{:S(2)}) collective-permute-start(f32[384,128]{1,0:T(8,128)S(1)} %get-tuple-element.57), channel_id=1, source_target_pairs={{0,2},{1,3},{2,0},{3,1},{4,6},{5,7},{6,4},{7,5},{8,10},{9,11},{10,... | collective-permute-start | bytes 589832 | tf_op jit(solution)/shard_map/ppermute | solution.py:538
  21.4 3.0 %summaries.5 = (f32[384,128]{1,0:T(8,128)S(1)}, f32[384,128]{1,0:T(8,128)S(1)}, f32[64,128]{1,0:T(8,128)S(1)}) custom-call(bf16[128,4096]{1,0:T(8,128)(2,1)S(1)} %get-tuple-element.40.x, bf16[128,4096]{1,0:T(8,128)(2,1)S(1)} %get-tuple-element.37.c.cot, f32[16,4096]{1,0:T(8,128)S(1)} %get-tuple-element.38.rate.refs_4_, ...), custom_call_target="tpu_custom_call" | custom-call | tf_op jit(solution)/shard_map/summaries/pallas_call | solution.py:38
  24.8 1.4 %collective-permute-done.5.one.refs_1_ = f32[384,128]{1,0:T(8,128)S(1)} collective-permute-done((f32[384,128]{1,0:T(8,128)S(1)}, f32[384,128]{1,0:T(8,128)S(1)}, u32[]{:S(2)}, u32[]{:S(2)}) %collective-permute-start.5) | collective-permute-done | bytes 196640 | tf_op jit(solution)/shard_map/ppermute | solution.py:538
  26.4 1.5 %collective-permute-start.7 = (f32[128,128]{1,0:T(8,128)S(1)}, f32[128,128]{1,0:T(8,128)S(1)}, u32[]{:S(2)}, u32[]{:S(2)}) collective-permute-start(f32[128,128]{1,0:T(8,128)S(1)} %get-tuple-element.61), channel_id=1, source_target_pairs={{0,2},{1,3},{2,0},{3,1},{4,6},{5,7},{6,4},{7,5},{8,10},{9,11},{10,... | collective-permute-start | bytes 196616 | tf_op jit(solution)/shard_map/ppermute | solution.py:538
  28.0 1.6 %collective-permute-start.8 = (f32[64,128]{1,0:T(8,128)S(1)}, f32[64,128]{1,0:T(8,128)S(1)}, u32[]{:S(2)}, u32[]{:S(2)}) collective-permute-start(f32[64,128]{1,0:T(8,128)S(1)} %get-tuple-element.63), channel_id=1, source_target_pairs={{0,8},{8,0},{16,24},{24,16},{1,9},{9,1},{17,25},{25,17},{2,10},{10... | collective-permute-start | bytes 98312 | tf_op jit(solution)/shard_map/ppermute | solution.py:542
  29.6 2.3 %collective-permute-done.8.got = f32[64,128]{1,0:T(8,128)S(1)} collective-permute-done((f32[64,128]{1,0:T(8,128)S(1)}, f32[64,128]{1,0:T(8,128)S(1)}, u32[]{:S(2)}, u32[]{:S(2)}) %collective-permute-start.8) | collective-permute-done | bytes 32800 | tf_op jit(solution)/shard_map/ppermute | solution.py:542
  31.9 0.6 %collective-permute-start.9 = (f32[128,128]{1,0:T(8,128)S(1)}, f32[128,128]{1,0:T(8,128)S(1)}, u32[]{:S(2)}, u32[]{:S(2)}) collective-permute-start(f32[128,128]{1,0:T(8,128)S(1)} %stacked.7), channel_id=1, source_target_pairs={{0,4},{1,5},{2,6},{3,7},{4,0},{5,1},{6,2},{7,3},{8,12},{9,13},{10,... | collective-permute-start | bytes 196616 | tf_op jit(solution)/shard_map/ppermute | solution.py:538
  32.5 2.6 %collective-permute-start.10 = (f32[32,128]{1,0:T(8,128)S(1)}, f32[32,128]{1,0:T(8,128)S(1)}, u32[]{:S(2)}, u32[]{:S(2)}) collective-permute-start(f32[32,128]{1,0:T(8,128)S(1)} %get-tuple-element.64.refs_0_), channel_id=1, source_target_pairs={{0,16},{8,24},{16,0},{24,8},{1,17},{9,25},{17,1},{25,9},{2,18},{10... | collective-permute-start | bytes 49160 | tf_op jit(solution)/shard_map/ppermute | solution.py:542
  35.1 2.0 %collective-permute-done.10 = f32[32,128]{1,0:T(8,128)S(1)} collective-permute-done((f32[32,128]{1,0:T(8,128)S(1)}, f32[32,128]{1,0:T(8,128)S(1)}, u32[]{:S(2)}, u32[]{:S(2)}) %collective-permute-start.10) | collective-permute-done | bytes 16416 | tf_op jit(solution)/shard_map/ppermute | solution.py:542
  37.3 0.5 %collective-permute-start.12 = (f32[32,128]{1,0:T(8,128)S(1)}, f32[32,128]{1,0:T(8,128)S(1)}, u32[]{:S(2)}, u32[]{:S(2)}) collective-permute-start(f32[32,128]{1,0:T(8,128)S(1)} %add.3.refs_7_.one), channel_id=1, source_target_pairs={{0,1},{1,0},{2,3},{3,2},{4,5},{5,4},{6,7},{7,6},{8,9},{9,8},{10,11... | collective-permute-start | bytes 49160 | tf_op jit(solution)/shard_map/ppermute | solution.py:538
  37.8 0.9 %collective-permute-done.12.two = f32[32,128]{1,0:T(8,128)S(1)} collective-permute-done((f32[32,128]{1,0:T(8,128)S(1)}, f32[32,128]{1,0:T(8,128)S(1)}, u32[]{:S(2)}, u32[]{:S(2)}) %collective-permute-start.12) | collective-permute-done | bytes 16416 | tf_op jit(solution)/shard_map/ppermute | solution.py:538
  38.6 0.5 %collective-permute-start.13 = (f32[64,128]{1,0:T(8,128)S(1)}, f32[64,128]{1,0:T(8,128)S(1)}, u32[]{:S(2)}, u32[]{:S(2)}) collective-permute-start(f32[64,128]{1,0:T(8,128)S(1)} %stacked.8.one), channel_id=1, source_target_pairs={{0,2},{1,3},{2,0},{3,1},{4,6},{5,7},{6,4},{7,5},{8,10},{9,11},{10,... | collective-permute-start | bytes 98312 | tf_op jit(solution)/shard_map/ppermute | solution.py:538
  39.2 3.6 %input_gradients.2.refs_2_.refs_0_ = bf16[128,4096]{1,0:T(8,128)(2,1)} custom-call(bf16[128,4096]{1,0:T(8,128)(2,1)S(1)} %get-tuple-element.37.c.cot, f32[16,4096]{1,0:T(8,128)S(1)} %get-tuple-element.38.rate.refs_4_, f32[16,4096]{1,0:T(8,128)S(1)} %get-tuple-element.39.refs_5_.res, f32[256,128]{1,0:T(8,128)S(1)} %get-tuple-element.67.refs_0_, ...), custom_call_target="tpu_custom_call" | custom-call | tf_op jit(solution)/shard_map/input_gradients/pallas_call | solution.py:490
  42.8 1.6 %collective-permute-start.14 = (f32[128,128]{1,0:T(8,128)S(1)}, f32[128,128]{1,0:T(8,128)S(1)}, u32[]{:S(2)}, u32[]{:S(2)}) collective-permute-start(f32[128,128]{1,0:T(8,128)S(1)} %stacked.9.refs_0_), channel_id=1, source_target_pairs={{0,4},{1,5},{2,6},{3,7},{4,0},{5,1},{6,2},{7,3},{8,12},{9,13},{10,... | collective-permute-start | bytes 196616 | tf_op jit(solution)/shard_map/ppermute | solution.py:538
  44.4 3.6 %input_gradients.3.refs_2_ = bf16[128,4096]{1,0:T(8,128)(2,1)} custom-call(bf16[128,4096]{1,0:T(8,128)(2,1)S(1)} %get-tuple-element.37.c.cot, f32[16,4096]{1,0:T(8,128)S(1)} %get-tuple-element.38.rate.refs_4_, f32[16,4096]{1,0:T(8,128)S(1)} %get-tuple-element.39.refs_5_.res, ...), custom_call_target="tpu_custom_call", output_to_operand_aliasing={{}: (5, {})} | custom-call | tf_op jit(solution)/shard_map/input_gradients/pallas_call | solution.py:490
  48.0 0.7 %placed.1 = (f32[16,1024]{1,0:T(8,128)}, f32[16,1024]{1,0:T(8,128)}) custom-call(f32[128,128]{1,0:T(8,128)S(1)} %stacked.9.refs_0_, f32[128,128]{1,0:T(8,128)S(1)} %collective-permute-done.14.refs_1_, bf16[128,4096]{1,0:T(8,128)(2,1)} %input_gradients.3.refs_2_), custom_call_target="tpu_custom_call" | custom-call | tf_op jit(solution)/shard_map/placed/pallas_call | solution.py:524
  (26 shorter events, 1.1 us)
Async XLA Ops:
  5.3 3.6 %collective-permute-start.1 = (f32[384,128]{1,0:T(8,128)S(1)}, f32[384,128]{1,0:T(8,128)S(1)}, u32[]{:S(2)}, u32[]{:S(2)}) collective-permute-start(f32[384,128]{1,0:T(8,128)S(1)} %get-tuple-element.45), channel_id=1, source_target_pairs={{0,1},{1,0},{2,3},{3,2},{4,5},{5,4},{6,7},{7,6},{8,9},{9,8},{10,11... | collective-permute-start | bytes 589832 | tf_op jit(solution)/shard_map/ppermute | solution.py:538
  8.9 9.1 %collective-permute-start.2 = (f32[384,128]{1,0:T(8,128)S(1)}, f32[384,128]{1,0:T(8,128)S(1)}, u32[]{:S(2)}, u32[]{:S(2)}) collective-permute-start(f32[384,128]{1,0:T(8,128)S(1)} %get-tuple-element.47), channel_id=1, source_target_pairs={{0,6},{1,7},{2,4},{3,5},{4,2},{5,3},{6,0},{7,1},{8,14},{9,15},{10,... | collective-permute-start | bytes 589832 | tf_op jit(solution)/shard_map/ppermute | solution.py:538
  12.4 5.6 %collective-permute-start = (f32[384,128]{1,0:T(8,128)S(1)}, f32[384,128]{1,0:T(8,128)S(1)}, u32[]{:S(2)}, u32[]{:S(2)}) collective-permute-start(f32[384,128]{1,0:T(8,128)S(1)} %get-tuple-element.42), channel_id=1, source_target_pairs={{0,1},{1,0},{2,3},{3,2},{4,5},{5,4},{6,7},{7,6},{8,9},{9,8},{10,11... | collective-permute-start | bytes 589832 | tf_op jit(solution)/shard_map/ppermute | solution.py:538
  15.7 4.1 %collective-permute-start.3 = (f32[384,128]{1,0:T(8,128)S(1)}, f32[384,128]{1,0:T(8,128)S(1)}, u32[]{:S(2)}, u32[]{:S(2)}) collective-permute-start(f32[384,128]{1,0:T(8,128)S(1)} %get-tuple-element.52), channel_id=1, source_target_pairs={{0,1},{1,0},{2,3},{3,2},{4,5},{5,4},{6,7},{7,6},{8,9},{9,8},{10,11... | collective-permute-start | bytes 589832 | tf_op jit(solution)/shard_map/ppermute | solution.py:538
  18.1 6.8 %collective-permute-start.6 = (f32[384,128]{1,0:T(8,128)S(1)}, f32[384,128]{1,0:T(8,128)S(1)}, u32[]{:S(2)}, u32[]{:S(2)}) collective-permute-start(f32[384,128]{1,0:T(8,128)S(1)} %get-tuple-element.58), channel_id=1, source_target_pairs={{0,4},{1,5},{2,6},{3,7},{4,0},{5,1},{6,2},{7,3},{8,12},{9,13},{10,... | collective-permute-start | bytes 589832 | tf_op jit(solution)/shard_map/ppermute | solution.py:538
  19.9 6.3 %collective-permute-start.5 = (f32[384,128]{1,0:T(8,128)S(1)}, f32[384,128]{1,0:T(8,128)S(1)}, u32[]{:S(2)}, u32[]{:S(2)}) collective-permute-start(f32[384,128]{1,0:T(8,128)S(1)} %get-tuple-element.57), channel_id=1, source_target_pairs={{0,2},{1,3},{2,0},{3,1},{4,6},{5,7},{6,4},{7,5},{8,10},{9,11},{10,... | collective-permute-start | bytes 589832 | tf_op jit(solution)/shard_map/ppermute | solution.py:538
  24.5 1.7 %collective-permute-start.4 = (f32[384,128]{1,0:T(8,128)S(1)}, f32[384,128]{1,0:T(8,128)S(1)}, u32[]{:S(2)}, u32[]{:S(2)}) collective-permute-start(f32[384,128]{1,0:T(8,128)S(1)} %get-tuple-element.55), channel_id=1, source_target_pairs={{0,1},{1,0},{2,3},{3,2},{4,5},{5,4},{6,7},{7,6},{8,9},{9,8},{10,11... | collective-permute-start | bytes 589832 | tf_op jit(solution)/shard_map/ppermute | solution.py:538
  26.4 5.5 %collective-permute-start.7 = (f32[128,128]{1,0:T(8,128)S(1)}, f32[128,128]{1,0:T(8,128)S(1)}, u32[]{:S(2)}, u32[]{:S(2)}) collective-permute-start(f32[128,128]{1,0:T(8,128)S(1)} %get-tuple-element.61), channel_id=1, source_target_pairs={{0,2},{1,3},{2,0},{3,1},{4,6},{5,7},{6,4},{7,5},{8,10},{9,11},{10,... | collective-permute-start | bytes 196616 | tf_op jit(solution)/shard_map/ppermute | solution.py:538
  28.0 3.9 %collective-permute-start.8 = (f32[64,128]{1,0:T(8,128)S(1)}, f32[64,128]{1,0:T(8,128)S(1)}, u32[]{:S(2)}, u32[]{:S(2)}) collective-permute-start(f32[64,128]{1,0:T(8,128)S(1)} %get-tuple-element.63), channel_id=1, source_target_pairs={{0,8},{8,0},{16,24},{24,16},{1,9},{9,1},{17,25},{25,17},{2,10},{10... | collective-permute-start | bytes 98312 | tf_op jit(solution)/shard_map/ppermute | solution.py:542
  31.9 5.2 %collective-permute-start.9 = (f32[128,128]{1,0:T(8,128)S(1)}, f32[128,128]{1,0:T(8,128)S(1)}, u32[]{:S(2)}, u32[]{:S(2)}) collective-permute-start(f32[128,128]{1,0:T(8,128)S(1)} %stacked.7), channel_id=1, source_target_pairs={{0,4},{1,5},{2,6},{3,7},{4,0},{5,1},{6,2},{7,3},{8,12},{9,13},{10,... | collective-permute-start | bytes 196616 | tf_op jit(solution)/shard_map/ppermute | solution.py:538
  32.5 4.6 %collective-permute-start.10 = (f32[32,128]{1,0:T(8,128)S(1)}, f32[32,128]{1,0:T(8,128)S(1)}, u32[]{:S(2)}, u32[]{:S(2)}) collective-permute-start(f32[32,128]{1,0:T(8,128)S(1)} %get-tuple-element.64.refs_0_), channel_id=1, source_target_pairs={{0,16},{8,24},{16,0},{24,8},{1,17},{9,25},{17,1},{25,9},{2,18},{10... | collective-permute-start | bytes 49160 | tf_op jit(solution)/shard_map/ppermute | solution.py:542
  37.2 2.0 %collective-permute-start.11 = (f32[256,128]{1,0:T(8,128)S(1)}, f32[256,128]{1,0:T(8,128)S(1)}, u32[]{:S(2)}, u32[]{:S(2)}) collective-permute-start(f32[256,128]{1,0:T(8,128)S(1)} %get-tuple-element.68), channel_id=1, source_target_pairs={{0,1},{1,0},{2,3},{3,2},{4,5},{5,4},{6,7},{7,6},{8,9},{9,8},{10,11... | collective-permute-start | bytes 393224 | tf_op jit(solution)/shard_map/ppermute | solution.py:538
  37.3 1.4 %collective-permute-start.12 = (f32[32,128]{1,0:T(8,128)S(1)}, f32[32,128]{1,0:T(8,128)S(1)}, u32[]{:S(2)}, u32[]{:S(2)}) collective-permute-start(f32[32,128]{1,0:T(8,128)S(1)} %add.3.refs_7_.one), channel_id=1, source_target_pairs={{0,1},{1,0},{2,3},{3,2},{4,5},{5,4},{6,7},{7,6},{8,9},{9,8},{10,11... | collective-permute-start | bytes 49160 | tf_op jit(solution)/shard_map/ppermute | solution.py:538
  38.6 4.2 %collective-permute-start.13 = (f32[64,128]{1,0:T(8,128)S(1)}, f32[64,128]{1,0:T(8,128)S(1)}, u32[]{:S(2)}, u32[]{:S(2)}) collective-permute-start(f32[64,128]{1,0:T(8,128)S(1)} %stacked.8.one), channel_id=1, source_target_pairs={{0,2},{1,3},{2,0},{3,1},{4,6},{5,7},{6,4},{7,5},{8,10},{9,11},{10,... | collective-permute-start | bytes 98312 | tf_op jit(solution)/shard_map/ppermute | solution.py:538
  42.8 5.2 %collective-permute-start.14 = (f32[128,128]{1,0:T(8,128)S(1)}, f32[128,128]{1,0:T(8,128)S(1)}, u32[]{:S(2)}, u32[]{:S(2)}) collective-permute-start(f32[128,128]{1,0:T(8,128)S(1)} %stacked.9.refs_0_), channel_id=1, source_target_pairs={{0,4},{1,5},{2,6},{3,7},{4,0},{5,1},{6,2},{7,3},{8,12},{9,13},{10,... | collective-permute-start | bytes 196616 | tf_op jit(solution)/shard_map/ppermute | solution.py:538

commit v4 on v3

--- a/solution.py
+++ b/solution.py
@@ -12,7 +12,7 @@
 SUBS = 8
 SPAN = 8
 PARTS = 6
-ORDER = (3, 2, 1, 0)
+ORDER = (3, 1, 2, 0)
 END, START, DEND, DSTART, RES, POLE = range(PARTS)
 f32 = jnp.float32
 
@@ -32,6 +32,11 @@
 
 def room(megabytes):
     return pltpu.CompilerParams(vmem_limit_bytes=megabytes << 20)
+
+
+def bits():
+    chip, core, _ = position()
+    return core, chip % 2, chip // 2
 
 
 def local_call(kernel, name, shapes, operands, scratch=(), megabytes=2, after=()):
@@ -247,7 +252,7 @@
     )
 
 
-def pair_kernel(own, other, rates, *refs, rows, modes):
+def pair_kernel(own, other, rates, *refs, level, rows, modes):
     send, hold = refs[-2:]
     size = modes * 4
 
@@ -263,66 +268,43 @@
         hold[pl.ds(0, size), :] = second[START]
         hold[pl.ds(size, size), :] = power
 
-    core = position()[1]
-
-    @pl.when(core == 0)
+    later = bits()[level]
+
+    @pl.when(later == 0)
     def _():
         body(own, other)
 
-    @pl.when(core != 0)
+    @pl.when(later != 0)
     def _():
         body(other, own)
 
 
-def paired(own, other, rates, rows, modes, after):
+def paired(own, other, rates, level, rows, modes, after=()):
     return local_call(
-        functools.partial(pair_kernel, rows=rows, modes=modes),
+        functools.partial(pair_kernel, level=level, rows=rows, modes=modes),
         "paired",
         [(PARTS * modes * 4, LANES), (2 * modes * 4, LANES)],
         [own, other, rates, *after],
     )
 
 
-def chain_kernel(*refs, rows, modes, scale):
-    pieces, (rate, residues) = refs[:4], refs[4:6]
-    back_keep, back_send, term_keep, term_send = refs[6:10]
-    ordered, adjoints, small, owned = refs[10:]
+def close_kernel(own, other, rates, residues, term_keep, term_send, small, owned, *, modes, scale):
     chip, core, depth = position()
     size = modes * 4
-    for j in range(4):
-        ordered[chip ^ j] = pieces[j][...]
     for q in range(4):
         lanes = pl.ds(pl.multiple_of((8 * q + 2 * chip + core) * LANES, LANES), LANES)
-        small[0, pl.ds(q, modes, stride=4), :] = rate[:, lanes]
-        small[1, pl.ds(q, modes, stride=4), :] = residues[:, lanes]
-    r = small[0]
-    pole = jnp.exp(-r)
-    power = jnp.exp(-r * rows)
-    slope = jnp.exp(-r * (rows - 1)) * float(rows)
-    read = lambda c, a: ordered[c, pl.ds(a * size, size), :]
-    now, dnow = read(0, END), read(0, DEND)
-    sum_res, sum_pole = read(0, RES), read(0, POLE)
-    for c in range(1, 4):
-        start, dstart = read(c, START), read(c, DSTART)
-        cross = now * start
-        sum_res = sum_res + read(c, RES) + pole * cross
-        sum_pole = sum_pole + read(c, POLE) + cross + pole * (dnow * start + now * dstart)
-        if c < 3:
-            now, dnow = (
-                power * now + read(c, END),
-                slope * now + power * dnow + read(c, DEND),
-            )
-    back = jnp.zeros((size, LANES), f32)
-    adjoints[3] = back
-    for c in range(2, -1, -1):
-        back = read(c + 1, START) + power * back
-        adjoints[c] = back
-    for place in range(2):
-        rows_of = pl.ds(place * size, size)
-        back_keep[rows_of, :] = adjoints[chip ^ (2 * place)]
-        back_send[rows_of, :] = adjoints[chip ^ (2 * place + 1)]
+        small[pl.ds(q, modes, stride=4), :] = residues[:, lanes]
+    pole = jnp.exp(-rates[...])
+    later = chip // 2 != 0
+    read = lambda ref, a: ref[pl.ds(a * size, size), :]
+    pick = lambda a, one, two: jnp.where(later, read(two, a), read(one, a))
+    now, dnow = pick(END, own, other), pick(DEND, own, other)
+    start, dstart = pick(START, other, own), pick(DSTART, other, own)
+    cross = now * start
+    sum_res = read(own, RES) + read(other, RES) + pole * cross
+    sum_pole = read(own, POLE) + read(other, POLE) + cross + pole * (dnow * start + now * dstart)
     owned[pl.ds(0, size), :] = sum_res * scale
-    owned[pl.ds(size, size), :] = sum_pole * (-pole * small[1]) * scale
+    owned[pl.ds(size, size), :] = sum_pole * (-pole * small[...]) * scale
     for place in range(2):
         for ref, q in ((term_keep, 2 * place + depth % 2), (term_send, 2 * place + 1 - depth % 2)):
             for a in range(2):
@@ -331,19 +313,46 @@
                 ]
 
 
-def chained(pieces, rate, residues, rows, scale):
-    modes = rate.shape[0]
+def closed(own, other, rates, residues, scale):
+    modes = residues.shape[0]
     size = modes * 4
     return local_call(
-        functools.partial(chain_kernel, rows=rows, modes=modes, scale=scale),
-        "chained",
-        [(2 * size, LANES)] * 2 + [(4 * modes, LANES)] * 2,
-        [*pieces, rate, residues],
-        [(4, PARTS * size, LANES), (4, size, LANES), (2, size, LANES), (2 * size, LANES)],
-    )
-
-
-def halve_kernel(kept, got, keep, send):
+        functools.partial(close_kernel, modes=modes, scale=scale),
+        "closed",
+        [(4 * modes, LANES)] * 2,
+        [own, other, rates, residues],
+        [(size, LANES), (2 * size, LANES)],
+    )
+
+
+def hand_kernel(other, beside, hold_own, hold_side, *refs, modes):
+    keep, send = refs[-2:]
+    _, right, later = bits()
+    size = modes * 4
+    entering = (other[pl.ds(START * size, size), :], beside[...])
+    for place, hold in enumerate((hold_own, hold_side)):
+        rows_of = pl.ds(place * size, size)
+        late = jnp.where(later == 0, entering[place], 0.0)
+        early = hold[:size, :] + hold[size:, :] * late
+        keep[rows_of, :] = jnp.where(right == 0, early, late)
+        send[rows_of, :] = jnp.where(right == 0, late, early)
+
+
+def handed(other, beside, hold_own, hold_side, modes, near):
+    return local_call(
+        functools.partial(hand_kernel, modes=modes),
+        "handed",
+        [(2 * modes * 4, LANES)] * 2,
+        [other, beside, hold_own, hold_side, *near],
+    )
+
+
+def add_kernel(one, two, *refs):
+    refs[-1][...] = one[...] + two[...]
+
+
+def halve_kernel(kept, got, *refs):
+    keep, send = refs[-2:]
     upper = position()[2] // 2
     half = kept.shape[0] // 2
     for ref, place in ((keep, upper), (send, 1 - upper)):
@@ -364,10 +373,10 @@
 
 
 def entry_kernel(*refs, modes):
-    kept, near, far = refs[:3]
-    holds, (mine, theirs) = refs[3:7], refs[-2:]
+    kept, near = refs[:2]
+    holds, (mine, theirs) = refs[2:6], refs[-2:]
     size = modes * 4
-    backs = [kept[:size, :], near[:size, :], far[:size, :], far[size:, :]]
+    backs = [kept[:size, :], near[:size, :], kept[size:, :], near[size:, :]]
 
     def body(late, early):
         for j in range(4):
@@ -386,46 +395,35 @@
         body(mine, theirs)
 
 
-def entries(backs, holds, modes, after):
+def entries(kept, near, holds, modes, after):
     return local_call(
         functools.partial(entry_kernel, modes=modes),
         "entries",
         [(4 * modes * 4, LANES)] * 2,
-        [*backs, *holds, *after],
-    )
-
-
-def input_kernel(cot, rate, res, *refs, blocks, rows, modes, together):
-    given, (out, cs, ys, ps, rs, ads, sent, done) = refs[:-8], refs[-8:]
-    given = [ref for ref in given if ref.dtype == f32]
-    chip, half, _ = position() if len(given) == 2 else (None,) * 3
+        [kept, near, *holds, *after],
+    )
+
+
+def input_kernel(*refs, block, last, given, lead, rows, modes, together):
+    cot, rate, res = refs[:3]
+    entry, lead_ref = refs[3 : 3 + given], refs[3 + given : 4 + given]
+    *outs, cs, ys, ps, rs, ads, done = refs[-(6 + (lead or last) + 1) :]
     width = SUBS * LANES
-    first, count = blocks
-
-    def copy(q):
-        lanes = pl.ds(pl.multiple_of((first + q) * width, width), width)
-        return pltpu.make_async_copy(sent.at[q], out.at[:, lanes], done.at[q])
-
-    def one_block(q, carry):
-        block_of_inputs(
-            first + q,
-            cot,
-            rate,
-            res,
-            given,
-            (chip, half),
-            sent.at[q],
-            (cs, ys, ps, rs, ads),
-            rows,
-            modes,
-            together,
-        )
-        copy(q).start()
-        return carry
-
-    lax.fori_loop(0, count, one_block, 0)
-    for q in range(count):
-        copy(q).wait()
+    copies = []
+    if lead:
+        lanes = pl.ds((block - 1) * width, width)
+        copies.append(pltpu.make_async_copy(lead_ref[0], outs[0].at[:, lanes], done.at[0]))
+        copies[0].start()
+    place = position()[:2] if given == 2 else None
+    scratch = (cs, ys, ps, rs, ads)
+    sent = outs[-1]
+    block_of_inputs(block, cot, rate, res, entry, place, sent, scratch, rows, modes, together)
+    if last:
+        lanes = pl.ds(block * width, width)
+        copies.append(pltpu.make_async_copy(sent, outs[0].at[:, lanes], done.at[1]))
+        copies[-1].start()
+    for copy in copies:
+        copy.wait()
 
 
 def block_of_inputs(q, cot, rate, res, given, place, sent, scratch, rows, modes, together):
@@ -433,7 +431,7 @@
     size = modes * 4
 
     def tile(i):
-        return pl.ds(pl.multiple_of((q * SUBS + i) * LANES, LANES), LANES)
+        return pl.ds((q * SUBS + i) * LANES, LANES)
 
     for i in range(SUBS):
         lanes = tile(i)
@@ -475,34 +473,50 @@
     return pltpu.with_memory_space_constraint(value, pltpu.HBM)
 
 
-def input_gradients(cotangent, rate, residues, given, blocks, onto=None):
+def input_gradients(cotangent, rate, residues, given, block, lead=None, onto=None, last=False):
     rows, channels = cotangent.shape
     modes = rate.shape[0]
     width = SUBS * LANES
     scratch = lambda height: pltpu.VMEM((height * SUBS, LANES), f32)
     operands = [here(item) for item in (cotangent, rate, residues, *given)]
-    specs = [vmem() for _ in operands]
+    shapes, specs = [], []
+    if lead is not None:
+        operands.append(here(lead))
+    in_specs = [vmem() for _ in operands]
     aliases = {}
+    if lead is not None or last:
+        shapes.append(jax.ShapeDtypeStruct((rows, channels), cotangent.dtype))
+        specs.append(far_away())
     if onto is not None:
         aliases = {len(operands): 0}
         operands.append(outside(onto))
-        specs.append(far_away())
+        in_specs.append(far_away())
+    shapes.append(pltpu.VMEM((rows, width), cotangent.dtype))
+    specs.append(vmem())
     return pl.pallas_call(
-        functools.partial(input_kernel, blocks=blocks, rows=rows, modes=modes, together=16),
-        in_specs=specs,
-        out_specs=far_away(),
-        out_shape=jax.ShapeDtypeStruct((rows, channels), cotangent.dtype),
+        functools.partial(
+            input_kernel,
+            block=block,
+            last=last,
+            given=len(given),
+            lead=lead is not None,
+            rows=rows,
+            modes=modes,
+            together=16,
+        ),
+        in_specs=in_specs,
+        out_specs=specs,
+        out_shape=shapes,
         scratch_shapes=[
             scratch(rows),
             scratch(rows),
             scratch(modes),
             scratch(modes),
             scratch(modes),
-            pltpu.VMEM((blocks[1], rows, width), cotangent.dtype),
-            pltpu.SemaphoreType.DMA((blocks[1],)),
+            pltpu.SemaphoreType.DMA((2,)),
         ],
         input_output_aliases=aliases,
-        compiler_params=room(5),
+        compiler_params=room(4),
         name="input_gradients",
     )(*operands)
 
@@ -548,44 +562,48 @@
     theirs, ours, rates, x, c, rate, residues = first_summaries(
         x, c, rate, residues, chip_tiles(ORDER[0])
     )
-    sends, holds, got = {}, {}, {}
-    waiting = (ORDER[0], ours, crossed(theirs, 1), rates)
-
-    def pair(waiting, after=()):
-        away, ours, others, rates = waiting
-        sends[away], holds[away] = paired(ours, others, rates, rows, modes, after)
-        if away:
-            got[away] = crossed(sends[away], 2 * away)
-
-    for away in ORDER[1:]:
-        if away == 0:
-            pair(waiting, (landed,))
-        after = {2: (), 1: (holds.get(3),), 0: (holds.get(2), holds.get(1))}[away]
-        theirs, ours, next_rates = summaries(x, c, rate, chip_tiles(away), after)
-        if away == 1:
-            landed = stacked(got[3], next_rates, 8)
-            pair(waiting, (landed,))
-        elif away:
-            pair(waiting, (next_rates,))
-        waiting = (away, ours, crossed(theirs, 1), next_rates)
-    pair(waiting, (stacked(got[1], got[2], 8),))
+    holds = {}
+
+    def cores(away, ours, others, rates, after=()):
+        sums, holds[away] = paired(ours, others, rates, 0, rows, modes, after)
+        return sums
+
+    def more(away, after=()):
+        theirs, ours, rates = summaries(x, c, rate, chip_tiles(away), after)
+        return crossed(theirs, 1), ours, rates
+
+    theirs3 = crossed(theirs, 1)
+    theirs1, ours1, rates1 = more(1)
+    got2 = crossed(cores(3, ours, theirs3, rates, (rates1,)), 2)
+    theirs2, ours2, rates2 = more(2, (holds[3],))
+    got0 = crossed(cores(1, ours1, theirs1, rates1, (rates2,)), 2)
+    landed = stacked(got2, holds[1], 8)
+    row2 = cores(2, ours2, theirs2, rates2, (landed,))
+    row2, hold_side = paired(row2, got2, rates2, 1, 2 * rows, modes)
+    other = crossed(row2, 4)
+    theirs0, ours0, rates0 = more(0, (hold_side, holds[1]))
+    landed = stacked(stacked(other, rates0, 8), got0, 8)
+    row0 = cores(0, ours0, theirs0, rates0, (landed,))
+    row0, hold_own = paired(row0, got0, rates0, 1, 2 * rows, modes)
+    beside = crossed(row0[START * 4 * modes : (START + 1) * 4 * modes], 4)
     scale = 1.0 / math.sqrt(4 * rows * 8)
-    back_keep, back_send, term_keep, term_send = chained(
-        [sends[0], got[1], got[2], got[3]], rate, residues, 2 * rows, scale
-    )
+    term_keep, term_send = closed(row0, other, rates0, residues, scale)
     half = (2 * modes, LANES)
     keep, send = local_call(
         halve_kernel, "halved", [half, half], [term_keep, shifted(term_send, 1)]
     )
-    near = crossed(back_send, 2)
-    total = keep + shifted(send, 2)
-    far = crossed(stacked(back_keep, near, 4 * modes, (), (send,)), 4)
-    mine, others = entries([back_keep, near, far], [holds[j] for j in range(4)], modes, (total,))
+    back_keep, back_send = handed(other, beside, hold_own, hold_side, modes, (send,))
+    back_near = crossed(back_send, 2)
+    (total,) = local_call(add_kernel, "added", [half], [keep, shifted(send, 2)])
+    mine, others = entries(back_keep, back_near, [holds[j] for j in range(4)], modes, (total,))
     entry = (mine, crossed(others, 1))
     both = stacked(total, crossed(total, 1), 2 * modes)
-    grad_inputs = input_gradients(c, rate, residues, entry, (0, 2))
-    four = stacked(both, crossed(both, 2), 4 * modes, (grad_inputs,))
-    grad_inputs = input_gradients(c, rate, residues, entry, (2, 2), grad_inputs)
+    gradients = functools.partial(input_gradients, c, rate, residues, entry)
+    (part0,) = gradients(0)
+    grad_inputs, part1 = gradients(1, part0)
+    four = stacked(both, crossed(both, 2), 4 * modes, (), (part1,))
+    grad_inputs, part2 = gradients(2, part1, grad_inputs)
+    grad_inputs, _ = gradients(3, part2, grad_inputs, True)
     grad_residues, grad_rate = placed([four, crossed(four, 4)], modes, grad_inputs)
     return (grad_inputs[None], grad_residues, grad_rate)
 
@@ -593,7 +611,7 @@
 def any_mesh(inputs, cotangent, rate, residues):
     x, c = inputs[0], cotangent[0]
     rows, channels, modes = x.shape[0], x.shape[1], rate.shape[0]
-    count, mine = lax.axis_size("context"), lax.axis_index("context")
+    slab_count, mine = lax.axis_size("context"), lax.axis_index("context")
     blocks = [
         summaries(x, c, rate, next_tiles(first))[:2] for first in range(0, channels // LANES, SUBS)
     ]
@@ -604,18 +622,24 @@
     pole, power = jnp.exp(-rate), jnp.exp(-rate * rows)
     slope = jnp.exp(-rate * (rows - 1)) * rows
     total = tuple(slabs[0])
-    for place in range(1, count):
+    for place in range(1, slab_count):
         total = joined(total, slabs[place], pole, power, slope)
     zero = jnp.zeros_like(pole)
 
     def behind(index, entry):
-        place = count - 1 - index
+        place = slab_count - 1 - index
         return jnp.where(place > mine, slabs[place, START] + power * entry, entry)
 
-    entry = lax.fori_loop(0, count, behind, zero)
-    blocks = (0, channels // (SUBS * LANES))
-    grad_inputs = input_gradients(c, rate, residues, [entry], blocks)
-    scale = 1.0 / math.sqrt(lax.axis_size("dp") * rows * count)
+    entry = lax.fori_loop(0, slab_count, behind, zero)
+    count = channels // (SUBS * LANES)
+    lead = grad_inputs = None
+    for block in range(count):
+        last = block == count - 1
+        *grad_inputs, lead = input_gradients(
+            c, rate, residues, [entry], block, lead, grad_inputs, last
+        )
+        grad_inputs = grad_inputs[0] if grad_inputs else None
+    scale = 1.0 / math.sqrt(lax.axis_size("dp") * rows * slab_count)
     terms = jnp.stack([total[RES], total[POLE] * (-pole * residues)]) * scale
     owned = lax.psum_scatter(terms, "dp", scatter_dimension=2, tiled=True)
     return (grad_inputs[None], owned[0], owned[1])

time: 48.9 us -> 47.9 us (0.980)
  starting transfers between devices: 17 us -> 15 us
  waiting for transfers between devices: 8.83 us -> 9.87 us
    ppermute x13, starting transfers between devices: 12.9 us -> 10.8 us  [crossed(): return lax.ppermute(value, 'context', [(i, i ^ distance) for i in range(8)])]
    ppermute x13, waiting for transfers between devices: 4.45 us -> 5.94 us  [crossed(): return lax.ppermute(value, 'context', [(i, i ^ distance) for i in range(8)])]
    pallas_call x2 -> x4, Pallas kernels: 7.23 us -> 7.14 us  [input_gradients(): pl.pallas_call(functools.partial(input_kernel, block=block, last=last, gi...]
    pallas_call x15 -> x19, Pallas kernels: 9.53 us -> 9.57 us  [local_call(): pl.pallas_call(kernel, in_specs=[vmem() for _ in operands] + [far_away()...]
  transfers between devices with their start and end apart: 15 -> 15, of which waited for: 6 -> 8; matrix products, arithmetic and copies ran while one was open for 0% -> 0% of each run, Pallas kernels for 34% -> 34%
where the time goes in v4:
time: 47.9 us; the launch traced here: 47.8 us
  Pallas kernels  22 us (46%)
  starting transfers between devices  15 us (31%)
  waiting for transfers between devices  9.87 us (21%)
  between operations  0.82 us (2%)
    ppermute x13, starting transfers between devices, crossed(): return lax.ppermute(value, 'context', [(i, i ^ distance) for i in range(8)])  10.8 us
    pallas_call x19, Pallas kernels, local_call(): pl.pallas_call(kernel, in_specs=[vmem() for _ in operands] + [far_away()...  9.57 us
    pallas_call x4, Pallas kernels, input_gradients(): pl.pallas_call(functools.partial(input_kernel, block=block, last=last, gi...  7.14 us
    ppermute x13, waiting for transfers between devices, crossed(): return lax.ppermute(value, 'context', [(i, i ^ distance) for i in range(8)])  5.94 us
    pallas_call x1, Pallas kernels, first_summaries(): pl.pallas_call(functools.partial(first_kernel, **static), in_specs=[far_a...  4.62 us
    ppermute x2, starting transfers between devices, shifted(): return lax.ppermute(value, 'dp', [(i, i ^ distance) for i in range(4)])  4.23 us
    ppermute x2, waiting for transfers between devices, shifted(): return lax.ppermute(value, 'dp', [(i, i ^ distance) for i in range(4)])  3.93 us
  transfers between devices with their start and end apart: 15, of which 8 were waited for; matrix products, arithmetic and copies ran while one was open for 0% of the time, Pallas kernels for 34%

profile of v4, /device:TPU:0, one launch (start us, length us, event | category | flops | bytes accessed | tf_op | source)
XLA Modules:
  0.0 47.8 jit_solution(6934514593535788948)
XLA Ops:
  0.6 4.6 %first_summaries.1 = (f32[384,128]{1,0:T(8,128)S(1)}, f32[384,128]{1,0:T(8,128)S(1)}, f32[64,128]{1,0:T(8,128)S(1)}, bf16[128,4096]{1,0:T(8,128)(2,1)S(1)}, bf16...) custom-call(bf16[128,4096]{1,0:T(8,128)(2,1)} %bitcast.4, bf16[128,4096]{1,0:T(8,128)(2,1)} %bitcast.5, ...), custom_call_target="tpu_custom_call" | custom-call | tf_op jit(solution)/shard_map/first_summaries/pallas_call | solution.py:230
  5.3 0.5 %collective-permute-start = (f32[384,128]{1,0:T(8,128)S(1)}, f32[384,128]{1,0:T(8,128)S(1)}, u32[]{:S(2)}, u32[]{:S(2)}) collective-permute-start(f32[384,128]{1,0:T(8,128)S(1)} %get-tuple-element.51), channel_id=1, source_target_pairs={{0,1},{1,0},{2,3},{3,2},{4,5},{5,4},{6,7},{7,6},{8,9},{9,8},{10,11... | collective-permute-start | bytes 589832 | tf_op jit(solution)/shard_map/ppermute | solution.py:552
  5.8 3.0 %summaries.3 = (f32[384,128]{1,0:T(8,128)S(1)}, f32[384,128]{1,0:T(8,128)S(1)}, f32[64,128]{1,0:T(8,128)S(1)}) custom-call(bf16[128,4096]{1,0:T(8,128)(2,1)S(1)} %get-tuple-element.49.x, bf16[128,4096]{1,0:T(8,128)(2,1)S(1)} %get-tuple-element.46.c.refs_0_, f32[16,4096]{1,0:T(8,128)S(1)} %get-tuple-element.47.rate.refs_1_), custom_call_target="tpu_custom_call" | custom-call | tf_op jit(solution)/shard_map/summaries/pallas_call | solution.py:43
  9.0 3.0 %collective-permute-start.2 = (f32[384,128]{1,0:T(8,128)S(1)}, f32[384,128]{1,0:T(8,128)S(1)}, u32[]{:S(2)}, u32[]{:S(2)}) collective-permute-start(f32[384,128]{1,0:T(8,128)S(1)} %get-tuple-element.58), channel_id=1, source_target_pairs={{0,2},{1,3},{2,0},{3,1},{4,6},{5,7},{6,4},{7,5},{8,10},{9,11},{10,... | collective-permute-start | bytes 589832 | tf_op jit(solution)/shard_map/ppermute | solution.py:552
  12.0 3.0 %summaries.4 = (f32[384,128]{1,0:T(8,128)S(1)}, f32[384,128]{1,0:T(8,128)S(1)}, f32[64,128]{1,0:T(8,128)S(1)}) custom-call(bf16[128,4096]{1,0:T(8,128)(2,1)S(1)} %get-tuple-element.49.x, bf16[128,4096]{1,0:T(8,128)(2,1)S(1)} %get-tuple-element.46.c.refs_0_, f32[16,4096]{1,0:T(8,128)S(1)} %get-tuple-element.47.rate.refs_1_, ...), custom_call_target="tpu_custom_call" | custom-call | tf_op jit(solution)/shard_map/summaries/pallas_call | solution.py:43
  15.2 1.9 %collective-permute-done.2.one.other = f32[384,128]{1,0:T(8,128)S(1)} collective-permute-done((f32[384,128]{1,0:T(8,128)S(1)}, f32[384,128]{1,0:T(8,128)S(1)}, u32[]{:S(2)}, u32[]{:S(2)}) %collective-permute-start.2) | collective-permute-done | bytes 196640 | tf_op jit(solution)/shard_map/ppermute | solution.py:552
  17.3 1.8 %collective-permute-start.4 = (f32[384,128]{1,0:T(8,128)S(1)}, f32[384,128]{1,0:T(8,128)S(1)}, u32[]{:S(2)}, u32[]{:S(2)}) collective-permute-start(f32[384,128]{1,0:T(8,128)S(1)} %get-tuple-element.63), channel_id=1, source_target_pairs={{0,4},{1,5},{2,6},{3,7},{4,0},{5,1},{6,2},{7,3},{8,12},{9,13},{10,... | collective-permute-start | bytes 589832 | tf_op jit(solution)/shard_map/ppermute | solution.py:552
  19.1 1.5 %collective-permute-start.6 = (f32[384,128]{1,0:T(8,128)S(1)}, f32[384,128]{1,0:T(8,128)S(1)}, u32[]{:S(2)}, u32[]{:S(2)}) collective-permute-start(f32[384,128]{1,0:T(8,128)S(1)} %get-tuple-element.68), channel_id=1, source_target_pairs={{0,2},{1,3},{2,0},{3,1},{4,6},{5,7},{6,4},{7,5},{8,10},{9,11},{10,... | collective-permute-start | bytes 589832 | tf_op jit(solution)/shard_map/ppermute | solution.py:552
  20.6 3.0 %summaries.5 = (f32[384,128]{1,0:T(8,128)S(1)}, f32[384,128]{1,0:T(8,128)S(1)}, f32[64,128]{1,0:T(8,128)S(1)}) custom-call(bf16[128,4096]{1,0:T(8,128)(2,1)S(1)} %get-tuple-element.49.x, bf16[128,4096]{1,0:T(8,128)(2,1)S(1)} %get-tuple-element.46.c.refs_0_, f32[16,4096]{1,0:T(8,128)S(1)} %get-tuple-element.47.rate.refs_1_, ...), custom_call_target="tpu_custom_call" | custom-call | tf_op jit(solution)/shard_map/summaries/pallas_call | solution.py:43
  23.7 1.2 %collective-permute-done.6.two.other = f32[384,128]{1,0:T(8,128)S(1)} collective-permute-done((f32[384,128]{1,0:T(8,128)S(1)}, f32[384,128]{1,0:T(8,128)S(1)}, u32[]{:S(2)}, u32[]{:S(2)}) %collective-permute-start.6) | collective-permute-done | bytes 196640 | tf_op jit(solution)/shard_map/ppermute | solution.py:552
  25.3 1.6 %collective-permute-start.8 = (f32[64,128]{1,0:T(8,128)S(1)}, f32[64,128]{1,0:T(8,128)S(1)}, u32[]{:S(2)}, u32[]{:S(2)}) collective-permute-start(f32[64,128]{1,0:T(8,128)S(1)} %get-tuple-element.73), channel_id=1, source_target_pairs={{0,8},{8,0},{16,24},{24,16},{1,9},{9,1},{17,25},{25,17},{2,10},{10... | collective-permute-start | bytes 98312 | tf_op jit(solution)/shard_map/ppermute | solution.py:556
  27.0 0.5 %collective-permute-start.7 = (f32[64,128]{1,0:T(8,128)S(1)}, f32[64,128]{1,0:T(8,128)S(1)}, u32[]{:S(2)}, u32[]{:S(2)}) collective-permute-start(f32[64,128]{1,0:T(8,128)S(1)} %slice.3), channel_id=1, source_target_pairs={{0,4},{1,5},{2,6},{3,7},{4,0},{5,1},{6,2},{7,3},{8,12},{9,13},{10,... | collective-permute-start | bytes 98312 | tf_op jit(solution)/shard_map/ppermute | solution.py:552
  27.5 1.8 %collective-permute-done.8.got = f32[64,128]{1,0:T(8,128)S(1)} collective-permute-done((f32[64,128]{1,0:T(8,128)S(1)}, f32[64,128]{1,0:T(8,128)S(1)}, u32[]{:S(2)}, u32[]{:S(2)}) %collective-permute-start.8) | collective-permute-done | bytes 32800 | tf_op jit(solution)/shard_map/ppermute | solution.py:556
  29.3 1.6 %collective-permute-done.7.beside = f32[64,128]{1,0:T(8,128)S(1)} collective-permute-done((f32[64,128]{1,0:T(8,128)S(1)}, f32[64,128]{1,0:T(8,128)S(1)}, u32[]{:S(2)}, u32[]{:S(2)}) %collective-permute-start.7) | collective-permute-done | bytes 32800 | tf_op jit(solution)/shard_map/ppermute | solution.py:552
  30.9 1.2 %collective-permute-start.9 = (f32[128,128]{1,0:T(8,128)S(1)}, f32[128,128]{1,0:T(8,128)S(1)}, u32[]{:S(2)}, u32[]{:S(2)}) collective-permute-start(f32[128,128]{1,0:T(8,128)S(1)} %get-tuple-element.76), channel_id=1, source_target_pairs={{0,2},{1,3},{2,0},{3,1},{4,6},{5,7},{6,4},{7,5},{8,10},{9,11},{10,... | collective-permute-start | bytes 196616 | tf_op jit(solution)/shard_map/ppermute | solution.py:552
  32.1 2.6 %collective-permute-start.10 = (f32[32,128]{1,0:T(8,128)S(1)}, f32[32,128]{1,0:T(8,128)S(1)}, u32[]{:S(2)}, u32[]{:S(2)}) collective-permute-start(f32[32,128]{1,0:T(8,128)S(1)} %get-tuple-element.74.refs_0_), channel_id=1, source_target_pairs={{0,16},{8,24},{16,0},{24,8},{1,17},{9,25},{17,1},{25,9},{2,18},{10... | collective-permute-start | bytes 49160 | tf_op jit(solution)/shard_map/ppermute | solution.py:556
  34.7 2.1 %collective-permute-done.10.two = f32[32,128]{1,0:T(8,128)S(1)} collective-permute-done((f32[32,128]{1,0:T(8,128)S(1)}, f32[32,128]{1,0:T(8,128)S(1)}, u32[]{:S(2)}, u32[]{:S(2)}) %collective-permute-start.10) | collective-permute-done | bytes 16416 | tf_op jit(solution)/shard_map/ppermute | solution.py:556
  37.5 0.9 %collective-permute-done.12.two = f32[32,128]{1,0:T(8,128)S(1)} collective-permute-done((f32[32,128]{1,0:T(8,128)S(1)}, f32[32,128]{1,0:T(8,128)S(1)}, u32[]{:S(2)}, u32[]{:S(2)}) %collective-permute-start.12) | collective-permute-done | bytes 16416 | tf_op jit(solution)/shard_map/ppermute | solution.py:552
  38.3 0.8 %collective-permute-start.13 = (f32[64,128]{1,0:T(8,128)S(1)}, f32[64,128]{1,0:T(8,128)S(1)}, u32[]{:S(2)}, u32[]{:S(2)}) collective-permute-start(f32[64,128]{1,0:T(8,128)S(1)} %stacked.8.one), channel_id=1, source_target_pairs={{0,2},{1,3},{2,0},{3,1},{4,6},{5,7},{6,4},{7,5},{8,10},{9,11},{10,... | collective-permute-start | bytes 98312 | tf_op jit(solution)/shard_map/ppermute | solution.py:552
  39.2 1.4 %input_gradients.4.refs_5_ = bf16[128,1024]{1,0:T(8,128)(2,1)S(1)} custom-call(bf16[128,4096]{1,0:T(8,128)(2,1)S(1)} %get-tuple-element.46.c.refs_0_, f32[16,4096]{1,0:T(8,128)S(1)} %get-tuple-element.47.rate.refs_1_, f32[16,4096]{1,0:T(8,128)S(1)} %get-tuple-element.48.residues.refs_2_, f32[256,128]{1,0:T(8,128)S(1)} %get-tuple-element.80.refs_3_, ...), custom_call_target="tpu_custom_call" | custom-call | tf_op jit(solution)/shard_map/input_gradients/pallas_call | solution.py:496
  40.6 1.4 %input_gradients.5 = (bf16[128,4096]{1,0:T(8,128)(2,1)}, bf16[128,1024]{1,0:T(8,128)(2,1)S(1)}) custom-call(bf16[128,4096]{1,0:T(8,128)(2,1)S(1)} %get-tuple-element.46.c.refs_0_, f32[16,4096]{1,0:T(8,128)S(1)} %get-tuple-element.47.rate.refs_1_, f32[16,4096]{1,0:T(8,128)S(1)} %get-tuple-element.48.residues.refs_2_, ...), custom_call_target="tpu_custom_call" | custom-call | tf_op jit(solution)/shard_map/input_gradients/pallas_call | solution.py:496
  42.8 1.4 %input_gradients.6 = (bf16[128,4096]{1,0:T(8,128)(2,1)}, bf16[128,1024]{1,0:T(8,128)(2,1)S(1)}) custom-call(bf16[128,4096]{1,0:T(8,128)(2,1)S(1)} %get-tuple-element.46.c.refs_0_, f32[16,4096]{1,0:T(8,128)S(1)} %get-tuple-element.47.rate.refs_1_, f32[16,4096]{1,0:T(8,128)S(1)} %get-tuple-element.48.residues.refs_2_, ...), custom_call_target="tpu_custom_call", output_to_operand_aliasing={{0}: (6, {})} | custom-call | tf_op jit(solution)/shard_map/input_gradients/pallas_call | solution.py:496
  44.2 2.8 %input_gradients.7 = (bf16[128,4096]{1,0:T(8,128)(2,1)}, bf16[128,1024]{1,0:T(8,128)(2,1)}) custom-call(bf16[128,4096]{1,0:T(8,128)(2,1)S(1)} %get-tuple-element.46.c.refs_0_, f32[16,4096]{1,0:T(8,128)S(1)} %get-tuple-element.47.rate.refs_1_, f32[16,4096]{1,0:T(8,128)S(1)} %get-tuple-element.48.residues.refs_2_, ...), custom_call_target="tpu_custom_call", output_to_operand_aliasing={{0}: (6, {})} | custom-call | tf_op jit(solution)/shard_map/input_gradients/pallas_call | solution.py:496
  47.1 0.7 %placed.1 = (f32[16,1024]{1,0:T(8,128)}, f32[16,1024]{1,0:T(8,128)}) custom-call(f32[128,128]{1,0:T(8,128)S(1)} %stacked.9.refs_0_, f32[128,128]{1,0:T(8,128)S(1)} %collective-permute-done.14.refs_1_, bf16[128,4096]{1,0:T(8,128)(2,1)} %get-tuple-element.86.refs_2_), custom_call_target="tpu_custom_call" | custom-call | tf_op jit(solution)/shard_map/placed/pallas_call | solution.py:538
  (32 shorter events, 2.2 us)
Async XLA Ops:
  5.3 3.7 %collective-permute-start = (f32[384,128]{1,0:T(8,128)S(1)}, f32[384,128]{1,0:T(8,128)S(1)}, u32[]{:S(2)}, u32[]{:S(2)}) collective-permute-start(f32[384,128]{1,0:T(8,128)S(1)} %get-tuple-element.51), channel_id=1, source_target_pairs={{0,1},{1,0},{2,3},{3,2},{4,5},{5,4},{6,7},{7,6},{8,9},{9,8},{10,11... | collective-permute-start | bytes 589832 | tf_op jit(solution)/shard_map/ppermute | solution.py:552
  8.8 6.3 %collective-permute-start.3 = (f32[384,128]{1,0:T(8,128)S(1)}, f32[384,128]{1,0:T(8,128)S(1)}, u32[]{:S(2)}, u32[]{:S(2)}) collective-permute-start(f32[384,128]{1,0:T(8,128)S(1)} %get-tuple-element.60), channel_id=1, source_target_pairs={{0,1},{1,0},{2,3},{3,2},{4,5},{5,4},{6,7},{7,6},{8,9},{9,8},{10,11... | collective-permute-start | bytes 589832 | tf_op jit(solution)/shard_map/ppermute | solution.py:552
  9.0 8.1 %collective-permute-start.2 = (f32[384,128]{1,0:T(8,128)S(1)}, f32[384,128]{1,0:T(8,128)S(1)}, u32[]{:S(2)}, u32[]{:S(2)}) collective-permute-start(f32[384,128]{1,0:T(8,128)S(1)} %get-tuple-element.58), channel_id=1, source_target_pairs={{0,2},{1,3},{2,0},{3,1},{4,6},{5,7},{6,4},{7,5},{8,10},{9,11},{10,... | collective-permute-start | bytes 589832 | tf_op jit(solution)/shard_map/ppermute | solution.py:552
  15.1 2.1 %collective-permute-start.1 = (f32[384,128]{1,0:T(8,128)S(1)}, f32[384,128]{1,0:T(8,128)S(1)}, u32[]{:S(2)}, u32[]{:S(2)}) collective-permute-start(f32[384,128]{1,0:T(8,128)S(1)} %get-tuple-element.56), channel_id=1, source_target_pairs={{0,1},{1,0},{2,3},{3,2},{4,5},{5,4},{6,7},{7,6},{8,9},{9,8},{10,11... | collective-permute-start | bytes 589832 | tf_op jit(solution)/shard_map/ppermute | solution.py:552
  17.3 6.4 %collective-permute-start.4 = (f32[384,128]{1,0:T(8,128)S(1)}, f32[384,128]{1,0:T(8,128)S(1)}, u32[]{:S(2)}, u32[]{:S(2)}) collective-permute-start(f32[384,128]{1,0:T(8,128)S(1)} %get-tuple-element.63), channel_id=1, source_target_pairs={{0,4},{1,5},{2,6},{3,7},{4,0},{5,1},{6,2},{7,3},{8,12},{9,13},{10,... | collective-permute-start | bytes 589832 | tf_op jit(solution)/shard_map/ppermute | solution.py:552
  19.1 5.8 %collective-permute-start.6 = (f32[384,128]{1,0:T(8,128)S(1)}, f32[384,128]{1,0:T(8,128)S(1)}, u32[]{:S(2)}, u32[]{:S(2)}) collective-permute-start(f32[384,128]{1,0:T(8,128)S(1)} %get-tuple-element.68), channel_id=1, source_target_pairs={{0,2},{1,3},{2,0},{3,1},{4,6},{5,7},{6,4},{7,5},{8,10},{9,11},{10,... | collective-permute-start | bytes 589832 | tf_op jit(solution)/shard_map/ppermute | solution.py:552
  23.6 1.5 %collective-permute-start.5 = (f32[384,128]{1,0:T(8,128)S(1)}, f32[384,128]{1,0:T(8,128)S(1)}, u32[]{:S(2)}, u32[]{:S(2)}) collective-permute-start(f32[384,128]{1,0:T(8,128)S(1)} %get-tuple-element.66), channel_id=1, source_target_pairs={{0,1},{1,0},{2,3},{3,2},{4,5},{5,4},{6,7},{7,6},{8,9},{9,8},{10,11... | collective-permute-start | bytes 589832 | tf_op jit(solution)/shard_map/ppermute | solution.py:552
  25.3 4.0 %collective-permute-start.8 = (f32[64,128]{1,0:T(8,128)S(1)}, f32[64,128]{1,0:T(8,128)S(1)}, u32[]{:S(2)}, u32[]{:S(2)}) collective-permute-start(f32[64,128]{1,0:T(8,128)S(1)} %get-tuple-element.73), channel_id=1, source_target_pairs={{0,8},{8,0},{16,24},{24,16},{1,9},{9,1},{17,25},{25,17},{2,10},{10... | collective-permute-start | bytes 98312 | tf_op jit(solution)/shard_map/ppermute | solution.py:556
  27.0 3.9 %collective-permute-start.7 = (f32[64,128]{1,0:T(8,128)S(1)}, f32[64,128]{1,0:T(8,128)S(1)}, u32[]{:S(2)}, u32[]{:S(2)}) collective-permute-start(f32[64,128]{1,0:T(8,128)S(1)} %slice.3), channel_id=1, source_target_pairs={{0,4},{1,5},{2,6},{3,7},{4,0},{5,1},{6,2},{7,3},{8,12},{9,13},{10,... | collective-permute-start | bytes 98312 | tf_op jit(solution)/shard_map/ppermute | solution.py:552
  30.9 6.0 %collective-permute-start.9 = (f32[128,128]{1,0:T(8,128)S(1)}, f32[128,128]{1,0:T(8,128)S(1)}, u32[]{:S(2)}, u32[]{:S(2)}) collective-permute-start(f32[128,128]{1,0:T(8,128)S(1)} %get-tuple-element.76), channel_id=1, source_target_pairs={{0,2},{1,3},{2,0},{3,1},{4,6},{5,7},{6,4},{7,5},{8,10},{9,11},{10,... | collective-permute-start | bytes 196616 | tf_op jit(solution)/shard_map/ppermute | solution.py:552
  32.1 4.7 %collective-permute-start.10 = (f32[32,128]{1,0:T(8,128)S(1)}, f32[32,128]{1,0:T(8,128)S(1)}, u32[]{:S(2)}, u32[]{:S(2)}) collective-permute-start(f32[32,128]{1,0:T(8,128)S(1)} %get-tuple-element.74.refs_0_), channel_id=1, source_target_pairs={{0,16},{8,24},{16,0},{24,8},{1,17},{9,25},{17,1},{25,9},{2,18},{10... | collective-permute-start | bytes 49160 | tf_op jit(solution)/shard_map/ppermute | solution.py:556
  36.9 2.3 %collective-permute-start.11 = (f32[256,128]{1,0:T(8,128)S(1)}, f32[256,128]{1,0:T(8,128)S(1)}, u32[]{:S(2)}, u32[]{:S(2)}) collective-permute-start(f32[256,128]{1,0:T(8,128)S(1)} %get-tuple-element.81), channel_id=1, source_target_pairs={{0,1},{1,0},{2,3},{3,2},{4,5},{5,4},{6,7},{7,6},{8,9},{9,8},{10,11... | collective-permute-start | bytes 393224 | tf_op jit(solution)/shard_map/ppermute | solution.py:552
  37.0 1.4 %collective-permute-start.12 = (f32[32,128]{1,0:T(8,128)S(1)}, f32[32,128]{1,0:T(8,128)S(1)}, u32[]{:S(2)}, u32[]{:S(2)}) collective-permute-start(f32[32,128]{1,0:T(8,128)S(1)} %added.1.refs_6_.one), channel_id=1, source_target_pairs={{0,1},{1,0},{2,3},{3,2},{4,5},{5,4},{6,7},{7,6},{8,9},{9,8},{10,11... | collective-permute-start | bytes 49160 | tf_op jit(solution)/shard_map/ppermute | solution.py:552
  38.3 3.9 %collective-permute-start.13 = (f32[64,128]{1,0:T(8,128)S(1)}, f32[64,128]{1,0:T(8,128)S(1)}, u32[]{:S(2)}, u32[]{:S(2)}) collective-permute-start(f32[64,128]{1,0:T(8,128)S(1)} %stacked.8.one), channel_id=1, source_target_pairs={{0,2},{1,3},{2,0},{3,1},{4,6},{5,7},{6,4},{7,5},{8,10},{9,11},{10,... | collective-permute-start | bytes 98312 | tf_op jit(solution)/shard_map/ppermute | solution.py:552
  42.3 4.8 %collective-permute-start.14 = (f32[128,128]{1,0:T(8,128)S(1)}, f32[128,128]{1,0:T(8,128)S(1)}, u32[]{:S(2)}, u32[]{:S(2)}) collective-permute-start(f32[128,128]{1,0:T(8,128)S(1)} %stacked.9.refs_0_), channel_id=1, source_target_pairs={{0,4},{1,5},{2,6},{3,7},{4,0},{5,1},{6,2},{7,3},{8,12},{9,13},{10,... | collective-permute-start | bytes 196616 | tf_op jit(solution)/shard_map/ppermute | solution.py:552

commit v5 on v4

--- a/solution.py
+++ b/solution.py
@@ -288,7 +288,8 @@
     )
 
 
-def close_kernel(own, other, rates, residues, term_keep, term_send, small, owned, *, modes, scale):
+def close_kernel(own, other, rates, residues, *refs, modes, scale):
+    term_keep, term_send, small, owned = refs
     chip, core, depth = position()
     size = modes * 4
     for q in range(4):
@@ -347,8 +348,11 @@
     )
 
 
-def add_kernel(one, two, *refs):
-    refs[-1][...] = one[...] + two[...]
+def add_kernel(*refs, count):
+    total = refs[0][...]
+    for ref in refs[1:count]:
+        total = total + ref[...]
+    refs[-1][...] = total
 
 
 def halve_kernel(kept, got, *refs):
@@ -404,67 +408,115 @@
     )
 
 
-def input_kernel(*refs, block, last, given, lead, rows, modes, together):
-    cot, rate, res = refs[:3]
-    entry, lead_ref = refs[3 : 3 + given], refs[3 + given : 4 + given]
-    *outs, cs, ys, ps, rs, ads, done = refs[-(6 + (lead or last) + 1) :]
+def arranged(ref, scratch, block, height, change=None):
+    for i in range(SUBS):
+        tile = ref[:, pl.ds((block * SUBS + i) * LANES, LANES)].astype(f32)
+        scratch[pl.ds(i, height, stride=SUBS), :] = tile if change is None else change(tile)
+
+
+def mode_rows(ref, modes):
+    return [ref[pl.ds(n * SUBS, SUBS), :] for n in range(modes)]
+
+
+def tree_sum(terms):
+    while len(terms) > 1:
+        pairs = [a + b for a, b in zip(terms[::2], terms[1::2])]
+        terms = pairs + ([terms[-1]] if len(terms) % 2 else [])
+    return terms[0]
+
+
+def slab_kernel(cot, rate, res, *refs, block, rows, modes):
+    out, cs, ps, rs = refs[-4:]
+    arranged(cot, cs, block, rows)
+    arranged(rate, ps, block, modes, lambda tile: jnp.exp(-tile))
+    arranged(res, rs, block, modes)
+    poles, weights = mode_rows(ps, modes), mode_rows(rs, modes)
+
+    def step(index, adjoint):
+        now = pl.ds(pl.multiple_of((rows - 1 - index) * SUBS, SUBS), SUBS)
+        value = cs[now, :]
+        adjoint = tuple(a * p + value for a, p in zip(adjoint, poles))
+        out[now, :] = tree_sum([a * w for a, w in zip(adjoint, weights)])
+        return adjoint
+
+    zero = jnp.zeros((SUBS, LANES), f32)
+    lax.fori_loop(0, rows, step, (zero,) * modes, unroll=8)
+
+
+def slab_gradients(cotangent, rate, residues, block, near=()):
+    rows, modes = cotangent.shape[0], rate.shape[0]
+    small = (modes * SUBS, LANES)
+    return local_call(
+        functools.partial(slab_kernel, block=block, rows=rows, modes=modes),
+        "slab_gradients",
+        [(rows * SUBS, LANES)],
+        [cotangent, rate, residues, *near],
+        [(rows * SUBS, LANES), small, small],
+        megabytes=3,
+    )[0]
+
+
+def input_kernel(*refs, block, given, lead, own, fresh, rows, modes):
+    refs = list(refs)
+    take = lambda count: [refs.pop(0) for _ in range(count)]
+    base, rate, res = take(3)
+    entry, before = take(given), take(lead)
+    done, ads, rs, ps, cs, ys, sent = [refs.pop() for _ in range(7)]
+    whole = refs.pop() if lead or own else None
     width = SUBS * LANES
     copies = []
+
+    def send(source, target):
+        copies.append(pltpu.make_async_copy(source, target, done.at[len(copies)]))
+        copies[-1].start()
+
     if lead:
-        lanes = pl.ds((block - 1) * width, width)
-        copies.append(pltpu.make_async_copy(lead_ref[0], outs[0].at[:, lanes], done.at[0]))
-        copies[0].start()
-    place = position()[:2] if given == 2 else None
-    scratch = (cs, ys, ps, rs, ads)
-    sent = outs[-1]
-    block_of_inputs(block, cot, rate, res, entry, place, sent, scratch, rows, modes, together)
-    if last:
-        lanes = pl.ds(block * width, width)
-        copies.append(pltpu.make_async_copy(sent, outs[0].at[:, lanes], done.at[1]))
-        copies[-1].start()
+        send(before[0], whole.at[:, pl.ds((block - 1) * width, width)])
+    if fresh:
+        arranged(base, cs, block, rows)
+    arranged(rate, ps, block, modes, lambda tile: jnp.exp(-tile))
+    arranged(res, rs, block, modes)
+    if given == 1:
+        arranged(entry[0], ads, block, modes)
+    else:
+        chip, half, _ = position()
+        for j in range(4):
+            for core, source in enumerate(entry):
+                rows_of = pl.ds(j * modes * 4 + block, modes, stride=4)
+                i = 2 * (chip ^ j) + (half ^ core)
+                ads[pl.ds(i, modes, stride=SUBS), :] = source[rows_of, :]
+    poles, weights = mode_rows(ps, modes), mode_rows(rs, modes)
+    state = tuple(mode_rows(ads, modes))
+    if not fresh:
+        state = tuple(a * w for a, w in zip(state, weights))
+    pieces = 4 if own else 1
+    height = rows // pieces
+
+    for piece in reversed(range(pieces)):
+
+        def step(index, state):
+            position_in = (piece + 1) * height - 1 - index
+            now = pl.ds(pl.multiple_of(position_in * SUBS, SUBS), SUBS)
+            if fresh:
+                value = cs[now, :]
+                state = tuple(a * p + value for a, p in zip(state, poles))
+                ys[now, :] = tree_sum([a * w for a, w in zip(state, weights)])
+            else:
+                state = tuple(a * p for a, p in zip(state, poles))
+                ys[now, :] = base[now, :] + tree_sum(list(state))
+            return state
+
+        state = lax.fori_loop(0, height, step, state, unroll=8)
+        span = pl.ds(piece * height, height)
+        for i in range(SUBS):
+            tile = ys[pl.ds(piece * height * SUBS + i, height, stride=SUBS), :].astype(sent.dtype)
+            sent[span, pl.ds(i * LANES, LANES)] = tile
+        if own:
+            send(sent.at[span], whole.at[span, pl.ds(block * width, width)])
     for copy in copies:
         copy.wait()
 
 
-def block_of_inputs(q, cot, rate, res, given, place, sent, scratch, rows, modes, together):
-    cs, ys, ps, rs, ads = scratch
-    size = modes * 4
-
-    def tile(i):
-        return pl.ds((q * SUBS + i) * LANES, LANES)
-
-    for i in range(SUBS):
-        lanes = tile(i)
-        cs[pl.ds(i, rows, stride=SUBS), :] = cot[:, lanes].astype(f32)
-        ps[pl.ds(i, modes, stride=SUBS), :] = jnp.exp(-rate[:, lanes])
-        rs[pl.ds(i, modes, stride=SUBS), :] = res[:, lanes]
-    if len(given) == 1:
-        spread([given[0][:, tile(i)] for i in range(SUBS)], ads, modes, SUBS)
-    for j in range(4 if len(given) == 2 else 0):
-        for core, source in enumerate(given):
-            i = 2 * (place[0] ^ j) + (place[1] ^ core)
-            ads[pl.ds(i, modes, stride=SUBS), :] = source[pl.ds(j * size + q, modes, stride=4), :]
-
-    for group in range(modes // together):
-        at = [pl.ds((group * together + m) * SUBS, SUBS) for m in range(together)]
-        poles = [ps[a, :] for a in at]
-        weights = [rs[a, :] for a in at]
-
-        def step(index, adjoint):
-            now = pl.ds(pl.multiple_of((rows - 1 - index) * SUBS, SUBS), SUBS)
-            value = cs[now, :]
-            adjoint = tuple(a * p + value for a, p in zip(adjoint, poles))
-            terms = [a * w for a, w in zip(adjoint, weights)]
-            while len(terms) > 1:
-                terms = [a + b for a, b in zip(terms[::2], terms[1::2])]
-            ys[now, :] = terms[0] if group == 0 else ys[now, :] + terms[0]
-            return adjoint
-
-        lax.fori_loop(0, rows, step, tuple(ads[a, :] for a in at), unroll=8)
-    for i in range(SUBS):
-        sent[:, pl.ds(i * LANES, LANES)] = ys[pl.ds(i, rows, stride=SUBS), :].astype(sent.dtype)
-
-
 def far_away():
     return pl.BlockSpec(memory_space=pltpu.HBM)
 
@@ -473,50 +525,43 @@
     return pltpu.with_memory_space_constraint(value, pltpu.HBM)
 
 
-def input_gradients(cotangent, rate, residues, given, block, lead=None, onto=None, last=False):
+def input_gradients(cotangent, rate, residues, given, block, lead=None, onto=None, own=False, slab=None):
     rows, channels = cotangent.shape
-    modes = rate.shape[0]
+    modes, dtype = rate.shape[0], cotangent.dtype
     width = SUBS * LANES
-    scratch = lambda height: pltpu.VMEM((height * SUBS, LANES), f32)
-    operands = [here(item) for item in (cotangent, rate, residues, *given)]
-    shapes, specs = [], []
-    if lead is not None:
-        operands.append(here(lead))
+    base = cotangent if slab is None else slab
+    small = pltpu.VMEM((modes * SUBS, LANES), f32)
+    operands = [base, rate, residues, *given, *([] if lead is None else [lead])]
+    operands = [here(item) for item in operands]
     in_specs = [vmem() for _ in operands]
-    aliases = {}
-    if lead is not None or last:
-        shapes.append(jax.ShapeDtypeStruct((rows, channels), cotangent.dtype))
+    shapes, specs, aliases = [], [], {}
+    if lead is not None or own:
+        shapes.append(jax.ShapeDtypeStruct((rows, channels), dtype))
         specs.append(far_away())
     if onto is not None:
         aliases = {len(operands): 0}
         operands.append(outside(onto))
         in_specs.append(far_away())
-    shapes.append(pltpu.VMEM((rows, width), cotangent.dtype))
+    shapes.append(pltpu.VMEM((rows, width), dtype))
     specs.append(vmem())
     return pl.pallas_call(
         functools.partial(
             input_kernel,
             block=block,
-            last=last,
             given=len(given),
-            lead=lead is not None,
+            lead=int(lead is not None),
+            own=own,
+            fresh=slab is None,
             rows=rows,
             modes=modes,
-            together=16,
         ),
         in_specs=in_specs,
         out_specs=specs,
         out_shape=shapes,
-        scratch_shapes=[
-            scratch(rows),
-            scratch(rows),
-            scratch(modes),
-            scratch(modes),
-            scratch(modes),
-            pltpu.SemaphoreType.DMA((2,)),
-        ],
+        scratch_shapes=[pltpu.VMEM((rows * SUBS, LANES), f32)] * 2
+        + [small, small, small, pltpu.SemaphoreType.DMA((5,))],
         input_output_aliases=aliases,
-        compiler_params=room(4),
+        compiler_params=room(3),
         name="input_gradients",
     )(*operands)
 
@@ -577,6 +622,7 @@
     got2 = crossed(cores(3, ours, theirs3, rates, (rates1,)), 2)
     theirs2, ours2, rates2 = more(2, (holds[3],))
     got0 = crossed(cores(1, ours1, theirs1, rates1, (rates2,)), 2)
+    slab = functools.partial(slab_gradients, c, rate, residues)
     landed = stacked(got2, holds[1], 8)
     row2 = cores(2, ours2, theirs2, rates2, (landed,))
     row2, hold_side = paired(row2, got2, rates2, 1, 2 * rows, modes)
@@ -589,12 +635,16 @@
     scale = 1.0 / math.sqrt(4 * rows * 8)
     term_keep, term_send = closed(row0, other, rates0, residues, scale)
     half = (2 * modes, LANES)
+    slab2 = slab(2, (term_keep,))
     keep, send = local_call(
-        halve_kernel, "halved", [half, half], [term_keep, shifted(term_send, 1)]
+        halve_kernel, "halved", [half, half], [term_keep, shifted(term_send, 1), slab2]
     )
     back_keep, back_send = handed(other, beside, hold_own, hold_side, modes, (send,))
     back_near = crossed(back_send, 2)
-    (total,) = local_call(add_kernel, "added", [half], [keep, shifted(send, 2)])
+    slab3 = slab(3, (back_keep,))
+    (total,) = local_call(
+        functools.partial(add_kernel, count=2), "added", [half], [keep, shifted(send, 2), slab3]
+    )
     mine, others = entries(back_keep, back_near, [holds[j] for j in range(4)], modes, (total,))
     entry = (mine, crossed(others, 1))
     both = stacked(total, crossed(total, 1), 2 * modes)
@@ -602,8 +652,8 @@
     (part0,) = gradients(0)
     grad_inputs, part1 = gradients(1, part0)
     four = stacked(both, crossed(both, 2), 4 * modes, (), (part1,))
-    grad_inputs, part2 = gradients(2, part1, grad_inputs)
-    grad_inputs, _ = gradients(3, part2, grad_inputs, True)
+    grad_inputs, part2 = gradients(2, part1, grad_inputs, False, slab2)
+    grad_inputs, _ = gradients(3, part2, grad_inputs, True, slab3)
     grad_residues, grad_rate = placed([four, crossed(four, 4)], modes, grad_inputs)
     return (grad_inputs[None], grad_residues, grad_rate)
 

time: 47.9 us -> 47.3 us (0.987)
  waiting for transfers between devices: 9.87 us -> 7.69 us
  Pallas kernels: 22 us -> 23.6 us
    ppermute x2, waiting for transfers between devices: 3.93 us -> 1.31 us  [shifted(): return lax.ppermute(value, 'dp', [(i, i ^ distance) for i in range(4)])]
    pallas_call x19 -> x21, Pallas kernels: 9.57 us -> 12.2 us  [local_call(): pl.pallas_call(kernel, in_specs=[vmem() for _ in operands] + [far_away()...]
    pallas_call x4, Pallas kernels: 7.14 us -> 6.16 us  [input_gradients(): pl.pallas_call(functools.partial(input_kernel, block=block, given=len(giv...]
  transfers between devices with their start and end apart: 15 -> 15, of which waited for: 8 -> 9; matrix products, arithmetic and copies ran while one was open for 0% -> 0% of each run, Pallas kernels for 34% -> 38%
where the time goes in v5:
time: 47.3 us; the launch traced here: 47.2 us
  Pallas kernels  23.6 us (50%)
  starting transfers between devices  15 us (32%)
  waiting for transfers between devices  7.69 us (16%)
  between operations  0.83 us (2%)
    pallas_call x21, Pallas kernels, local_call(): pl.pallas_call(kernel, in_specs=[vmem() for _ in operands] + [far_away()...  12.2 us
    ppermute x13, starting transfers between devices, crossed(): return lax.ppermute(value, 'context', [(i, i ^ distance) for i in range(8)])  10.8 us
    ppermute x13, waiting for transfers between devices, crossed(): return lax.ppermute(value, 'context', [(i, i ^ distance) for i in range(8)])  6.38 us
    pallas_call x4, Pallas kernels, input_gradients(): pl.pallas_call(functools.partial(input_kernel, block=block, given=len(giv...  6.16 us
    pallas_call x1, Pallas kernels, first_summaries(): pl.pallas_call(functools.partial(first_kernel, **static), in_specs=[far_a...  4.62 us
    ppermute x2, starting transfers between devices, shifted(): return lax.ppermute(value, 'dp', [(i, i ^ distance) for i in range(4)])  4.23 us
    ppermute x2, waiting for transfers between devices, shifted(): return lax.ppermute(value, 'dp', [(i, i ^ distance) for i in range(4)])  1.31 us
  transfers between devices with their start and end apart: 15, of which 9 were waited for; matrix products, arithmetic and copies ran while one was open for 0% of the time, Pallas kernels for 38%

profile of v5, /device:TPU:0, one launch (start us, length us, event | category | flops | bytes accessed | tf_op | source)
XLA Modules:
  0.0 47.2 jit_solution(13805010362418990393)
XLA Ops:
  0.6 4.6 %first_summaries.1 = (f32[384,128]{1,0:T(8,128)S(1)}, f32[384,128]{1,0:T(8,128)S(1)}, f32[64,128]{1,0:T(8,128)S(1)}, bf16[128,4096]{1,0:T(8,128)(2,1)S(1)}, bf16...) custom-call(bf16[128,4096]{1,0:T(8,128)(2,1)} %bitcast.4, bf16[128,4096]{1,0:T(8,128)(2,1)} %bitcast.5, ...), custom_call_target="tpu_custom_call" | custom-call | tf_op jit(solution)/shard_map/first_summaries/pallas_call | solution.py:230
  5.3 0.5 %collective-permute-start = (f32[384,128]{1,0:T(8,128)S(1)}, f32[384,128]{1,0:T(8,128)S(1)}, u32[]{:S(2)}, u32[]{:S(2)}) collective-permute-start(f32[384,128]{1,0:T(8,128)S(1)} %get-tuple-element.51), channel_id=1, source_target_pairs={{0,1},{1,0},{2,3},{3,2},{4,5},{5,4},{6,7},{7,6},{8,9},{9,8},{10,11... | collective-permute-start | bytes 589832 | tf_op jit(solution)/shard_map/ppermute | solution.py:597
  5.8 3.0 %summaries.3 = (f32[384,128]{1,0:T(8,128)S(1)}, f32[384,128]{1,0:T(8,128)S(1)}, f32[64,128]{1,0:T(8,128)S(1)}) custom-call(bf16[128,4096]{1,0:T(8,128)(2,1)S(1)} %get-tuple-element.49.x, bf16[128,4096]{1,0:T(8,128)(2,1)S(1)} %get-tuple-element.46.c.cot.refs_0_, f32[16,4096]{1,0:T(8,128)S(1)} %get-tuple-element.47.rate.refs_1_), custom_call_target="tpu_custom_call" | custom-call | tf_op jit(solution)/shard_map/summaries/pallas_call | solution.py:43
  9.0 3.0 %collective-permute-start.2 = (f32[384,128]{1,0:T(8,128)S(1)}, f32[384,128]{1,0:T(8,128)S(1)}, u32[]{:S(2)}, u32[]{:S(2)}) collective-permute-start(f32[384,128]{1,0:T(8,128)S(1)} %get-tuple-element.58), channel_id=1, source_target_pairs={{0,2},{1,3},{2,0},{3,1},{4,6},{5,7},{6,4},{7,5},{8,10},{9,11},{10,... | collective-permute-start | bytes 589832 | tf_op jit(solution)/shard_map/ppermute | solution.py:597
  12.0 3.0 %summaries.4 = (f32[384,128]{1,0:T(8,128)S(1)}, f32[384,128]{1,0:T(8,128)S(1)}, f32[64,128]{1,0:T(8,128)S(1)}) custom-call(bf16[128,4096]{1,0:T(8,128)(2,1)S(1)} %get-tuple-element.49.x, bf16[128,4096]{1,0:T(8,128)(2,1)S(1)} %get-tuple-element.46.c.cot.refs_0_, f32[16,4096]{1,0:T(8,128)S(1)} %get-tuple-element.47.rate.refs_1_, ...), custom_call_target="tpu_custom_call" | custom-call | tf_op jit(solution)/shard_map/summaries/pallas_call | solution.py:43
  15.2 1.9 %collective-permute-done.2.one.other = f32[384,128]{1,0:T(8,128)S(1)} collective-permute-done((f32[384,128]{1,0:T(8,128)S(1)}, f32[384,128]{1,0:T(8,128)S(1)}, u32[]{:S(2)}, u32[]{:S(2)}) %collective-permute-start.2) | collective-permute-done | bytes 196640 | tf_op jit(solution)/shard_map/ppermute | solution.py:597
  17.3 1.8 %collective-permute-start.4 = (f32[384,128]{1,0:T(8,128)S(1)}, f32[384,128]{1,0:T(8,128)S(1)}, u32[]{:S(2)}, u32[]{:S(2)}) collective-permute-start(f32[384,128]{1,0:T(8,128)S(1)} %get-tuple-element.63), channel_id=1, source_target_pairs={{0,4},{1,5},{2,6},{3,7},{4,0},{5,1},{6,2},{7,3},{8,12},{9,13},{10,... | collective-permute-start | bytes 589832 | tf_op jit(solution)/shard_map/ppermute | solution.py:597
  19.1 1.5 %collective-permute-start.6 = (f32[384,128]{1,0:T(8,128)S(1)}, f32[384,128]{1,0:T(8,128)S(1)}, u32[]{:S(2)}, u32[]{:S(2)}) collective-permute-start(f32[384,128]{1,0:T(8,128)S(1)} %get-tuple-element.68), channel_id=1, source_target_pairs={{0,2},{1,3},{2,0},{3,1},{4,6},{5,7},{6,4},{7,5},{8,10},{9,11},{10,... | collective-permute-start | bytes 589832 | tf_op jit(solution)/shard_map/ppermute | solution.py:597
  20.6 3.0 %summaries.5 = (f32[384,128]{1,0:T(8,128)S(1)}, f32[384,128]{1,0:T(8,128)S(1)}, f32[64,128]{1,0:T(8,128)S(1)}) custom-call(bf16[128,4096]{1,0:T(8,128)(2,1)S(1)} %get-tuple-element.49.x, bf16[128,4096]{1,0:T(8,128)(2,1)S(1)} %get-tuple-element.46.c.cot.refs_0_, f32[16,4096]{1,0:T(8,128)S(1)} %get-tuple-element.47.rate.refs_1_, ...), custom_call_target="tpu_custom_call" | custom-call | tf_op jit(solution)/shard_map/summaries/pallas_call | solution.py:43
  23.7 1.2 %collective-permute-done.6.two.other = f32[384,128]{1,0:T(8,128)S(1)} collective-permute-done((f32[384,128]{1,0:T(8,128)S(1)}, f32[384,128]{1,0:T(8,128)S(1)}, u32[]{:S(2)}, u32[]{:S(2)}) %collective-permute-start.6) | collective-permute-done | bytes 196640 | tf_op jit(solution)/shard_map/ppermute | solution.py:597
  25.3 1.6 %collective-permute-start.8 = (f32[64,128]{1,0:T(8,128)S(1)}, f32[64,128]{1,0:T(8,128)S(1)}, u32[]{:S(2)}, u32[]{:S(2)}) collective-permute-start(f32[64,128]{1,0:T(8,128)S(1)} %get-tuple-element.73), channel_id=1, source_target_pairs={{0,8},{8,0},{16,24},{24,16},{1,9},{9,1},{17,25},{25,17},{2,10},{10... | collective-permute-start | bytes 98312 | tf_op jit(solution)/shard_map/ppermute | solution.py:601
  27.5 1.3 %slab_gradients.2.refs_0_ = f32[1024,128]{1,0:T(8,128)S(1)} custom-call(bf16[128,4096]{1,0:T(8,128)(2,1)S(1)} %get-tuple-element.46.c.cot.refs_0_, f32[16,4096]{1,0:T(8,128)S(1)} %get-tuple-element.47.rate.refs_1_, f32[16,4096]{1,0:T(8,128)S(1)} %get-tuple-element.48.residues.res.refs_2_, f32[64,128]{1,0:T(8,128)S(1)} %get-tuple-element.72.refs_0_.kept), custom_call_target="tpu_custom_call" | custom-call | tf_op jit(solution)/shard_map/slab_gradients/pallas_call | solution.py:43
  29.3 1.6 %collective-permute-done.7.beside = f32[64,128]{1,0:T(8,128)S(1)} collective-permute-done((f32[64,128]{1,0:T(8,128)S(1)}, f32[64,128]{1,0:T(8,128)S(1)}, u32[]{:S(2)}, u32[]{:S(2)}) %collective-permute-start.7) | collective-permute-done | bytes 32800 | tf_op jit(solution)/shard_map/ppermute | solution.py:597
  30.9 1.2 %collective-permute-start.9 = (f32[128,128]{1,0:T(8,128)S(1)}, f32[128,128]{1,0:T(8,128)S(1)}, u32[]{:S(2)}, u32[]{:S(2)}) collective-permute-start(f32[128,128]{1,0:T(8,128)S(1)} %get-tuple-element.76), channel_id=1, source_target_pairs={{0,2},{1,3},{2,0},{3,1},{4,6},{5,7},{6,4},{7,5},{8,10},{9,11},{10,... | collective-permute-start | bytes 196616 | tf_op jit(solution)/shard_map/ppermute | solution.py:597
  32.1 2.6 %collective-permute-start.10 = (f32[32,128]{1,0:T(8,128)S(1)}, f32[32,128]{1,0:T(8,128)S(1)}, u32[]{:S(2)}, u32[]{:S(2)}) collective-permute-start(f32[32,128]{1,0:T(8,128)S(1)} %get-tuple-element.74.refs_0_), channel_id=1, source_target_pairs={{0,16},{8,24},{16,0},{24,8},{1,17},{9,25},{17,1},{25,9},{2,18},{10... | collective-permute-start | bytes 49160 | tf_op jit(solution)/shard_map/ppermute | solution.py:601
  34.7 1.3 %slab_gradients.3.refs_2_.refs_0_ = f32[1024,128]{1,0:T(8,128)S(1)} custom-call(bf16[128,4096]{1,0:T(8,128)(2,1)S(1)} %get-tuple-element.46.c.cot.refs_0_, f32[16,4096]{1,0:T(8,128)S(1)} %get-tuple-element.47.rate.refs_1_, f32[16,4096]{1,0:T(8,128)S(1)} %get-tuple-element.48.residues.res.refs_2_, f32[128,128]{1,0:T(8,128)S(1)} %get-tuple-element.75.refs_0_), custom_call_target="tpu_custom_call" | custom-call | tf_op jit(solution)/shard_map/slab_gradients/pallas_call | solution.py:43
  36.0 0.8 %collective-permute-done.10.refs_1_ = f32[32,128]{1,0:T(8,128)S(1)} collective-permute-done((f32[32,128]{1,0:T(8,128)S(1)}, f32[32,128]{1,0:T(8,128)S(1)}, u32[]{:S(2)}, u32[]{:S(2)}) %collective-permute-start.10) | collective-permute-done | bytes 16416 | tf_op jit(solution)/shard_map/ppermute | solution.py:601
  37.5 0.9 %collective-permute-done.12.two = f32[32,128]{1,0:T(8,128)S(1)} collective-permute-done((f32[32,128]{1,0:T(8,128)S(1)}, f32[32,128]{1,0:T(8,128)S(1)}, u32[]{:S(2)}, u32[]{:S(2)}) %collective-permute-start.12) | collective-permute-done | bytes 16416 | tf_op jit(solution)/shard_map/ppermute | solution.py:597
  38.3 0.8 %collective-permute-start.13 = (f32[64,128]{1,0:T(8,128)S(1)}, f32[64,128]{1,0:T(8,128)S(1)}, u32[]{:S(2)}, u32[]{:S(2)}) collective-permute-start(f32[64,128]{1,0:T(8,128)S(1)} %stacked.8.one), channel_id=1, source_target_pairs={{0,2},{1,3},{2,0},{3,1},{4,6},{5,7},{6,4},{7,5},{8,10},{9,11},{10,... | collective-permute-start | bytes 98312 | tf_op jit(solution)/shard_map/ppermute | solution.py:597
  39.2 1.5 %input_gradients.4.refs_5_ = bf16[128,1024]{1,0:T(8,128)(2,1)S(1)} custom-call(bf16[128,4096]{1,0:T(8,128)(2,1)S(1)} %get-tuple-element.46.c.cot.refs_0_, f32[16,4096]{1,0:T(8,128)S(1)} %get-tuple-element.47.rate.refs_1_, f32[16,4096]{1,0:T(8,128)S(1)} %get-tuple-element.48.residues.res.refs_2_, f32[256,128]{1,0:T(8,128)S(1)} %get-tuple-element.80.refs_3_, ...), custom_call_target="tpu_custom_call" | custom-call | tf_op jit(solution)/shard_map/input_gradients/pallas_call | solution.py:547
  40.7 1.5 %input_gradients.5 = (bf16[128,4096]{1,0:T(8,128)(2,1)}, bf16[128,1024]{1,0:T(8,128)(2,1)S(1)}) custom-call(bf16[128,4096]{1,0:T(8,128)(2,1)S(1)} %get-tuple-element.46.c.cot.refs_0_, f32[16,4096]{1,0:T(8,128)S(1)} %get-tuple-element.47.rate.refs_1_, f32[16,4096]{1,0:T(8,128)S(1)} %get-tuple-element.48.residues.res.refs_2_, ...), custom_call_target="tpu_custom_call" | custom-call | tf_op jit(solution)/shard_map/input_gradients/pallas_call | solution.py:547
  42.8 0.9 %input_gradients.6 = (bf16[128,4096]{1,0:T(8,128)(2,1)}, bf16[128,1024]{1,0:T(8,128)(2,1)S(1)}) custom-call(f32[1024,128]{1,0:T(8,128)S(1)} %slab_gradients.2.refs_0_, f32[16,4096]{1,0:T(8,128)S(1)} %get-tuple-element.47.rate.refs_1_, f32[16,4096]{1,0:T(8,128)S(1)} %get-tuple-element.48.residues.res.refs_2_, ...), custom_call_target="tpu_custom_call", output_to_operand_aliasing={{0}: (6, {})} | custom-call | tf_op jit(solution)/shard_map/input_gradients/pallas_call | solution.py:547
  43.7 2.3 %input_gradients.7 = (bf16[128,4096]{1,0:T(8,128)(2,1)}, bf16[128,1024]{1,0:T(8,128)(2,1)}) custom-call(f32[1024,128]{1,0:T(8,128)S(1)} %slab_gradients.3.refs_2_.refs_0_, f32[16,4096]{1,0:T(8,128)S(1)} %get-tuple-element.47.rate.refs_1_, f32[16,4096]{1,0:T(8,128)S(1)} %get-tuple-element.48.residues.res.refs_2_, ...), custom_call_target="tpu_custom_call", output_to_operand_aliasing={{0}: (6, {})} | custom-call | tf_op jit(solution)/shard_map/input_gradients/pallas_call | solution.py:547
  46.5 0.7 %placed.1 = (f32[16,1024]{1,0:T(8,128)}, f32[16,1024]{1,0:T(8,128)}) custom-call(f32[128,128]{1,0:T(8,128)S(1)} %stacked.9.refs_0_, f32[128,128]{1,0:T(8,128)S(1)} %collective-permute-done.14.refs_1_, bf16[128,4096]{1,0:T(8,128)(2,1)} %get-tuple-element.86.refs_2_), custom_call_target="tpu_custom_call" | custom-call | tf_op jit(solution)/shard_map/placed/pallas_call | solution.py:583
  (34 shorter events, 3.7 us)
Async XLA Ops:
  5.3 3.7 %collective-permute-start = (f32[384,128]{1,0:T(8,128)S(1)}, f32[384,128]{1,0:T(8,128)S(1)}, u32[]{:S(2)}, u32[]{:S(2)}) collective-permute-start(f32[384,128]{1,0:T(8,128)S(1)} %get-tuple-element.51), channel_id=1, source_target_pairs={{0,1},{1,0},{2,3},{3,2},{4,5},{5,4},{6,7},{7,6},{8,9},{9,8},{10,11... | collective-permute-start | bytes 589832 | tf_op jit(solution)/shard_map/ppermute | solution.py:597
  8.8 6.3 %collective-permute-start.3 = (f32[384,128]{1,0:T(8,128)S(1)}, f32[384,128]{1,0:T(8,128)S(1)}, u32[]{:S(2)}, u32[]{:S(2)}) collective-permute-start(f32[384,128]{1,0:T(8,128)S(1)} %get-tuple-element.60), channel_id=1, source_target_pairs={{0,1},{1,0},{2,3},{3,2},{4,5},{5,4},{6,7},{7,6},{8,9},{9,8},{10,11... | collective-permute-start | bytes 589832 | tf_op jit(solution)/shard_map/ppermute | solution.py:597
  9.0 8.1 %collective-permute-start.2 = (f32[384,128]{1,0:T(8,128)S(1)}, f32[384,128]{1,0:T(8,128)S(1)}, u32[]{:S(2)}, u32[]{:S(2)}) collective-permute-start(f32[384,128]{1,0:T(8,128)S(1)} %get-tuple-element.58), channel_id=1, source_target_pairs={{0,2},{1,3},{2,0},{3,1},{4,6},{5,7},{6,4},{7,5},{8,10},{9,11},{10,... | collective-permute-start | bytes 589832 | tf_op jit(solution)/shard_map/ppermute | solution.py:597
  15.1 2.1 %collective-permute-start.1 = (f32[384,128]{1,0:T(8,128)S(1)}, f32[384,128]{1,0:T(8,128)S(1)}, u32[]{:S(2)}, u32[]{:S(2)}) collective-permute-start(f32[384,128]{1,0:T(8,128)S(1)} %get-tuple-element.56), channel_id=1, source_target_pairs={{0,1},{1,0},{2,3},{3,2},{4,5},{5,4},{6,7},{7,6},{8,9},{9,8},{10,11... | collective-permute-start | bytes 589832 | tf_op jit(solution)/shard_map/ppermute | solution.py:597
  17.3 6.4 %collective-permute-start.4 = (f32[384,128]{1,0:T(8,128)S(1)}, f32[384,128]{1,0:T(8,128)S(1)}, u32[]{:S(2)}, u32[]{:S(2)}) collective-permute-start(f32[384,128]{1,0:T(8,128)S(1)} %get-tuple-element.63), channel_id=1, source_target_pairs={{0,4},{1,5},{2,6},{3,7},{4,0},{5,1},{6,2},{7,3},{8,12},{9,13},{10,... | collective-permute-start | bytes 589832 | tf_op jit(solution)/shard_map/ppermute | solution.py:597
  19.1 5.8 %collective-permute-start.6 = (f32[384,128]{1,0:T(8,128)S(1)}, f32[384,128]{1,0:T(8,128)S(1)}, u32[]{:S(2)}, u32[]{:S(2)}) collective-permute-start(f32[384,128]{1,0:T(8,128)S(1)} %get-tuple-element.68), channel_id=1, source_target_pairs={{0,2},{1,3},{2,0},{3,1},{4,6},{5,7},{6,4},{7,5},{8,10},{9,11},{10,... | collective-permute-start | bytes 589832 | tf_op jit(solution)/shard_map/ppermute | solution.py:597
  23.6 1.5 %collective-permute-start.5 = (f32[384,128]{1,0:T(8,128)S(1)}, f32[384,128]{1,0:T(8,128)S(1)}, u32[]{:S(2)}, u32[]{:S(2)}) collective-permute-start(f32[384,128]{1,0:T(8,128)S(1)} %get-tuple-element.66), channel_id=1, source_target_pairs={{0,1},{1,0},{2,3},{3,2},{4,5},{5,4},{6,7},{7,6},{8,9},{9,8},{10,11... | collective-permute-start | bytes 589832 | tf_op jit(solution)/shard_map/ppermute | solution.py:597
  25.3 4.0 %collective-permute-start.8 = (f32[64,128]{1,0:T(8,128)S(1)}, f32[64,128]{1,0:T(8,128)S(1)}, u32[]{:S(2)}, u32[]{:S(2)}) collective-permute-start(f32[64,128]{1,0:T(8,128)S(1)} %get-tuple-element.73), channel_id=1, source_target_pairs={{0,8},{8,0},{16,24},{24,16},{1,9},{9,1},{17,25},{25,17},{2,10},{10... | collective-permute-start | bytes 98312 | tf_op jit(solution)/shard_map/ppermute | solution.py:601
  27.0 3.9 %collective-permute-start.7 = (f32[64,128]{1,0:T(8,128)S(1)}, f32[64,128]{1,0:T(8,128)S(1)}, u32[]{:S(2)}, u32[]{:S(2)}) collective-permute-start(f32[64,128]{1,0:T(8,128)S(1)} %slice.3), channel_id=1, source_target_pairs={{0,4},{1,5},{2,6},{3,7},{4,0},{5,1},{6,2},{7,3},{8,12},{9,13},{10,... | collective-permute-start | bytes 98312 | tf_op jit(solution)/shard_map/ppermute | solution.py:597
  30.9 6.0 %collective-permute-start.9 = (f32[128,128]{1,0:T(8,128)S(1)}, f32[128,128]{1,0:T(8,128)S(1)}, u32[]{:S(2)}, u32[]{:S(2)}) collective-permute-start(f32[128,128]{1,0:T(8,128)S(1)} %get-tuple-element.76), channel_id=1, source_target_pairs={{0,2},{1,3},{2,0},{3,1},{4,6},{5,7},{6,4},{7,5},{8,10},{9,11},{10,... | collective-permute-start | bytes 196616 | tf_op jit(solution)/shard_map/ppermute | solution.py:597
  32.1 4.7 %collective-permute-start.10 = (f32[32,128]{1,0:T(8,128)S(1)}, f32[32,128]{1,0:T(8,128)S(1)}, u32[]{:S(2)}, u32[]{:S(2)}) collective-permute-start(f32[32,128]{1,0:T(8,128)S(1)} %get-tuple-element.74.refs_0_), channel_id=1, source_target_pairs={{0,16},{8,24},{16,0},{24,8},{1,17},{9,25},{17,1},{25,9},{2,18},{10... | collective-permute-start | bytes 49160 | tf_op jit(solution)/shard_map/ppermute | solution.py:601
  36.9 2.3 %collective-permute-start.11 = (f32[256,128]{1,0:T(8,128)S(1)}, f32[256,128]{1,0:T(8,128)S(1)}, u32[]{:S(2)}, u32[]{:S(2)}) collective-permute-start(f32[256,128]{1,0:T(8,128)S(1)} %get-tuple-element.81), channel_id=1, source_target_pairs={{0,1},{1,0},{2,3},{3,2},{4,5},{5,4},{6,7},{7,6},{8,9},{9,8},{10,11... | collective-permute-start | bytes 393224 | tf_op jit(solution)/shard_map/ppermute | solution.py:597
  37.0 1.4 %collective-permute-start.12 = (f32[32,128]{1,0:T(8,128)S(1)}, f32[32,128]{1,0:T(8,128)S(1)}, u32[]{:S(2)}, u32[]{:S(2)}) collective-permute-start(f32[32,128]{1,0:T(8,128)S(1)} %added.1.refs_6_.one), channel_id=1, source_target_pairs={{0,1},{1,0},{2,3},{3,2},{4,5},{5,4},{6,7},{7,6},{8,9},{9,8},{10,11... | collective-permute-start | bytes 49160 | tf_op jit(solution)/shard_map/ppermute | solution.py:597
  38.3 3.9 %collective-permute-start.13 = (f32[64,128]{1,0:T(8,128)S(1)}, f32[64,128]{1,0:T(8,128)S(1)}, u32[]{:S(2)}, u32[]{:S(2)}) collective-permute-start(f32[64,128]{1,0:T(8,128)S(1)} %stacked.8.one), channel_id=1, source_target_pairs={{0,2},{1,3},{2,0},{3,1},{4,6},{5,7},{6,4},{7,5},{8,10},{9,11},{10,... | collective-permute-start | bytes 98312 | tf_op jit(solution)/shard_map/ppermute | solution.py:597
  42.3 4.3 %collective-permute-start.14 = (f32[128,128]{1,0:T(8,128)S(1)}, f32[128,128]{1,0:T(8,128)S(1)}, u32[]{:S(2)}, u32[]{:S(2)}) collective-permute-start(f32[128,128]{1,0:T(8,128)S(1)} %stacked.9.refs_0_), channel_id=1, source_target_pairs={{0,4},{1,5},{2,6},{3,7},{4,0},{5,1},{6,2},{7,3},{8,12},{9,13},{10,... | collective-permute-start | bytes 196616 | tf_op jit(solution)/shard_map/ppermute | solution.py:597

commit v6 on v5

--- a/solution.py
+++ b/solution.py
@@ -77,26 +77,33 @@
 def first_kernel(*refs, **static):
     x, c, rate, res, *outs, x_in, c_in, rate_in, res_in, xs, cs, held, kept, done = refs
     chip, _, _ = position()
-    width = 2 * LANES
-    copies = []
-    for away in ORDER:
+    half = 4 * LANES
+    copies = [(rate, rate_in)]
+
+    def tiles(away, width):
         for q in range(4):
-            start = 8 * LANES * q + width * (chip ^ away)
-            lanes = pl.ds(pl.multiple_of(start, width), width)
-            copies += [(ref.at[:, lanes], into.at[:, lanes]) for ref, into in ((x, x_in), (c, c_in))]
-        if away == ORDER[0]:
-            copies.append((rate, rate_in))
+            first = (chip ^ away) * 2 * LANES // width * width
+            lanes = pl.ds(pl.multiple_of(8 * LANES * q + first, width), width)
+            pairs = ((x, x_in), (c, c_in))
+            copies.extend((ref.at[:, lanes], into.at[:, lanes]) for ref, into in pairs)
+
+    tiles(3, half // 2)
+    ahead = len(copies)
+    tiles(2, half // 2)
+    tiles(0, half)
     copies.append((res, res_in))
     copies = [
         pltpu.make_async_copy(source, into, done.at[place])
         for place, (source, into) in enumerate(copies)
     ]
-    for copy in copies:
+    for copy in copies[:ahead]:
         copy.start()
-    for copy in copies[:9]:
+    for copy in copies[:ahead]:
         copy.wait()
+    for copy in copies[ahead:]:
+        copy.start()
     summarize(x_in, c_in, rate_in, *outs, xs, cs, held, kept, **static)
-    for copy in copies[9:]:
+    for copy in copies[ahead:]:
         copy.wait()
 
 
@@ -234,7 +241,7 @@
         out_shape=[pltpu.VMEM(shape, f32) for shape in shapes]
         + [pltpu.VMEM(item.shape, item.dtype) for item in operands],
         scratch_shapes=[pltpu.VMEM(shape, f32) for shape in scratch]
-        + [pltpu.SemaphoreType.DMA((34,))],
+        + [pltpu.SemaphoreType.DMA((26,))],
         compiler_params=room(4),
         name="first_summaries",
     )(*[outside(item) for item in operands])
@@ -628,7 +635,7 @@
     row2, hold_side = paired(row2, got2, rates2, 1, 2 * rows, modes)
     other = crossed(row2, 4)
     theirs0, ours0, rates0 = more(0, (hold_side, holds[1]))
-    landed = stacked(stacked(other, rates0, 8), got0, 8)
+    landed = stacked(other, got0, 8)
     row0 = cores(0, ours0, theirs0, rates0, (landed,))
     row0, hold_own = paired(row0, got0, rates0, 1, 2 * rows, modes)
     beside = crossed(row0[START * 4 * modes : (START + 1) * 4 * modes], 4)

time: 47.3 us -> 46.4 us (0.981)
  waiting for transfers between devices: 7.69 us -> 6.38 us
  starting transfers between devices: 15 us -> 15.6 us
    ppermute x13, waiting for transfers between devices: 6.38 us -> 5.57 us  [crossed(): return lax.ppermute(value, 'context', [(i, i ^ distance) for i in range(8)])]
    ppermute x13, starting transfers between devices: 10.8 us -> 11.4 us  [crossed(): return lax.ppermute(value, 'context', [(i, i ^ distance) for i in range(8)])]
    ppermute x2, waiting for transfers between devices: 1.31 us -> 0.8 us  [shifted(): return lax.ppermute(value, 'dp', [(i, i ^ distance) for i in range(4)])]
    pallas_call x21 -> x20, Pallas kernels: 12.2 us -> 12.2 us  [local_call(): pl.pallas_call(kernel, in_specs=[vmem() for _ in operands] + [far_away()...]
  transfers between devices with their start and end apart: 15 -> 15, of which waited for: 9 -> 7; matrix products, arithmetic and copies ran while one was open for 0% -> 0% of each run, Pallas kernels for 38% -> 39%
where the time goes in v6:
time: 46.4 us; the launch traced here: 46.3 us
  Pallas kernels  23.5 us (51%)
  starting transfers between devices  15.6 us (34%)
  waiting for transfers between devices  6.38 us (14%)
  between operations  0.84 us (2%)
    pallas_call x20, Pallas kernels, local_call(): pl.pallas_call(kernel, in_specs=[vmem() for _ in operands] + [far_away()...  12.2 us
    ppermute x13, starting transfers between devices, crossed(): return lax.ppermute(value, 'context', [(i, i ^ distance) for i in range(8)])  11.4 us
    pallas_call x4, Pallas kernels, input_gradients(): pl.pallas_call(functools.partial(input_kernel, block=block, given=len(giv...  6.16 us
    ppermute x13, waiting for transfers between devices, crossed(): return lax.ppermute(value, 'context', [(i, i ^ distance) for i in range(8)])  5.57 us
    pallas_call x1, Pallas kernels, first_summaries(): pl.pallas_call(functools.partial(first_kernel, **static), in_specs=[far_a...  4.41 us
    ppermute x2, starting transfers between devices, shifted(): return lax.ppermute(value, 'dp', [(i, i ^ distance) for i in range(4)])  4.23 us
  transfers between devices with their start and end apart: 15, of which 7 were waited for; matrix products, arithmetic and copies ran while one was open for 0% of the time, Pallas kernels for 39%

profile of v6, /device:TPU:0, one launch (start us, length us, event | category | flops | bytes accessed | tf_op | source)
XLA Modules:
  0.0 46.3 jit_solution(798581526224961952)
XLA Ops:
  0.6 4.4 %first_summaries.1 = (f32[384,128]{1,0:T(8,128)S(1)}, f32[384,128]{1,0:T(8,128)S(1)}, f32[64,128]{1,0:T(8,128)S(1)}, bf16[128,4096]{1,0:T(8,128)(2,1)S(1)}, bf16...) custom-call(bf16[128,4096]{1,0:T(8,128)(2,1)} %bitcast.4, bf16[128,4096]{1,0:T(8,128)(2,1)} %bitcast.5, ...), custom_call_target="tpu_custom_call" | custom-call | tf_op jit(solution)/shard_map/first_summaries/pallas_call | solution.py:237
  5.6 3.0 %summaries.3 = (f32[384,128]{1,0:T(8,128)S(1)}, f32[384,128]{1,0:T(8,128)S(1)}, f32[64,128]{1,0:T(8,128)S(1)}) custom-call(bf16[128,4096]{1,0:T(8,128)(2,1)S(1)} %get-tuple-element.49.x, bf16[128,4096]{1,0:T(8,128)(2,1)S(1)} %get-tuple-element.46.c.cot.refs_0_, f32[16,4096]{1,0:T(8,128)S(1)} %get-tuple-element.47.rate.refs_1_), custom_call_target="tpu_custom_call" | custom-call | tf_op jit(solution)/shard_map/summaries/pallas_call | solution.py:43
  8.8 3.0 %collective-permute-start.2 = (f32[384,128]{1,0:T(8,128)S(1)}, f32[384,128]{1,0:T(8,128)S(1)}, u32[]{:S(2)}, u32[]{:S(2)}) collective-permute-start(f32[384,128]{1,0:T(8,128)S(1)} %get-tuple-element.58), channel_id=1, source_target_pairs={{0,2},{1,3},{2,0},{3,1},{4,6},{5,7},{6,4},{7,5},{8,10},{9,11},{10,... | collective-permute-start | bytes 589832 | tf_op jit(solution)/shard_map/ppermute | solution.py:604
  11.8 3.0 %summaries.4 = (f32[384,128]{1,0:T(8,128)S(1)}, f32[384,128]{1,0:T(8,128)S(1)}, f32[64,128]{1,0:T(8,128)S(1)}) custom-call(bf16[128,4096]{1,0:T(8,128)(2,1)S(1)} %get-tuple-element.49.x, bf16[128,4096]{1,0:T(8,128)(2,1)S(1)} %get-tuple-element.46.c.cot.refs_0_, f32[16,4096]{1,0:T(8,128)S(1)} %get-tuple-element.47.rate.refs_1_, ...), custom_call_target="tpu_custom_call" | custom-call | tf_op jit(solution)/shard_map/summaries/pallas_call | solution.py:43
  15.1 1.8 %collective-permute-done.2.one.other = f32[384,128]{1,0:T(8,128)S(1)} collective-permute-done((f32[384,128]{1,0:T(8,128)S(1)}, f32[384,128]{1,0:T(8,128)S(1)}, u32[]{:S(2)}, u32[]{:S(2)}) %collective-permute-start.2) | collective-permute-done | bytes 196640 | tf_op jit(solution)/shard_map/ppermute | solution.py:604
  17.1 1.8 %collective-permute-start.4 = (f32[384,128]{1,0:T(8,128)S(1)}, f32[384,128]{1,0:T(8,128)S(1)}, u32[]{:S(2)}, u32[]{:S(2)}) collective-permute-start(f32[384,128]{1,0:T(8,128)S(1)} %get-tuple-element.63), channel_id=1, source_target_pairs={{0,4},{1,5},{2,6},{3,7},{4,0},{5,1},{6,2},{7,3},{8,12},{9,13},{10,... | collective-permute-start | bytes 589832 | tf_op jit(solution)/shard_map/ppermute | solution.py:604
  18.9 3.0 %summaries.5 = (f32[384,128]{1,0:T(8,128)S(1)}, f32[384,128]{1,0:T(8,128)S(1)}, f32[64,128]{1,0:T(8,128)S(1)}) custom-call(bf16[128,4096]{1,0:T(8,128)(2,1)S(1)} %get-tuple-element.49.x, bf16[128,4096]{1,0:T(8,128)(2,1)S(1)} %get-tuple-element.46.c.cot.refs_0_, f32[16,4096]{1,0:T(8,128)S(1)} %get-tuple-element.47.rate.refs_1_, ...), custom_call_target="tpu_custom_call" | custom-call | tf_op jit(solution)/shard_map/summaries/pallas_call | solution.py:43
  22.4 1.1 %collective-permute-done.4.one.other = f32[384,128]{1,0:T(8,128)S(1)} collective-permute-done((f32[384,128]{1,0:T(8,128)S(1)}, f32[384,128]{1,0:T(8,128)S(1)}, u32[]{:S(2)}, u32[]{:S(2)}) %collective-permute-start.4) | collective-permute-done | bytes 196640 | tf_op jit(solution)/shard_map/ppermute | solution.py:604
  23.7 1.6 %collective-permute-start.8 = (f32[64,128]{1,0:T(8,128)S(1)}, f32[64,128]{1,0:T(8,128)S(1)}, u32[]{:S(2)}, u32[]{:S(2)}) collective-permute-start(f32[64,128]{1,0:T(8,128)S(1)} %get-tuple-element.73), channel_id=1, source_target_pairs={{0,8},{8,0},{16,24},{24,16},{1,9},{9,1},{17,25},{25,17},{2,10},{10... | collective-permute-start | bytes 98312 | tf_op jit(solution)/shard_map/ppermute | solution.py:608
  25.3 1.5 %collective-permute-start.7 = (f32[64,128]{1,0:T(8,128)S(1)}, f32[64,128]{1,0:T(8,128)S(1)}, u32[]{:S(2)}, u32[]{:S(2)}) collective-permute-start(f32[64,128]{1,0:T(8,128)S(1)} %slice.3), channel_id=1, source_target_pairs={{0,4},{1,5},{2,6},{3,7},{4,0},{5,1},{6,2},{7,3},{8,12},{9,13},{10,... | collective-permute-start | bytes 98312 | tf_op jit(solution)/shard_map/ppermute | solution.py:604
  26.9 1.3 %slab_gradients.2.refs_0_ = f32[1024,128]{1,0:T(8,128)S(1)} custom-call(bf16[128,4096]{1,0:T(8,128)(2,1)S(1)} %get-tuple-element.46.c.cot.refs_0_, f32[16,4096]{1,0:T(8,128)S(1)} %get-tuple-element.47.rate.refs_1_, f32[16,4096]{1,0:T(8,128)S(1)} %get-tuple-element.48.residues.res.refs_2_, f32[64,128]{1,0:T(8,128)S(1)} %get-tuple-element.72.refs_0_.kept), custom_call_target="tpu_custom_call" | custom-call | tf_op jit(solution)/shard_map/slab_gradients/pallas_call | solution.py:43
  28.2 1.1 %collective-permute-done.7.beside = f32[64,128]{1,0:T(8,128)S(1)} collective-permute-done((f32[64,128]{1,0:T(8,128)S(1)}, f32[64,128]{1,0:T(8,128)S(1)}, u32[]{:S(2)}, u32[]{:S(2)}) %collective-permute-start.7) | collective-permute-done | bytes 32800 | tf_op jit(solution)/shard_map/ppermute | solution.py:604
  29.3 1.5 %collective-permute-start.9 = (f32[128,128]{1,0:T(8,128)S(1)}, f32[128,128]{1,0:T(8,128)S(1)}, u32[]{:S(2)}, u32[]{:S(2)}) collective-permute-start(f32[128,128]{1,0:T(8,128)S(1)} %get-tuple-element.76), channel_id=1, source_target_pairs={{0,2},{1,3},{2,0},{3,1},{4,6},{5,7},{6,4},{7,5},{8,10},{9,11},{10,... | collective-permute-start | bytes 196616 | tf_op jit(solution)/shard_map/ppermute | solution.py:604
  30.8 2.6 %collective-permute-start.10 = (f32[32,128]{1,0:T(8,128)S(1)}, f32[32,128]{1,0:T(8,128)S(1)}, u32[]{:S(2)}, u32[]{:S(2)}) collective-permute-start(f32[32,128]{1,0:T(8,128)S(1)} %get-tuple-element.74.refs_0_), channel_id=1, source_target_pairs={{0,16},{8,24},{16,0},{24,8},{1,17},{9,25},{17,1},{25,9},{2,18},{10... | collective-permute-start | bytes 49160 | tf_op jit(solution)/shard_map/ppermute | solution.py:608
  33.4 1.3 %slab_gradients.3.refs_2_.refs_0_ = f32[1024,128]{1,0:T(8,128)S(1)} custom-call(bf16[128,4096]{1,0:T(8,128)(2,1)S(1)} %get-tuple-element.46.c.cot.refs_0_, f32[16,4096]{1,0:T(8,128)S(1)} %get-tuple-element.47.rate.refs_1_, f32[16,4096]{1,0:T(8,128)S(1)} %get-tuple-element.48.residues.res.refs_2_, f32[128,128]{1,0:T(8,128)S(1)} %get-tuple-element.75.refs_0_), custom_call_target="tpu_custom_call" | custom-call | tf_op jit(solution)/shard_map/slab_gradients/pallas_call | solution.py:43
  34.7 0.8 %collective-permute-done.10.refs_1_ = f32[32,128]{1,0:T(8,128)S(1)} collective-permute-done((f32[32,128]{1,0:T(8,128)S(1)}, f32[32,128]{1,0:T(8,128)S(1)}, u32[]{:S(2)}, u32[]{:S(2)}) %collective-permute-start.10) | collective-permute-done | bytes 16416 | tf_op jit(solution)/shard_map/ppermute | solution.py:608
  36.1 0.9 %collective-permute-done.12.two = f32[32,128]{1,0:T(8,128)S(1)} collective-permute-done((f32[32,128]{1,0:T(8,128)S(1)}, f32[32,128]{1,0:T(8,128)S(1)}, u32[]{:S(2)}, u32[]{:S(2)}) %collective-permute-start.12) | collective-permute-done | bytes 16416 | tf_op jit(solution)/shard_map/ppermute | solution.py:604
  37.0 0.6 %collective-permute-start.13 = (f32[64,128]{1,0:T(8,128)S(1)}, f32[64,128]{1,0:T(8,128)S(1)}, u32[]{:S(2)}, u32[]{:S(2)}) collective-permute-start(f32[64,128]{1,0:T(8,128)S(1)} %stacked.6.one), channel_id=1, source_target_pairs={{0,2},{1,3},{2,0},{3,1},{4,6},{5,7},{6,4},{7,5},{8,10},{9,11},{10,... | collective-permute-start | bytes 98312 | tf_op jit(solution)/shard_map/ppermute | solution.py:604
  37.6 1.5 %input_gradients.4.refs_5_ = bf16[128,1024]{1,0:T(8,128)(2,1)S(1)} custom-call(bf16[128,4096]{1,0:T(8,128)(2,1)S(1)} %get-tuple-element.46.c.cot.refs_0_, f32[16,4096]{1,0:T(8,128)S(1)} %get-tuple-element.47.rate.refs_1_, f32[16,4096]{1,0:T(8,128)S(1)} %get-tuple-element.48.residues.res.refs_2_, f32[256,128]{1,0:T(8,128)S(1)} %get-tuple-element.80.refs_3_, ...), custom_call_target="tpu_custom_call" | custom-call | tf_op jit(solution)/shard_map/input_gradients/pallas_call | solution.py:554
  39.0 1.5 %input_gradients.5 = (bf16[128,4096]{1,0:T(8,128)(2,1)}, bf16[128,1024]{1,0:T(8,128)(2,1)S(1)}) custom-call(bf16[128,4096]{1,0:T(8,128)(2,1)S(1)} %get-tuple-element.46.c.cot.refs_0_, f32[16,4096]{1,0:T(8,128)S(1)} %get-tuple-element.47.rate.refs_1_, f32[16,4096]{1,0:T(8,128)S(1)} %get-tuple-element.48.residues.res.refs_2_, ...), custom_call_target="tpu_custom_call" | custom-call | tf_op jit(solution)/shard_map/input_gradients/pallas_call | solution.py:554
  40.9 1.5 %collective-permute-start.14 = (f32[128,128]{1,0:T(8,128)S(1)}, f32[128,128]{1,0:T(8,128)S(1)}, u32[]{:S(2)}, u32[]{:S(2)}) collective-permute-start(f32[128,128]{1,0:T(8,128)S(1)} %stacked.7.refs_0_), channel_id=1, source_target_pairs={{0,4},{1,5},{2,6},{3,7},{4,0},{5,1},{6,2},{7,3},{8,12},{9,13},{10,... | collective-permute-start | bytes 196616 | tf_op jit(solution)/shard_map/ppermute | solution.py:604
  42.3 0.9 %input_gradients.6 = (bf16[128,4096]{1,0:T(8,128)(2,1)}, bf16[128,1024]{1,0:T(8,128)(2,1)S(1)}) custom-call(f32[1024,128]{1,0:T(8,128)S(1)} %slab_gradients.2.refs_0_, f32[16,4096]{1,0:T(8,128)S(1)} %get-tuple-element.47.rate.refs_1_, f32[16,4096]{1,0:T(8,128)S(1)} %get-tuple-element.48.residues.res.refs_2_, ...), custom_call_target="tpu_custom_call", output_to_operand_aliasing={{0}: (6, {})} | custom-call | tf_op jit(solution)/shard_map/input_gradients/pallas_call | solution.py:554
  43.3 2.3 %input_gradients.7 = (bf16[128,4096]{1,0:T(8,128)(2,1)}, bf16[128,1024]{1,0:T(8,128)(2,1)}) custom-call(f32[1024,128]{1,0:T(8,128)S(1)} %slab_gradients.3.refs_2_.refs_0_, f32[16,4096]{1,0:T(8,128)S(1)} %get-tuple-element.47.rate.refs_1_, f32[16,4096]{1,0:T(8,128)S(1)} %get-tuple-element.48.residues.res.refs_2_, ...), custom_call_target="tpu_custom_call", output_to_operand_aliasing={{0}: (6, {})} | custom-call | tf_op jit(solution)/shard_map/input_gradients/pallas_call | solution.py:554
  45.6 0.7 %placed.1 = (f32[16,1024]{1,0:T(8,128)}, f32[16,1024]{1,0:T(8,128)}) custom-call(f32[128,128]{1,0:T(8,128)S(1)} %stacked.7.refs_0_, f32[128,128]{1,0:T(8,128)S(1)} %collective-permute-done.14.refs_1_, bf16[128,4096]{1,0:T(8,128)(2,1)} %get-tuple-element.86.refs_2_), custom_call_target="tpu_custom_call" | custom-call | tf_op jit(solution)/shard_map/placed/pallas_call | solution.py:590
  (33 shorter events, 2.7 us)
Async XLA Ops:
  5.1 3.7 %collective-permute-start = (f32[384,128]{1,0:T(8,128)S(1)}, f32[384,128]{1,0:T(8,128)S(1)}, u32[]{:S(2)}, u32[]{:S(2)}) collective-permute-start(f32[384,128]{1,0:T(8,128)S(1)} %get-tuple-element.51), channel_id=1, source_target_pairs={{0,1},{1,0},{2,3},{3,2},{4,5},{5,4},{6,7},{7,6},{8,9},{9,8},{10,11... | collective-permute-start | bytes 589832 | tf_op jit(solution)/shard_map/ppermute | solution.py:604
  8.6 6.3 %collective-permute-start.3 = (f32[384,128]{1,0:T(8,128)S(1)}, f32[384,128]{1,0:T(8,128)S(1)}, u32[]{:S(2)}, u32[]{:S(2)}) collective-permute-start(f32[384,128]{1,0:T(8,128)S(1)} %get-tuple-element.60), channel_id=1, source_target_pairs={{0,1},{1,0},{2,3},{3,2},{4,5},{5,4},{6,7},{7,6},{8,9},{9,8},{10,11... | collective-permute-start | bytes 589832 | tf_op jit(solution)/shard_map/ppermute | solution.py:604
  8.8 8.1 %collective-permute-start.2 = (f32[384,128]{1,0:T(8,128)S(1)}, f32[384,128]{1,0:T(8,128)S(1)}, u32[]{:S(2)}, u32[]{:S(2)}) collective-permute-start(f32[384,128]{1,0:T(8,128)S(1)} %get-tuple-element.58), channel_id=1, source_target_pairs={{0,2},{1,3},{2,0},{3,1},{4,6},{5,7},{6,4},{7,5},{8,10},{9,11},{10,... | collective-permute-start | bytes 589832 | tf_op jit(solution)/shard_map/ppermute | solution.py:604
  14.9 2.1 %collective-permute-start.1 = (f32[384,128]{1,0:T(8,128)S(1)}, f32[384,128]{1,0:T(8,128)S(1)}, u32[]{:S(2)}, u32[]{:S(2)}) collective-permute-start(f32[384,128]{1,0:T(8,128)S(1)} %get-tuple-element.56), channel_id=1, source_target_pairs={{0,1},{1,0},{2,3},{3,2},{4,5},{5,4},{6,7},{7,6},{8,9},{9,8},{10,11... | collective-permute-start | bytes 589832 | tf_op jit(solution)/shard_map/ppermute | solution.py:604
  15.0 7.3 %collective-permute-start.6 = (f32[384,128]{1,0:T(8,128)S(1)}, f32[384,128]{1,0:T(8,128)S(1)}, u32[]{:S(2)}, u32[]{:S(2)}) collective-permute-start(f32[384,128]{1,0:T(8,128)S(1)} %get-tuple-element.68), channel_id=1, source_target_pairs={{0,2},{1,3},{2,0},{3,1},{4,6},{5,7},{6,4},{7,5},{8,10},{9,11},{10,... | collective-permute-start | bytes 589832 | tf_op jit(solution)/shard_map/ppermute | solution.py:604
  17.1 6.4 %collective-permute-start.4 = (f32[384,128]{1,0:T(8,128)S(1)}, f32[384,128]{1,0:T(8,128)S(1)}, u32[]{:S(2)}, u32[]{:S(2)}) collective-permute-start(f32[384,128]{1,0:T(8,128)S(1)} %get-tuple-element.63), channel_id=1, source_target_pairs={{0,4},{1,5},{2,6},{3,7},{4,0},{5,1},{6,2},{7,3},{8,12},{9,13},{10,... | collective-permute-start | bytes 589832 | tf_op jit(solution)/shard_map/ppermute | solution.py:604
  21.9 1.6 %collective-permute-start.5 = (f32[384,128]{1,0:T(8,128)S(1)}, f32[384,128]{1,0:T(8,128)S(1)}, u32[]{:S(2)}, u32[]{:S(2)}) collective-permute-start(f32[384,128]{1,0:T(8,128)S(1)} %get-tuple-element.66), channel_id=1, source_target_pairs={{0,1},{1,0},{2,3},{3,2},{4,5},{5,4},{6,7},{7,6},{8,9},{9,8},{10,11... | collective-permute-start | bytes 589832 | tf_op jit(solution)/shard_map/ppermute | solution.py:604
  23.7 4.5 %collective-permute-start.8 = (f32[64,128]{1,0:T(8,128)S(1)}, f32[64,128]{1,0:T(8,128)S(1)}, u32[]{:S(2)}, u32[]{:S(2)}) collective-permute-start(f32[64,128]{1,0:T(8,128)S(1)} %get-tuple-element.73), channel_id=1, source_target_pairs={{0,8},{8,0},{16,24},{24,16},{1,9},{9,1},{17,25},{25,17},{2,10},{10... | collective-permute-start | bytes 98312 | tf_op jit(solution)/shard_map/ppermute | solution.py:608
  25.3 3.9 %collective-permute-start.7 = (f32[64,128]{1,0:T(8,128)S(1)}, f32[64,128]{1,0:T(8,128)S(1)}, u32[]{:S(2)}, u32[]{:S(2)}) collective-permute-start(f32[64,128]{1,0:T(8,128)S(1)} %slice.3), channel_id=1, source_target_pairs={{0,4},{1,5},{2,6},{3,7},{4,0},{5,1},{6,2},{7,3},{8,12},{9,13},{10,... | collective-permute-start | bytes 98312 | tf_op jit(solution)/shard_map/ppermute | solution.py:604
  29.3 6.2 %collective-permute-start.9 = (f32[128,128]{1,0:T(8,128)S(1)}, f32[128,128]{1,0:T(8,128)S(1)}, u32[]{:S(2)}, u32[]{:S(2)}) collective-permute-start(f32[128,128]{1,0:T(8,128)S(1)} %get-tuple-element.76), channel_id=1, source_target_pairs={{0,2},{1,3},{2,0},{3,1},{4,6},{5,7},{6,4},{7,5},{8,10},{9,11},{10,... | collective-permute-start | bytes 196616 | tf_op jit(solution)/shard_map/ppermute | solution.py:604
  30.8 4.7 %collective-permute-start.10 = (f32[32,128]{1,0:T(8,128)S(1)}, f32[32,128]{1,0:T(8,128)S(1)}, u32[]{:S(2)}, u32[]{:S(2)}) collective-permute-start(f32[32,128]{1,0:T(8,128)S(1)} %get-tuple-element.74.refs_0_), channel_id=1, source_target_pairs={{0,16},{8,24},{16,0},{24,8},{1,17},{9,25},{17,1},{25,9},{2,18},{10... | collective-permute-start | bytes 49160 | tf_op jit(solution)/shard_map/ppermute | solution.py:608
  35.5 2.0 %collective-permute-start.11 = (f32[256,128]{1,0:T(8,128)S(1)}, f32[256,128]{1,0:T(8,128)S(1)}, u32[]{:S(2)}, u32[]{:S(2)}) collective-permute-start(f32[256,128]{1,0:T(8,128)S(1)} %get-tuple-element.81), channel_id=1, source_target_pairs={{0,1},{1,0},{2,3},{3,2},{4,5},{5,4},{6,7},{7,6},{8,9},{9,8},{10,11... | collective-permute-start | bytes 393224 | tf_op jit(solution)/shard_map/ppermute | solution.py:604
  35.6 1.4 %collective-permute-start.12 = (f32[32,128]{1,0:T(8,128)S(1)}, f32[32,128]{1,0:T(8,128)S(1)}, u32[]{:S(2)}, u32[]{:S(2)}) collective-permute-start(f32[32,128]{1,0:T(8,128)S(1)} %added.1.refs_6_.one), channel_id=1, source_target_pairs={{0,1},{1,0},{2,3},{3,2},{4,5},{5,4},{6,7},{7,6},{8,9},{9,8},{10,11... | collective-permute-start | bytes 49160 | tf_op jit(solution)/shard_map/ppermute | solution.py:604
  37.0 3.9 %collective-permute-start.13 = (f32[64,128]{1,0:T(8,128)S(1)}, f32[64,128]{1,0:T(8,128)S(1)}, u32[]{:S(2)}, u32[]{:S(2)}) collective-permute-start(f32[64,128]{1,0:T(8,128)S(1)} %stacked.6.one), channel_id=1, source_target_pairs={{0,2},{1,3},{2,0},{3,1},{4,6},{5,7},{6,4},{7,5},{8,10},{9,11},{10,... | collective-permute-start | bytes 98312 | tf_op jit(solution)/shard_map/ppermute | solution.py:604
  40.9 4.7 %collective-permute-start.14 = (f32[128,128]{1,0:T(8,128)S(1)}, f32[128,128]{1,0:T(8,128)S(1)}, u32[]{:S(2)}, u32[]{:S(2)}) collective-permute-start(f32[128,128]{1,0:T(8,128)S(1)} %stacked.7.refs_0_), channel_id=1, source_target_pairs={{0,4},{1,5},{2,6},{3,7},{4,0},{5,1},{6,2},{7,3},{8,12},{9,13},{10,... | collective-permute-start | bytes 196616 | tf_op jit(solution)/shard_map/ppermute | solution.py:604
